TPU v7x, 32 devices: a whole 2x2x4 slice. The times are simulated.
32 devices in a mesh: groups: 2 (over y), seq: 16 (over z, x, core), mp: 1.
Axes of the slice: x: 2, y: 2, z: 4, core: 2. Of those that a mesh axis runs over, the one named last changes fastest.
Arguments:
- hidden: bfloat16 [7200, 5120], P(('groups', 'seq'), 'mp'), parts along dimension 0, may hold values from -6 to 6
- modulation: float32 [4, 5120], P('groups', 'mp'), parts along dimension 0, may hold values from -3 to 3
- head_weight: bfloat16 [5120, 64], P('mp'), may hold values from -0.078125 to 0.078125
- head_bias: float32 [64], P('mp'), may hold values from -3 to 3
- residual: float32 [64, 7200], P('mp', ('groups', 'seq')), parts along dimension 1, may hold values from -4 to 4
- latent: float32 [64, 7200], P('mp', ('groups', 'seq')), parts along dimension 1, may hold values from -6 to 6
- band_gain: float32 [2, 16], P(None, 'mp'), may hold values from 0.5 to 2
- cut_rows: int32 [2], P('groups'), parts along dimension 0, may hold values from 0 to 45
- cut_cols: int32 [2], P('groups'), parts along dimension 0, may hold values from 0 to 80
- skip_flags: int32 [100], P('groups'), parts along dimension 0, may hold values 0 or 1
- step_index: int32 [2], P('groups'), parts along dimension 0, may hold values from 0 to 49
Outputs:
- velocity: float32 [64, 7200], P('mp', ('groups', 'seq')), parts along dimension 1
- latent_next: float32 [64, 7200], P('mp', ('groups', 'seq')), parts along dimension 1
There are 2 independent parts, one for each index of `groups`. A program takes and returns all parts, laid end to end along the dimension named above; an argument that names none is the same for every part. Nothing has to cross between parts.
Inputs may be any that keep to these rules, and one draw needn't show every extreme that they name: cut_rows[f] and cut_cols[f] belong to frame f.
All inputs are finite; a program needn't handle non-finite values.
Results may differ from a plain program's by a relative error of at most 0.0019.
Values sent between devices are 32-bit elements; how exact they have to be, the bound alone decides.
No kernel may reach another device: no remote copies, remote signals or barrier semaphores. Data moves between devices by JAX's collectives and lax.ppermute only.
A program may use at most 64 MiB of HBM per device.

v0:
```python
import math

import jax
import jax.numpy as jnp
from jax import lax
from jax.sharding import PartitionSpec as P

D = 5120
H = 90
W = 160
PH = 45
PW = 80
NSTEP = 50


EPSILON = 1e-06
GUIDE_EXTRA = 4.0
SHIFT_FACTOR = 5.0
HIGHEST = lax.Precision.HIGHEST


def from_partner(value, axis, bit):
    mask = 2**bit
    pairs = [(source, source ^ mask) for source in range(lax.axis_size(axis))]
    return lax.ppermute(value, axis, pairs)


def sigma_at(step_number):
    remain = 1.0 - step_number.astype(jnp.float32) / NSTEP
    return SHIFT_FACTOR * remain / (1.0 + (SHIFT_FACTOR - 1.0) * remain)


def band_weights(skip_flags, step_index, band_gain):
    current = step_index[0]
    counter = jnp.arange(NSTEP, dtype=jnp.int32)
    computed = (skip_flags == 0) & (counter <= current)
    last_full = jnp.max(jnp.where(computed, counter, -1))
    spacing = (current - last_full).astype(jnp.float32)
    gap_ratio = spacing / (spacing + 2.0)
    return (band_gain[0] * (1.0 + gap_ratio), band_gain[1] * (1.0 - 0.5 * gap_ratio))


def band_matrix(length, cutoff):
    counter = jnp.arange(length, dtype=jnp.int32)
    product = counter[:, None] * counter[None, :] % length
    angles = 2.0 * math.pi / length * product.astype(jnp.float32)
    cosine = jnp.cos(angles)
    sine_table = jnp.sin(angles)
    kept_modes = (jnp.minimum(counter, length - counter) <= cutoff).astype(jnp.float32)
    summed = jnp.dot(cosine * kept_modes, cosine.T, precision=HIGHEST) + jnp.dot(
        sine_table * kept_modes, sine_table.T, precision=HIGHEST
    )
    return summed / length


def body(
    hidden,
    modulation,
    head_weight,
    head_bias,
    residual,
    latent,
    band_gain,
    cut_rows,
    cut_cols,
    skip_flags,
    step_index,
):
    values = hidden.astype(jnp.float32)
    moments = lax.psum((jnp.sum(values, axis=1), jnp.sum(values * values, axis=1)), "mp")
    average = moments[0] / D
    scale_inv = lax.rsqrt(moments[1] / D - average * average + EPSILON)
    normed = (
        (values - average[:, None]) * scale_inv[:, None] * (1.0 + modulation[1]) + modulation[0]
    ).astype(jnp.bfloat16)
    conditional = (
        lax.psum_scatter(
            lax.dot_general(
                head_weight, normed, (((0,), (1,)), ((), ())), preferred_element_type=jnp.float32
            ),
            "mp",
            scatter_dimension=0,
            tiled=True,
        )
        + head_bias[:, None]
    )
    local_rows = residual.shape[0]
    local_tokens = residual.shape[1]
    frame_tokens = PH * PW
    members = frame_tokens // local_tokens
    seq_index = lax.axis_index("seq")
    position = seq_index % members
    frame_index = seq_index // members
    frame_data = residual
    for section_bit in range(members.bit_length() - 1):
        partner = from_partner(frame_data, "seq", section_bit)
        upper_half = seq_index // (1 << section_bit) % 2 == 1
        frame_data = jnp.where(
            upper_half,
            jnp.concatenate([partner, frame_data], axis=1),
            jnp.concatenate([frame_data, partner], axis=1),
        )
    channels = local_rows // 4
    planes = (
        frame_data.reshape(channels, 2, 2, PH, PW).transpose(0, 3, 1, 4, 2).reshape(channels, H, W)
    )
    row_filter = band_matrix(H, cut_rows[frame_index])
    col_filter = band_matrix(W, cut_cols[frame_index])
    row_total = min(local_tokens // PW + 2, PH)
    first_row = jnp.minimum(position * local_tokens // PW, PH - row_total)
    row_part = lax.dynamic_slice_in_dim(row_filter, 2 * first_row, 2 * row_total, 0)
    partial_rows = jnp.einsum("ij,cjw->ciw", row_part, planes, precision=HIGHEST)
    low_rows = jnp.dot(
        partial_rows.reshape(channels * 2 * row_total, W), col_filter, precision=HIGHEST
    ).reshape(channels, 2 * row_total, W)
    low_tokens = (
        low_rows.reshape(channels, row_total, 2, PW, 2)
        .transpose(0, 2, 4, 1, 3)
        .reshape(local_rows, row_total * PW)
    )
    low_band = lax.dynamic_slice_in_dim(
        low_tokens, position * local_tokens - first_row * PW, local_tokens, 1
    )
    high_band = residual - low_band
    w_low, w_high = band_weights(skip_flags, step_index, band_gain)
    row_low = jnp.repeat(w_low, 4)[:, None]
    row_high = jnp.repeat(w_high, 4)[:, None]
    velocity = conditional + GUIDE_EXTRA * (row_low * low_band + row_high * high_band)
    current = step_index[0]
    latent_next = latent + (sigma_at(current + 1) - sigma_at(current)) * velocity
    return (velocity, latent_next)


def solution(mesh):
    in_specs = (
        P(("groups", "seq"), "mp"),
        P("groups", "mp"),
        P("mp", None),
        P("mp"),
        P("mp", ("groups", "seq")),
        P("mp", ("groups", "seq")),
        P(None, "mp"),
        P("groups"),
        P("groups"),
        P("groups"),
        P("groups"),
    )
    out_specs = (P("mp", ("groups", "seq")), P("mp", ("groups", "seq")))
    return jax.shard_map(body, mesh=mesh, in_specs=in_specs, out_specs=out_specs, check_vma=False)
```

profile of v0, /device:TPU:0, one launch (start us, length us, event | category | flops | bytes accessed | tf_op | source)
XLA Modules:
  0.0 69.1 jit_solution(14506986031382928052)
XLA Ops:
  0.6 0.0 copy-start
  0.6 0.6 collective-permute-start
  2.5 0.9 %fusion.18 = f32[160,160]{1,0:T(8,128)S(1)} fusion(f32[160]{0:T(256)S(1)} %compare_convert_fusion), kind=kOutput, calls=%fused_computation.20 | convolution fusion | flops 49638400 | bytes 103040 | tf_op jit(solution)/shard_map/dot_general | solution.py:50
  4.1 2.4 %convert_reduce_fusion = (f32[225]{0:T(256)S(1)}, f32[225]{0:T(256)S(1)}) fusion(bf16[225,5120]{1,0:T(8,128)(2,1)} %param.11), kind=kLoop, calls=%fused_computation.2 | loop fusion | flops 4607550 | bytes 2305800 | tf_op jit(solution)/shard_map/reduce_sum | solution.py:70
  6.6 0.9 %slice_add_fusion = (f32[1,5120]{1,0:T(1,128)S(1)}, f32[1,5120]{1,0:T(1,128)S(1)}) fusion(f32[2,5120]{1,0:T(2,128)} %param.12), kind=kLoop, calls=%fused_computation.59 | loop fusion | flops 5120 | bytes 81920 | tf_op jit(solution)/shard_map/add | solution.py:74
  7.5 1.3 %fusion.69 = s32[]{:T(128)} fusion(s32[50]{0:T(128)} %param.20, s32[]{:T(128)} %bitcast.33), kind=kLoop, calls=%fused_computation.78 | loop fusion | flops 249 | bytes 208 | tf_op jit(solution)/shard_map/reduce_max | solution.py:37
  9.5 0.0 collective-permute-done
  9.5 1.0 %maximum_select_fusion.3 = f32[64,450]{1,0:T(8,128)S(1)} fusion(f32[64,225]{1,0:T(8,128)} %param.15, f32[64,225]{1,0:T(8,128)S(1)} %collective-permute-done, pred[]{:T(512)S(6)} %eq.33), kind=kLoop, calls=%fused_computation.32 | loop fusion | flops 86400 | bytes 230401 | tf_op jit(solution)/shard_map/jit(_where)/select_n | solution.py:98
  10.5 2.7 %collective-permute-start.1 = (f32[64,450]{1,0:T(8,128)S(1)}, f32[64,450]{1,0:T(8,128)S(1)}, u32[]{:S(2)}, u32[]{:S(2)}) collective-permute-start(f32[64,450]{1,0:T(8,128)S(1)} %maximum_select_fusion.3), channel_id=1, source_target_pairs={{0,2},{1,3},{2,0},{3,1},{4,6},{5,7},{6,4},{7,5},{8,10},{9,11},{10,... | collective-permute-start | bytes 345608 | tf_op jit(solution)/shard_map/ppermute | solution.py:25
  13.2 0.8 %multiply_bitcast_fusion.1 = (f32[16]{0:T(128)S(1)}, f32[16]{0:T(128)S(1)}) fusion(f32[2,16]{1,0:T(2,128)} %param.17, f32[]{:T(128)S(6)} %add.137, f32[]{:T(128)S(6)} %sub.84), kind=kLoop, calls=%fused_computation.77 | loop fusion | flops 32 | bytes 264 | tf_op jit(solution)/shard_map/mul | solution.py:40
  13.9 3.3 %collective-permute-done.1 = f32[64,450]{1,0:T(8,128)S(1)} collective-permute-done((f32[64,450]{1,0:T(8,128)S(1)}, f32[64,450]{1,0:T(8,128)S(1)}, u32[]{:S(2)}, u32[]{:S(2)}) %collective-permute-start.1) | collective-permute-done | bytes 115232 | tf_op jit(solution)/shard_map/ppermute | solution.py:25
  17.2 0.2 maximum_select_fusion.2
  17.4 1.9 %collective-permute-start.2 = (f32[64,900]{1,0:T(8,128)S(1)}, f32[64,900]{1,0:T(8,128)S(1)}, u32[]{:S(2)}, u32[]{:S(2)}) collective-permute-start(f32[64,900]{1,0:T(8,128)S(1)} %maximum_select_fusion.2), channel_id=1, source_target_pairs={{0,4},{1,5},{2,6},{3,7},{4,0},{5,1},{6,2},{7,3},{8,12},{9,13},{10,... | collective-permute-start | bytes 691208 | tf_op jit(solution)/shard_map/ppermute | solution.py:25
  19.3 0.9 %fusion.7 = f32[160,160]{1,0:T(8,128)S(1)} fusion(f32[160,160]{1,0:T(8,128)S(1)} %fusion.18, f32[160]{0:T(256)S(1)} %compare_convert_fusion), kind=kOutput, calls=%fused_computation.10 | convolution fusion | flops 49689600 | bytes 205440 | tf_op jit(solution)/shard_map/dot_general | solution.py:50
  20.2 5.2 %collective-permute-done.2 = f32[64,900]{1,0:T(8,128)S(1)} collective-permute-done((f32[64,900]{1,0:T(8,128)S(1)}, f32[64,900]{1,0:T(8,128)S(1)}, u32[]{:S(2)}, u32[]{:S(2)}) %collective-permute-start.2) | collective-permute-done | bytes 230432 | tf_op jit(solution)/shard_map/ppermute | solution.py:25
  25.5 0.2 maximum_select_fusion.1
  25.7 2.6 %collective-permute-start.3 = (f32[64,1800]{1,0:T(8,128)S(1)}, f32[64,1800]{1,0:T(8,128)S(1)}, u32[]{:S(2)}, u32[]{:S(2)}) collective-permute-start(f32[64,1800]{1,0:T(8,128)S(1)} %maximum_select_fusion.1), channel_id=1, source_target_pairs={{0,8},{1,9},{2,10},{3,11},{4,12},{5,13},{6,14},{7,15},{8,0},{9,1},... | collective-permute-start | bytes 1382408 | tf_op jit(solution)/shard_map/ppermute | solution.py:25
  28.3 0.1 dot_general.32
  28.4 0.1 broadcast_in_dim.8
  28.5 0.1 mul.224
  28.6 0.1 broadcast_in_dim.9
  28.7 0.1 mul.249
  28.8 0.4 fusion.38
  29.3 0.4 fusion.40
  29.7 19.5 %collective-permute-done.3 = f32[64,1800]{1,0:T(8,128)S(1)} collective-permute-done((f32[64,1800]{1,0:T(8,128)S(1)}, f32[64,1800]{1,0:T(8,128)S(1)}, u32[]{:S(2)}, u32[]{:S(2)}) %collective-permute-start.3) | collective-permute-done | bytes 460832 | tf_op jit(solution)/shard_map/ppermute | solution.py:25
  49.2 0.3 maximum_select_fusion
  49.6 1.1 %select_n.126 = f32[16,2,2,45,80]{4,3,2,1,0:T(8,128)S(1)} reshape(f32[64,3600]{1,0:T(8,128)S(1)} %maximum_select_fusion) | data formatting | bytes 1843200 | tf_op jit(solution)/shard_map/jit(_where)/select_n | solution.py:98
  50.7 6.9 %copy.17 = f32[16,45,2,80,2]{0,4,3,2,1:T(2,128)} copy(f32[16,45,2,80,2]{3,1,4,2,0:T(8,128)S(1)} %bitcast.38) | data formatting | bytes 1843200 | tf_op jit(solution)/shard_map/transpose | solution.py:105
  57.6 0.0 copy-start.1
  57.6 0.0 copy-start.2
  57.6 0.0 copy-start.3
  57.6 5.1 %copy.18 = f32[16,90,160]{1,2,0:T(8,128)S(1)} copy(f32[16,90,160]{0,2,1:T(8,128)} %bitcast.37) | data formatting | bytes 1843200 | tf_op jit(solution)/shard_map/reshape | solution.py:105
  62.7 2.1 %convolution_bitcast_fusion.1 = f32[16,8,160]{2,1,0:T(8,128)S(1)} fusion(f32[16,90,160]{1,2,0:T(8,128)S(1)} %copy.18, f32[90,90]{1,0:T(8,128)S(1)} %fusion.38, s32[]{:T(128)S(6)} %select_n.130, f32[90,90]{1,0:T(8,128)S(1)} %fusion.40), kind=kOutput, calls=%fused_computation.12 | convolution fusion | flops 22119840 | bytes 1400836 | tf_op jit(solution)/shard_map/ij,cjw->ciw/dot_general | solution.py:112
  64.9 0.1 copy.24
  64.9 0.4 convolution_bitcast_fusion
  65.3 0.1 copy.21
  65.4 0.1 reshape.55
  65.5 0.0 copy-done
  65.5 0.0 copy-done.1
  65.5 0.0 copy-done.2
  65.6 0.0 copy-done.3
  65.6 3.5 %multiply_add_fusion = (f32[64,225]{1,0:T(8,128)}, f32[64,225]{1,0:T(8,128)}) fusion(f32[64,225]{1,0:T(8,128)S(1)} %copy-done.2, f32[]{:T(128)S(6)} %sub.88, f32[64,225]{1,0:T(8,128)S(1)} %copy-done.1, f32[64]{0:T(128)S(1)} %mul.249, f32[64,320]{1,0:T(8,128)S(1)} %reshape.55, s32[]{:T(128)S(6)} %select_n.132, f32[64]{0:T(128)S(1)} %mul.224, ...), kind=kOutput, calls=%fused_computation.44 | convolution fusion | flops 154497600 | bytes 3290896 | tf_op jit(solution)/shard_map/dot_general | solution.py:78
  (3 shorter events, 0.0 us)
Async XLA Ops:
  0.6 64.9 %copy-start = (bf16[5120,64]{0,1:T(8,128)(2,1)S(1)}, bf16[5120,64]{0,1:T(8,128)(2,1)}, u32[]{:S(2)}) copy-start(bf16[5120,64]{0,1:T(8,128)(2,1)} %param.13) | copy-start | bytes 1966084
  0.6 8.8 %collective-permute-start = (f32[64,225]{1,0:T(8,128)}, f32[64,225]{1,0:T(8,128)S(1)}, u32[]{:S(2)}, u32[]{:S(2)}) collective-permute-start(f32[64,225]{1,0:T(8,128)} %param.15), channel_id=1, source_target_pairs={{0,1},{1,0},{2,3},{3,2},{4,5},{5,4},{6,7},{7,6},{8,9},{9,8},{10,11... | collective-permute-start | bytes 172808 | tf_op jit(solution)/shard_map/ppermute | solution.py:25
  10.5 6.7 %collective-permute-start.1 = (f32[64,450]{1,0:T(8,128)S(1)}, f32[64,450]{1,0:T(8,128)S(1)}, u32[]{:S(2)}, u32[]{:S(2)}) collective-permute-start(f32[64,450]{1,0:T(8,128)S(1)} %maximum_select_fusion.3), channel_id=1, source_target_pairs={{0,2},{1,3},{2,0},{3,1},{4,6},{5,7},{6,4},{7,5},{8,10},{9,11},{10,... | collective-permute-start | bytes 345608 | tf_op jit(solution)/shard_map/ppermute | solution.py:25
  17.4 8.1 %collective-permute-start.2 = (f32[64,900]{1,0:T(8,128)S(1)}, f32[64,900]{1,0:T(8,128)S(1)}, u32[]{:S(2)}, u32[]{:S(2)}) collective-permute-start(f32[64,900]{1,0:T(8,128)S(1)} %maximum_select_fusion.2), channel_id=1, source_target_pairs={{0,4},{1,5},{2,6},{3,7},{4,0},{5,1},{6,2},{7,3},{8,12},{9,13},{10,... | collective-permute-start | bytes 691208 | tf_op jit(solution)/shard_map/ppermute | solution.py:25
  25.7 23.6 %collective-permute-start.3 = (f32[64,1800]{1,0:T(8,128)S(1)}, f32[64,1800]{1,0:T(8,128)S(1)}, u32[]{:S(2)}, u32[]{:S(2)}) collective-permute-start(f32[64,1800]{1,0:T(8,128)S(1)} %maximum_select_fusion.1), channel_id=1, source_target_pairs={{0,8},{1,9},{2,10},{3,11},{4,12},{5,13},{6,14},{7,15},{8,0},{9,1},... | collective-permute-start | bytes 1382408 | tf_op jit(solution)/shard_map/ppermute | solution.py:25
  57.6 7.9 %copy-start.1 = (f32[64,225]{1,0:T(8,128)S(1)}, f32[64,225]{1,0:T(8,128)}, u32[]{:S(2)}) copy-start(f32[64,225]{1,0:T(8,128)} %param.15) | copy-start | bytes 172804
  57.6 8.0 %copy-start.2 = (f32[64,225]{1,0:T(8,128)S(1)}, f32[64,225]{1,0:T(8,128)}, u32[]{:S(2)}) copy-start(f32[64,225]{1,0:T(8,128)} %param.16) | copy-start | bytes 172804
  57.6 8.0 %copy-start.3 = (f32[64]{0:T(128)S(1)}, f32[64]{0:T(128)}, u32[]{:S(2)}) copy-start(f32[64]{0:T(128)} %param.14) | copy-start | bytes 772
where the time goes:
time: 69.5 us; the launch traced here: 69.1 us
  waiting for transfers between devices  28.1 us (40%)
  local copies, waits for them, and re-layouts  13.8 us (20%)
  matrix products  8.74 us (13%)
  starting transfers between devices  7.75 us (11%)
  other arithmetic  7.12 us (10%)
  between operations  3.57 us (5%)
    ppermute x4, waiting for transfers between devices, from_partner(): return lax.ppermute(value, axis, pairs)  28.1 us
    ppermute x4, starting transfers between devices, from_partner(): return lax.ppermute(value, axis, pairs)  7.75 us
    transpose x1, local copies, waits for them, and re-layouts, body(): frame_data.reshape(channels, 2, 2, PH, PW).transpose(0, 3, 1, 4, 2)  6.91 us
    reshape x1, local copies, waits for them, and re-layouts, body(): frame_data.reshape(channels, 2, 2, PH, PW).transpose(0, 3, 1, 4, 2)  5.13 us
    dot_general x1, matrix products, body(): lax.dot_general(head_weight, normed, (((0,), (1,)), ((), ())), preferred_...  3.51 us
    reduce_sum x1, other arithmetic, body(): jnp.sum(values, axis=1)  2.45 us
    dot_general x1, matrix products, body(): jnp.einsum('ij,cjw->ciw', row_part, planes, precision=HIGHEST)  2.14 us
    select_n x4, other arithmetic, body(): jnp.where(upper_half, jnp.concatenate([partner, frame_data], axis=1), jnp...  1.7 us
  transfers between devices with their start and end apart: 4, of which 3 were waited for; matrix products, arithmetic and copies ran while one was open for 12% of the time, Pallas kernels for 0%

commit v1 on v0

v1 whole, which is shorter than its diff:
```python
import functools
import math

import jax
import jax.numpy as jnp
from jax import lax
from jax.experimental import pallas as pl
from jax.experimental.pallas import tpu as pltpu
from jax.sharding import PartitionSpec as P


D = 5120
H = 90
W = 160
PH = 45
PW = 80
NSTEP = 50

EPSILON = 1e-06
GUIDE_EXTRA = 4.0
SHIFT_FACTOR = 5.0
LANES = 128


def sigma_at(step_number):
    remain = 1.0 - step_number.astype(jnp.float32) / NSTEP
    return SHIFT_FACTOR * remain / (1.0 + (SHIFT_FACTOR - 1.0) * remain)


def band_weights(skip_flags, step_index, band_gain):
    current = step_index[0]
    counter = jnp.arange(NSTEP, dtype=jnp.int32)
    computed = (skip_flags == 0) & (counter <= current)
    last_full = jnp.max(jnp.where(computed, counter, -1))
    spacing = (current - last_full).astype(jnp.float32)
    gap_ratio = spacing / (spacing + 2.0)
    return (band_gain[0] * (1.0 + gap_ratio), band_gain[1] * (1.0 - 0.5 * gap_ratio))


def split(value):
    high = value.astype(jnp.bfloat16)
    return high, (value - high.astype(jnp.float32)).astype(jnp.bfloat16)


def dot3(left, right, contract=((1,), (0,))):
    (lh, ll), (rh, rl) = left, right

    def dot(one, other):
        return lax.dot_general(
            one, other, (contract, ((), ())), preferred_element_type=jnp.float32
        )

    return dot(lh, rh) + (dot(ll, rh) + dot(lh, rl))


def iota(shape, axis):
    return lax.broadcasted_iota(jnp.int32, shape, axis)


class Layout:
    def __init__(self, local_rows, local_tokens):
        self.rows = local_rows
        self.tokens = local_tokens
        self.channels = local_rows // 4
        self.members = PH * PW // local_tokens
        bits = self.members.bit_length() - 1
        self.near = 1 << (bits // 2)
        self.far = self.members // self.near
        self.span = max(
            (p * local_tokens % PW + local_tokens + PW - 1) // PW
            for p in range(self.members)
        )
        self.lines = 2 * self.span
        self.groups = pl.cdiv(self.span * PW, LANES)

    def owners(self, position):
        givers = [position ^ (k * self.near) for k in range(self.far)]
        takers = [position ^ m for m in range(self.near)]
        return givers, takers

    def offset(self, owner):
        return lax.rem(owner * self.tokens, PW)

    def first_line(self, owner):
        return 2 * (owner * self.tokens // PW)


def wave_tables(places, length, cutoff):
    modes = iota(places.shape, 1)
    turns = lax.rem(places * modes, length).astype(jnp.float32)
    angles = turns * (2.0 * math.pi / length)
    table = jnp.concatenate([jnp.cos(angles), jnp.sin(angles)], axis=1)
    weight = jnp.where((modes == 0) | (2 * modes == length), 1.0, 2.0) / length
    kept = jnp.where((modes <= cutoff) & (2 * modes <= length), weight, 0.0)
    return table, jnp.concatenate([kept, kept], axis=1)


def bands_kernel(layout, cut_rows, cut_cols, col_high, col_low, row_high, row_low):
    seq_index = lax.axis_index("seq")
    position = lax.rem(seq_index, layout.members)
    frame = seq_index // layout.members
    shape = (2 * LANES, LANES)
    line = iota(shape, 0)
    odd = line >= LANES
    column = jnp.where(odd, line - LANES, line)
    table, kept = wave_tables(2 * column + odd.astype(jnp.int32), W, cut_cols[frame])
    table = jnp.where(jnp.concatenate([column, column], axis=1) < PW, table, 0.0)
    high, low = split(dot3(split(table * kept), split(table), ((1,), (1,))))
    col_high[...] = high
    col_low[...] = low

    def tables(owners):
        shape = (len(owners) * layout.lines, LANES)
        line = iota(shape, 0)
        places = line
        for n, owner in enumerate(owners):
            start = layout.first_line(owner) - n * layout.lines
            places = jnp.where(line >= n * layout.lines, line + start, places)
        return wave_tables(places, H, cut_rows[frame])

    givers, takers = layout.owners(position)
    given, kept = tables(givers)
    taken, _ = tables(takers)
    small = dot3(split(taken), split(given * kept), ((1,), (1,)))
    wide = given.shape[0]
    size = wide * layout.channels
    spread = (iota((wide, size), 1) // layout.channels == iota((wide, size), 0)).astype(
        jnp.bfloat16
    )
    shape = (layout.channels, size)
    same = lax.rem(iota(shape, 1), layout.channels) == iota(shape, 0)
    for part, out in zip(split(small), (row_high, row_low)):
        repeated = jnp.dot(part, spread, preferred_element_type=jnp.float32)
        for n in range(taken.shape[0]):
            block = jnp.where(same, repeated[n : n + 1], 0.0)
            place = slice(n * layout.channels, (n + 1) * layout.channels)
            out[place, :] = block.astype(jnp.bfloat16)


def mix_kernel(layout, *refs):
    far, near, span, groups = layout.far, layout.near, layout.span, layout.groups
    channels, tokens = layout.channels, layout.tokens
    col_high, col_low, row_high, row_low = refs[:4]
    sources = refs[4 : 4 + far]
    outs = refs[4 + far : 4 + far + near]
    window, lines, data_high, data_low = refs[4 + far + near :]
    givers, takers = layout.owners(lax.rem(lax.axis_index("seq"), layout.members))
    lane = iota((layout.rows, LANES), 1)
    chunks = window.shape[1] // LANES
    blank = jnp.zeros((layout.rows, LANES), jnp.float32)
    window[...] = jnp.zeros_like(window)
    for k in range(far):
        window[:, :tokens] = sources[k][...]
        offset = layout.offset(givers[k])
        turned = [
            pltpu.roll(window[:, g * LANES : (g + 1) * LANES], offset, 1) for g in range(chunks)
        ]
        turned = [blank] + turned + [blank] * (groups - chunks)
        placed = [jnp.where(lane >= offset, turned[g + 1], turned[g]) for g in range(groups)]
        for r in range(span):
            group, start = divmod(r * PW, LANES)
            if start == 0:
                line = placed[group]
            else:
                line = pltpu.roll(placed[group], LANES - start, 1)
                if start + PW > LANES:
                    rest = pltpu.roll(placed[group + 1], LANES - start, 1)
                    line = jnp.where(lane < LANES - start, line, rest)
            lines[r] = line
        for r in range(span):
            for dy in range(2):
                first = ((k * span + r) * 2 + dy) * channels
                for dx in range(2):
                    high, low = split(lines[r, pl.ds(2 * dy + dx, channels, stride=4), :])
                    place = (slice(first, first + channels), slice(dx * LANES, (dx + 1) * LANES))
                    data_high[place] = high
                    data_low[place] = low
    mixed = dot3((data_high[...], data_low[...]), (col_high[...], col_low[...]))
    mixed = dot3((row_high[...], row_low[...]), split(mixed))
    lane = iota((channels, LANES), 1)
    for m in range(near):
        offset = layout.offset(takers[m])
        back = lax.rem(LANES - offset, LANES)
        for dy in range(2):
            for dx in range(2):
                placed = [None] * (groups + 1)

                def put(group, value):
                    old = placed[group]
                    placed[group] = value if old is None else old + value

                for r in range(span):
                    first = ((m * span + r) * 2 + dy) * channels
                    line = mixed[first : first + channels, dx * LANES : (dx + 1) * LANES]
                    group, start = divmod(r * PW, LANES)
                    if start:
                        line = pltpu.roll(line, start, 1)
                    if start + PW <= LANES:
                        put(group, line)
                    else:
                        put(group, jnp.where(lane >= start, line, 0.0))
                        put(group + 1, jnp.where(lane < start, line, 0.0))
                turned = [pltpu.roll(p, back, 1) for p in placed[:groups]]
                first = (dy * 2 + dx) * channels
                for g in range(pl.cdiv(tokens, LANES)):
                    value = jnp.where(lane < LANES - offset, turned[g], turned[g + 1])
                    last = min(tokens, (g + 1) * LANES)
                    outs[m][first : first + channels, g * LANES : last] = value[
                        :, : last - g * LANES
                    ]


def finish_kernel(layout, *refs):
    near, channels, tokens = layout.near, layout.channels, layout.tokens
    parts = refs[:near]
    base, row_low, step, latent, velocity, latent_next, total = refs[near:]
    for g in range(total.shape[0]):
        last = min(tokens, (g + 1) * LANES)
        columns = slice(g * LANES, last)
        width = slice(0, last - g * LANES)
        low_band = parts[0][:, columns]
        for m in range(1, near):
            low_band += parts[m][:, columns]
        total[g, :, width] = low_band
        for c in range(channels):
            rows = slice(4 * c, 4 * c + 4)
            low_band = total[g, pl.ds(c, 4, stride=channels), :][:, width]
            value = base[rows, columns] + row_low[rows, columns] * low_band
            velocity[rows, columns] = value
            latent_next[rows, columns] = latent[rows, columns] + step[rows, columns] * value


VMEM = pl.BlockSpec(memory_space=pltpu.VMEM)
SMEM = pl.BlockSpec(memory_space=pltpu.SMEM)


def bands(layout, cut_rows, cut_cols):
    wide = layout.far * layout.lines * layout.channels
    tall = layout.near * layout.lines * layout.channels
    col = jax.ShapeDtypeStruct((2 * LANES, 2 * LANES), jnp.bfloat16)
    row = jax.ShapeDtypeStruct((tall, wide), jnp.bfloat16)
    return pl.pallas_call(
        functools.partial(bands_kernel, layout),
        out_shape=[col, col, row, row],
        in_specs=[SMEM, SMEM],
        out_specs=[VMEM] * 4,
        compiler_params=pltpu.CompilerParams(vmem_limit_bytes=8 * 2**20),
        cost_estimate=pl.CostEstimate(flops=10**8, bytes_accessed=10**6, transcendentals=0),
        name="bands",
    )(cut_rows, cut_cols)


def mix(layout, filters, sources):
    wide = layout.far * layout.lines * layout.channels
    shape = (layout.rows, layout.tokens)
    data = pltpu.VMEM((wide, 2 * LANES), jnp.bfloat16)
    return pl.pallas_call(
        functools.partial(mix_kernel, layout),
        out_shape=[jax.ShapeDtypeStruct(shape, jnp.float32)] * layout.near,
        in_specs=[VMEM] * (4 + layout.far),
        out_specs=[VMEM] * layout.near,
        scratch_shapes=[
            pltpu.VMEM((layout.rows, pl.cdiv(layout.tokens, LANES) * LANES), jnp.float32),
            pltpu.VMEM((layout.span, layout.rows, LANES), jnp.float32),
            data,
            data,
        ],
        compiler_params=pltpu.CompilerParams(vmem_limit_bytes=8 * 2**20),
        cost_estimate=pl.CostEstimate(flops=10**9, bytes_accessed=10**6, transcendentals=0),
        name="mix",
    )(*filters, *sources)


def finish(layout, parts, base, row_low, step, latent):
    shape = jax.ShapeDtypeStruct((layout.rows, layout.tokens), jnp.float32)
    return pl.pallas_call(
        functools.partial(finish_kernel, layout),
        out_shape=[shape, shape],
        in_specs=[VMEM] * (layout.near + 4),
        out_specs=[VMEM, VMEM],
        scratch_shapes=[
            pltpu.VMEM((pl.cdiv(layout.tokens, LANES), layout.rows, LANES), jnp.float32)
        ],
        compiler_params=pltpu.CompilerParams(vmem_limit_bytes=8 * 2**20),
        name="finish",
    )(*parts, base, row_low, step, latent)


def body(
    hidden,
    modulation,
    head_weight,
    head_bias,
    residual,
    latent,
    band_gain,
    cut_rows,
    cut_cols,
    skip_flags,
    step_index,
):
    layout = Layout(*residual.shape)
    places = lax.axis_size("seq")

    def exchange(values, unit):
        swapped = [values[0]] * len(values)
        for n in [*range(2, len(values)), 1]:
            pairs = [(s, s ^ (n * unit)) for s in range(places)]
            swapped[n] = lax.ppermute(values[n], "seq", pairs)
        return swapped

    sources = exchange([residual] * layout.far, layout.near)
    filters = bands(layout, cut_rows, cut_cols)
    values = hidden.astype(jnp.float32)
    moments = lax.psum((jnp.sum(values, axis=1), jnp.sum(values * values, axis=1)), "mp")
    average = moments[0] / D
    scale_inv = lax.rsqrt(moments[1] / D - average * average + EPSILON)
    normed = (
        (values - average[:, None]) * scale_inv[:, None] * (1.0 + modulation[1]) + modulation[0]
    ).astype(jnp.bfloat16)
    conditional = (
        lax.psum_scatter(
            lax.dot_general(
                head_weight, normed, (((0,), (1,)), ((), ())), preferred_element_type=jnp.float32
            ),
            "mp",
            scatter_dimension=0,
            tiled=True,
        )
        + head_bias[:, None]
    )
    w_low, w_high = band_weights(skip_flags, step_index, band_gain)
    row_high = GUIDE_EXTRA * jnp.repeat(w_high, 4)[:, None]
    row_low = GUIDE_EXTRA * jnp.repeat(w_low - w_high, 4)[:, None]
    base = conditional + row_high * residual
    current = step_index[0]
    step = sigma_at(current + 1) - sigma_at(current)

    parts = mix(layout, filters, sources)
    parts = exchange(parts, 1)
    shape = residual.shape
    return finish(
        layout,
        parts,
        base,
        jnp.broadcast_to(row_low, shape),
        jnp.broadcast_to(step, shape),
        latent,
    )


def solution(mesh):
    in_specs = (
        P(("groups", "seq"), "mp"),
        P("groups", "mp"),
        P("mp", None),
        P("mp"),
        P("mp", ("groups", "seq")),
        P("mp", ("groups", "seq")),
        P(None, "mp"),
        P("groups"),
        P("groups"),
        P("groups"),
        P("groups"),
    )
    out_specs = (P("mp", ("groups", "seq")), P("mp", ("groups", "seq")))
    return jax.shard_map(body, mesh=mesh, in_specs=in_specs, out_specs=out_specs, check_vma=False)
```

time: 69.5 us -> 23 us (0.33)
  waiting for transfers between devices: 28.1 us -> 0.81 us
  local copies, waits for them, and re-layouts: 13.8 us -> 0.42 us
  matrix products: 8.74 us -> 2.88 us
  Pallas kernels: 0 us -> 3.37 us
  other arithmetic: 7.12 us -> 4 us
    ppermute x4 -> x6, waiting for transfers between devices: 28.1 us -> 0.81 us  [exchange(): swapped[n] = lax.ppermute(values[n], 'seq', pairs)]
    transpose x2 -> x0, local copies, waits for them, and re-layouts: 7 us -> none  [the longest x1 6.91 us: body(): frame_data.reshape(channels, 2, 2, PH, PW).transpose(0, 3, 1, 4, 2)]
    reshape x2 -> x0, local copies, waits for them, and re-layouts: 5.25 us -> none  [the longest x1 5.13 us: body(): frame_data.reshape(channels, 2, 2, PH, PW).transpose(0, 3, 1, 4, 2)]
    dot_general x6 -> x0, matrix products: 5.23 us -> none  [the longest x1 2.14 us: body(): jnp.einsum('ij,cjw->ciw', row_part, planes, precision=HIGHEST)]
    pallas_call x0 -> x3, Pallas kernels: none -> 3.37 us  [the longest x1 1.72 us: mix(): pl.pallas_call(functools.partial(mix_kernel, layout), out_shape=[jax.Shap...]
    select_n x4 -> x0, other arithmetic: 1.7 us -> none  [body(): jnp.where(upper_half, jnp.concatenate([partner, frame_data], axis=1), jnp...]
    select_n x1 -> x0, local copies, waits for them, and re-layouts: 1.1 us -> none  [body(): jnp.where(upper_half, jnp.concatenate([partner, frame_data], axis=1), jnp...]
    mul x1, other arithmetic: 0.76 us -> 0.01 us  [body(): row_low = GUIDE_EXTRA * jnp.repeat(w_low - w_high, 4)[:, None]]
  transfers between devices with their start and end apart: 4 -> 6, of which waited for: 3 -> 1; matrix products, arithmetic and copies ran while one was open for 12% -> 32% of each run, Pallas kernels for 0% -> 4%
where the time goes in v1:
time: 23 us; the launch traced here: 22.7 us
  starting transfers between devices  7.63 us (33%)
  other arithmetic  4 us (17%)
  between operations  3.57 us (16%)
  Pallas kernels  3.37 us (15%)
  matrix products  2.88 us (13%)
  waiting for transfers between devices  0.81 us (4%)
  local copies, waits for them, and re-layouts  0.42 us (2%)
    ppermute x6, starting transfers between devices, exchange(): swapped[n] = lax.ppermute(values[n], 'seq', pairs)  7.63 us
    dot_general x1, matrix products, body(): lax.dot_general(head_weight, normed, (((0,), (1,)), ((), ())), preferred_...  2.88 us
    reduce_sum x1, other arithmetic, body(): jnp.sum(values, axis=1)  2.45 us
    pallas_call x1, Pallas kernels, mix(): pl.pallas_call(functools.partial(mix_kernel, layout), out_shape=[jax.Shap...  1.72 us
    pallas_call x1, Pallas kernels, bands(): pl.pallas_call(functools.partial(bands_kernel, layout), out_shape=[col, c...  0.91 us
    add x1, other arithmetic, body(): 1.0 + modulation[1]  0.9 us
    ppermute x6, waiting for transfers between devices, exchange(): swapped[n] = lax.ppermute(values[n], 'seq', pairs)  0.81 us
    pallas_call x1, Pallas kernels, finish(): pl.pallas_call(functools.partial(finish_kernel, layout), out_shape=[shape...  0.73 us
  transfers between devices with their start and end apart: 6, of which 1 were waited for; matrix products, arithmetic and copies ran while one was open for 32% of the time, Pallas kernels for 4%

profile of v1, /device:TPU:0, one launch (start us, length us, event | category | flops | bytes accessed | tf_op | source)
XLA Modules:
  0.0 22.7 jit_solution(14883558842520735099)
XLA Ops:
  0.6 0.0 copy-start
  0.6 0.0 copy-start.2
  0.7 0.0 copy-start.4
  0.7 0.0 copy-start.3
  0.7 3.1 %collective-permute-start = (f32[64,225]{1,0:T(8,128)}, f32[64,225]{1,0:T(8,128)S(1)}, u32[]{:S(2)}, u32[]{:S(2)}) collective-permute-start(f32[64,225]{1,0:T(8,128)} %refs_4_.1), channel_id=1, source_target_pairs={{0,4},{1,5},{2,6},{3,7},{4,0},{5,1},{6,2},{7,3},{8,12},{9,13},{10,... | collective-permute-start | bytes 172808 | tf_op jit(solution)/shard_map/ppermute | solution.py:309
  3.8 2.6 %collective-permute-start.1 = (f32[64,225]{1,0:T(8,128)}, f32[64,225]{1,0:T(8,128)S(1)}, u32[]{:S(2)}, u32[]{:S(2)}) collective-permute-start(f32[64,225]{1,0:T(8,128)} %refs_4_.1), channel_id=1, source_target_pairs={{0,8},{1,9},{2,10},{3,11},{4,12},{5,13},{6,14},{7,15},{8,0},{9,1},... | collective-permute-start | bytes 172808 | tf_op jit(solution)/shard_map/ppermute | solution.py:309
  6.4 0.0 collective-permute-start.2
  6.4 0.9 %slice_add_fusion = (f32[1,5120]{1,0:T(1,128)S(1)}, f32[1,5120]{1,0:T(1,128)S(1)}) fusion(f32[2,5120]{1,0:T(2,128)} %param.12), kind=kLoop, calls=%fused_computation.12 | loop fusion | flops 5120 | bytes 81920 | tf_op jit(solution)/shard_map/add | solution.py:319
  7.3 2.4 %convert_reduce_fusion = (f32[225]{0:T(256)S(1)}, f32[225]{0:T(256)S(1)}) fusion(bf16[225,5120]{1,0:T(8,128)(2,1)} %param.11), kind=kLoop, calls=%fused_computation.2 | loop fusion | flops 4607550 | bytes 2305800 | tf_op jit(solution)/shard_map/reduce_sum | solution.py:315
  9.7 0.0 copy-start.5
  10.4 0.0 copy-done.4
  10.4 0.6 %fusion.16 = s32[]{:T(128)} fusion(s32[50]{0:T(128)S(1)} %copy-done.4, s32[]{:T(128)} %bitcast.12), kind=kLoop, calls=%fused_computation.17 | loop fusion | flops 249 | bytes 208 | tf_op jit(solution)/shard_map/reduce_max | solution.py:34
  11.8 0.0 copy-done.3
  13.1 0.1 broadcast_in_dim.23
  13.2 0.1 mul.103
  13.2 0.9 %bands.1 = (bf16[256,256]{1,0:T(8,128)(2,1)S(1)}, bf16[256,256]{1,0:T(8,128)(2,1)S(1)}, bf16[512,512]{1,0:T(8,128)(2,1)S(1)}, bf16[512,512]{1,0:T(8,128)(2,1)S(1)}) custom-call(s32[1]{0:T(128)S(6)} %copy.13.cut_rows, s32[1]{0:T(128)S(6)} %copy.14.cut_cols), custom_call_target="tpu_custom_call" | custom-call | flops 100000000 | bytes 1000000 | tf_op jit(solution)/shard_map/bands/pallas_call | solution.py:242
  14.2 0.0 collective-permute-done.refs_5_
  14.2 0.0 collective-permute-done.1.refs_6_
  14.2 0.0 collective-permute-done.2.refs_7_
  14.2 0.0 copy-done.2
  14.2 1.7 %mix.1 = (f32[64,225]{1,0:T(8,128)S(1)}, f32[64,225]{1,0:T(8,128)S(1)}, f32[64,225]{1,0:T(8,128)S(1)}, f32[64,225]{1,0:T(8,128)S(1)}) custom-call(bf16[256,256]{1,0:T(8,128)(2,1)S(1)} %get-tuple-element.10.refs_0_, bf16[256,256]{1,0:T(8,128)(2,1)S(1)} %get-tuple-element.11.refs_1_, bf16[512,512]{1,0:T(8,128)(2,1)S(1)} %get-tuple-element.12.refs_2_, ...), custom_call_target="tpu_custom_call" | custom-call | flops 1000000000 | bytes 1000000 | tf_op jit(solution)/shard_map/mix/pallas_call | solution.py:257
  15.9 0.1 collective-permute-start.3
  16.0 1.8 %collective-permute-start.4 = (f32[64,225]{1,0:T(8,128)S(1)}, f32[64,225]{1,0:T(8,128)S(1)}, u32[]{:S(2)}, u32[]{:S(2)}) collective-permute-start(f32[64,225]{1,0:T(8,128)S(1)} %get-tuple-element.16), channel_id=1, source_target_pairs={{0,2},{1,3},{2,0},{3,1},{4,6},{5,7},{6,4},{7,5},{8,10},{9,11},{10,... | collective-permute-start | bytes 172808 | tf_op jit(solution)/shard_map/ppermute | solution.py:309
  17.8 0.1 collective-permute-start.5
  17.9 0.0 copy-done
  17.9 0.0 copy-done.5
  17.9 0.0 copy-start.1
  17.9 2.9 %fusion.13.refs_4_ = f32[64,225]{1,0:T(8,128)S(1)} fusion(bf16[5120,64]{0,1:T(8,128)(2,1)S(1)} %copy-done, bf16[225,5120]{1,0:T(8,128)(2,1)} %param.11, f32[5120]{0:T(1024)S(1)} %bitcast.17, f32[5120]{0:T(1024)S(1)} %bitcast.16, f32[225]{0:T(256)S(1)} %get-tuple-element.25, f32[225]{0:T(256)S(1)} %get-tuple-element.24, f32[64,225]{1,0:T(8,128)S(1)} %copy-done.2, ...), kind=kOutput, calls=%fused_computation.11 | convolution fusion | flops 154411200 | bytes 3117832 | tf_op jit(solution)/shard_map/dot_general | solution.py:323
  20.8 0.1 broadcast_in_dim.24
  20.8 0.1 mul.110
  21.0 0.0 collective-permute-done.3.refs_1_
  21.0 0.0 collective-permute-done.4.refs_2_
  21.1 0.8 %collective-permute-done.5.refs_3_ = f32[64,225]{1,0:T(8,128)S(1)} collective-permute-done((f32[64,225]{1,0:T(8,128)S(1)}, f32[64,225]{1,0:T(8,128)S(1)}, u32[]{:S(2)}, u32[]{:S(2)}) %collective-permute-start.5) | collective-permute-done | bytes 57632 | tf_op jit(solution)/shard_map/ppermute | solution.py:309
  21.9 0.1 broadcast_in_dim.25.refs_5_
  21.9 0.0 copy-done.1
  21.9 0.7 %finish.1 = (f32[64,225]{1,0:T(8,128)}, f32[64,225]{1,0:T(8,128)}) custom-call(f32[64,225]{1,0:T(8,128)S(1)} %get-tuple-element.14.refs_0_, f32[64,225]{1,0:T(8,128)S(1)} %collective-permute-done.3.refs_1_, f32[64,225]{1,0:T(8,128)S(1)} %collective-permute-done.4.refs_2_, f32[64,225]{1,0:T(8,128)S(1)} %collective-permute-done.5.refs_3_, ...), custom_call_target="tpu_custom_call" | custom-call | tf_op jit(solution)/shard_map/finish/pallas_call | solution.py:276
  (3 shorter events, 0.0 us)
Async XLA Ops:
  0.6 17.2 %copy-start = (bf16[5120,64]{0,1:T(8,128)(2,1)S(1)}, bf16[5120,64]{0,1:T(8,128)(2,1)}, u32[]{:S(2)}) copy-start(bf16[5120,64]{0,1:T(8,128)(2,1)} %param.13) | copy-start | bytes 1966084
  0.6 13.6 %copy-start.2 = (f32[64,225]{1,0:T(8,128)S(1)}, f32[64,225]{1,0:T(8,128)}, u32[]{:S(2)}) copy-start(f32[64,225]{1,0:T(8,128)} %refs_4_.1) | copy-start | bytes 172804
  0.7 9.8 %copy-start.4 = (s32[50]{0:T(128)S(1)}, s32[50]{0:T(128)}, u32[]{:S(2)}) copy-start(s32[50]{0:T(128)} %param.20) | copy-start | bytes 604
  0.7 11.1 %copy-start.3 = (f32[2,16]{1,0:T(2,128)S(1)}, f32[2,16]{1,0:T(2,128)}, u32[]{:S(2)}) copy-start(f32[2,16]{1,0:T(2,128)} %param.17) | copy-start | bytes 388
  0.7 13.5 %collective-permute-start = (f32[64,225]{1,0:T(8,128)}, f32[64,225]{1,0:T(8,128)S(1)}, u32[]{:S(2)}, u32[]{:S(2)}) collective-permute-start(f32[64,225]{1,0:T(8,128)} %refs_4_.1), channel_id=1, source_target_pairs={{0,4},{1,5},{2,6},{3,7},{4,0},{5,1},{6,2},{7,3},{8,12},{9,13},{10,... | collective-permute-start | bytes 172808 | tf_op jit(solution)/shard_map/ppermute | solution.py:309
  3.8 10.4 %collective-permute-start.1 = (f32[64,225]{1,0:T(8,128)}, f32[64,225]{1,0:T(8,128)S(1)}, u32[]{:S(2)}, u32[]{:S(2)}) collective-permute-start(f32[64,225]{1,0:T(8,128)} %refs_4_.1), channel_id=1, source_target_pairs={{0,8},{1,9},{2,10},{3,11},{4,12},{5,13},{6,14},{7,15},{8,0},{9,1},... | collective-permute-start | bytes 172808 | tf_op jit(solution)/shard_map/ppermute | solution.py:309
  6.4 7.8 %collective-permute-start.2 = (f32[64,225]{1,0:T(8,128)}, f32[64,225]{1,0:T(8,128)S(1)}, u32[]{:S(2)}, u32[]{:S(2)}) collective-permute-start(f32[64,225]{1,0:T(8,128)} %refs_4_.1), channel_id=1, source_target_pairs={{0,12},{1,13},{2,14},{3,15},{4,8},{5,9},{6,10},{7,11},{8,4},{9,5},... | collective-permute-start | bytes 172808 | tf_op jit(solution)/shard_map/ppermute | solution.py:309
  9.7 8.1 %copy-start.5 = (f32[64]{0:T(128)S(1)}, f32[64]{0:T(128)}, u32[]{:S(2)}) copy-start(f32[64]{0:T(128)} %param.14) | copy-start | bytes 772
  15.9 5.1 %collective-permute-start.3 = (f32[64,225]{1,0:T(8,128)S(1)}, f32[64,225]{1,0:T(8,128)S(1)}, u32[]{:S(2)}, u32[]{:S(2)}) collective-permute-start(f32[64,225]{1,0:T(8,128)S(1)} %get-tuple-element.15), channel_id=1, source_target_pairs={{0,1},{1,0},{2,3},{3,2},{4,5},{5,4},{6,7},{7,6},{8,9},{9,8},{10,11... | collective-permute-start | bytes 172808 | tf_op jit(solution)/shard_map/ppermute | solution.py:309
  16.0 5.0 %collective-permute-start.4 = (f32[64,225]{1,0:T(8,128)S(1)}, f32[64,225]{1,0:T(8,128)S(1)}, u32[]{:S(2)}, u32[]{:S(2)}) collective-permute-start(f32[64,225]{1,0:T(8,128)S(1)} %get-tuple-element.16), channel_id=1, source_target_pairs={{0,2},{1,3},{2,0},{3,1},{4,6},{5,7},{6,4},{7,5},{8,10},{9,11},{10,... | collective-permute-start | bytes 172808 | tf_op jit(solution)/shard_map/ppermute | solution.py:309
  17.8 4.1 %collective-permute-start.5 = (f32[64,225]{1,0:T(8,128)S(1)}, f32[64,225]{1,0:T(8,128)S(1)}, u32[]{:S(2)}, u32[]{:S(2)}) collective-permute-start(f32[64,225]{1,0:T(8,128)S(1)} %get-tuple-element.17), channel_id=1, source_target_pairs={{0,3},{1,2},{2,1},{3,0},{4,7},{5,6},{6,5},{7,4},{8,11},{9,10},{10,... | collective-permute-start | bytes 172808 | tf_op jit(solution)/shard_map/ppermute | solution.py:309
  17.9 4.1 %copy-start.1 = (f32[64,225]{1,0:T(8,128)S(1)}, f32[64,225]{1,0:T(8,128)}, u32[]{:S(2)}) copy-start(f32[64,225]{1,0:T(8,128)} %refs_7_.1) | copy-start | bytes 172804

commit v2 on v1

--- a/solution.py
+++ b/solution.py
@@ -74,9 +74,12 @@
         self.groups = pl.cdiv(self.span * PW, LANES)
 
     def owners(self, position):
-        givers = [position ^ (k * self.near) for k in range(self.far)]
+        givers = [position ^ (k * self.near) for k in self.order(self.far)]
         takers = [position ^ m for m in range(self.near)]
         return givers, takers
+
+    def order(self, count):
+        return [0, *range(2, count), 1][:count]
 
     def offset(self, owner):
         return lax.rem(owner * self.tokens, PW)
@@ -137,21 +140,18 @@
             out[place, :] = block.astype(jnp.bfloat16)
 
 
-def mix_kernel(layout, *refs):
-    far, near, span, groups = layout.far, layout.near, layout.span, layout.groups
-    channels, tokens = layout.channels, layout.tokens
-    col_high, col_low, row_high, row_low = refs[:4]
-    sources = refs[4 : 4 + far]
-    outs = refs[4 + far : 4 + far + near]
-    window, lines, data_high, data_low = refs[4 + far + near :]
-    givers, takers = layout.owners(lax.rem(lax.axis_index("seq"), layout.members))
+def filtered(layout, slots, sources, filters, scratch):
+    span, groups, channels, tokens = layout.span, layout.groups, layout.channels, layout.tokens
+    col_high, col_low, row_high, row_low = filters
+    window, lines, data_high, data_low = scratch
+    givers, _ = layout.owners(lax.rem(lax.axis_index("seq"), layout.members))
     lane = iota((layout.rows, LANES), 1)
     chunks = window.shape[1] // LANES
     blank = jnp.zeros((layout.rows, LANES), jnp.float32)
     window[...] = jnp.zeros_like(window)
-    for k in range(far):
-        window[:, :tokens] = sources[k][...]
-        offset = layout.offset(givers[k])
+    for k, (slot, source) in enumerate(zip(slots, sources)):
+        window[:, :tokens] = source[...]
+        offset = layout.offset(givers[slot])
         turned = [
             pltpu.roll(window[:, g * LANES : (g + 1) * LANES], offset, 1) for g in range(chunks)
         ]
@@ -176,7 +176,26 @@
                     data_high[place] = high
                     data_low[place] = low
     mixed = dot3((data_high[...], data_low[...]), (col_high[...], col_low[...]))
-    mixed = dot3((row_high[...], row_low[...]), split(mixed))
+    each = layout.lines * channels
+    columns = slice(slots[0] * each, (slots[-1] + 1) * each)
+    return dot3((row_high[:, columns], row_low[:, columns]), split(mixed))
+
+
+def early_kernel(layout, slots, *refs):
+    sources = refs[4 : 4 + len(slots)]
+    carry = refs[4 + len(slots)]
+    carry[...] = filtered(layout, slots, sources, refs[:4], refs[5 + len(slots) :])
+
+
+def mix_kernel(layout, slots, *refs):
+    near, span, groups = layout.near, layout.span, layout.groups
+    channels, tokens = layout.channels, layout.tokens
+    carry = refs[4]
+    sources = refs[5 : 5 + len(slots)]
+    outs = refs[5 + len(slots) : 5 + len(slots) + near]
+    scratch = refs[5 + len(slots) + near :]
+    mixed = carry[...] + filtered(layout, slots, sources, refs[:4], scratch)
+    _, takers = layout.owners(lax.rem(lax.axis_index("seq"), layout.members))
     lane = iota((channels, LANES), 1)
     for m in range(near):
         offset = layout.offset(takers[m])
@@ -210,6 +229,79 @@
                     ]
 
 
+def head_kernel(
+    layout,
+    hidden,
+    modulation,
+    weight,
+    bias,
+    residual,
+    band_gain,
+    skip_flags,
+    step_index,
+    base,
+    row_low,
+    step,
+    normed,
+):
+    tokens, width = hidden.shape
+    tiles = width // LANES
+    block = 16
+
+    def norm(rows):
+        count = rows.size if isinstance(rows, pl.Slice) else rows.stop - rows.start
+        sums = [jnp.zeros((count, LANES), jnp.float32) for _ in range(4)]
+        squares = list(sums)
+        for t in range(tiles):
+            value = hidden[rows, t * LANES : (t + 1) * LANES].astype(jnp.float32)
+            sums[t % 4] += value
+            squares[t % 4] += value * value
+        total = jnp.sum((sums[0] + sums[1]) + (sums[2] + sums[3]), axis=1, keepdims=True)
+        square = jnp.sum(
+            (squares[0] + squares[1]) + (squares[2] + squares[3]), axis=1, keepdims=True
+        )
+        average = total / D
+        scale_inv = lax.rsqrt(square / D - average * average + EPSILON)
+        average = jnp.broadcast_to(average, (count, LANES))
+        scale_inv = jnp.broadcast_to(scale_inv, (count, LANES))
+        for t in range(tiles):
+            columns = slice(t * LANES, (t + 1) * LANES)
+            value = hidden[rows, columns].astype(jnp.float32)
+            value = (value - average) * scale_inv
+            value = value * (1.0 + modulation[1:2, columns]) + modulation[0:1, columns]
+            normed[rows, columns] = value.astype(jnp.bfloat16)
+
+    @pl.loop(0, tokens // block)
+    def _(n):
+        norm(pl.ds(pl.multiple_of(n * block, block), block))
+
+    if tokens % block:
+        norm(slice(tokens // block * block, tokens))
+    conditional = lax.dot_general(
+        normed[...],
+        weight[...],
+        (((1,), (1,)), ((), ())),
+        preferred_element_type=jnp.float32,
+    )
+    conditional = (conditional + bias[...]).T
+
+    current = jnp.full((1, 1), step_index[0], jnp.int32)
+    counter = iota(skip_flags.shape, 1)
+    computed = (skip_flags[...] == 0) & (counter <= current)
+    last_full = jnp.max(jnp.where(computed, counter, -1), axis=1, keepdims=True)
+    spacing = (current - last_full).astype(jnp.float32)
+    gap_ratio = spacing / (spacing + 2.0)
+    shape = (layout.rows, layout.channels)
+    own = iota(shape, 0) // 4 == iota(shape, 1)
+    w_low, w_high = (
+        jnp.sum(jnp.where(own, band_gain[n : n + 1, :], 0.0), axis=1, keepdims=True) * factor
+        for n, factor in enumerate((1.0 + gap_ratio, 1.0 - 0.5 * gap_ratio))
+    )
+    base[...] = conditional + GUIDE_EXTRA * w_high * residual[...]
+    row_low[...] = jnp.broadcast_to(GUIDE_EXTRA * (w_low - w_high), row_low.shape)
+    step[...] = jnp.broadcast_to(sigma_at(current + 1) - sigma_at(current), step.shape)
+
+
 def finish_kernel(layout, *refs):
     near, channels, tokens = layout.near, layout.channels, layout.tokens
     parts = refs[:near]
@@ -225,9 +317,9 @@
         for c in range(channels):
             rows = slice(4 * c, 4 * c + 4)
             low_band = total[g, pl.ds(c, 4, stride=channels), :][:, width]
-            value = base[rows, columns] + row_low[rows, columns] * low_band
+            value = base[rows, columns] + row_low[rows, width] * low_band
             velocity[rows, columns] = value
-            latent_next[rows, columns] = latent[rows, columns] + step[rows, columns] * value
+            latent_next[rows, columns] = latent[rows, columns] + step[:4, width] * value
 
 
 VMEM = pl.BlockSpec(memory_space=pltpu.VMEM)
@@ -250,67 +342,75 @@
     )(cut_rows, cut_cols)
 
 
-def mix(layout, filters, sources):
-    wide = layout.far * layout.lines * layout.channels
+def mix_scratch(layout, count):
+    data = pltpu.VMEM((count * layout.lines * layout.channels, 2 * LANES), jnp.bfloat16)
+    return [
+        pltpu.VMEM((layout.rows, pl.cdiv(layout.tokens, LANES) * LANES), jnp.float32),
+        pltpu.VMEM((layout.span, layout.rows, LANES), jnp.float32),
+        data,
+        data,
+    ]
+
+
+def early(layout, filters, slots, sources):
+    tall = layout.near * layout.lines * layout.channels
+    return pl.pallas_call(
+        functools.partial(early_kernel, layout, slots),
+        out_shape=jax.ShapeDtypeStruct((tall, 2 * LANES), jnp.float32),
+        in_specs=[VMEM] * (4 + len(slots)),
+        out_specs=VMEM,
+        scratch_shapes=mix_scratch(layout, len(slots)),
+        compiler_params=pltpu.CompilerParams(vmem_limit_bytes=8 * 2**20),
+        cost_estimate=pl.CostEstimate(flops=10**9, bytes_accessed=10**6, transcendentals=0),
+        name="early",
+    )(*filters, *sources)
+
+
+def mix(layout, filters, carry, slots, sources):
     shape = (layout.rows, layout.tokens)
-    data = pltpu.VMEM((wide, 2 * LANES), jnp.bfloat16)
     return pl.pallas_call(
-        functools.partial(mix_kernel, layout),
+        functools.partial(mix_kernel, layout, slots),
         out_shape=[jax.ShapeDtypeStruct(shape, jnp.float32)] * layout.near,
-        in_specs=[VMEM] * (4 + layout.far),
+        in_specs=[VMEM] * (5 + len(slots)),
         out_specs=[VMEM] * layout.near,
-        scratch_shapes=[
-            pltpu.VMEM((layout.rows, pl.cdiv(layout.tokens, LANES) * LANES), jnp.float32),
-            pltpu.VMEM((layout.span, layout.rows, LANES), jnp.float32),
-            data,
-            data,
-        ],
+        scratch_shapes=mix_scratch(layout, len(slots)),
         compiler_params=pltpu.CompilerParams(vmem_limit_bytes=8 * 2**20),
         cost_estimate=pl.CostEstimate(flops=10**9, bytes_accessed=10**6, transcendentals=0),
         name="mix",
-    )(*filters, *sources)
-
-
-def finish(layout, parts, base, row_low, step, latent):
-    shape = jax.ShapeDtypeStruct((layout.rows, layout.tokens), jnp.float32)
+    )(*filters, carry, *sources)
+
+
+def head(layout, hidden, modulation, head_weight, head_bias, residual, gain, flags, step_index):
     return pl.pallas_call(
-        functools.partial(finish_kernel, layout),
-        out_shape=[shape, shape],
-        in_specs=[VMEM] * (layout.near + 4),
-        out_specs=[VMEM, VMEM],
-        scratch_shapes=[
-            pltpu.VMEM((pl.cdiv(layout.tokens, LANES), layout.rows, LANES), jnp.float32)
+        functools.partial(head_kernel, layout),
+        out_shape=[
+            jax.ShapeDtypeStruct(residual.shape, jnp.float32),
+            jax.ShapeDtypeStruct((layout.rows, LANES), jnp.float32),
+            jax.ShapeDtypeStruct((8, LANES), jnp.float32),
         ],
-        compiler_params=pltpu.CompilerParams(vmem_limit_bytes=8 * 2**20),
-        name="finish",
-    )(*parts, base, row_low, step, latent)
-
-
-def body(
-    hidden,
-    modulation,
-    head_weight,
-    head_bias,
-    residual,
-    latent,
-    band_gain,
-    cut_rows,
-    cut_cols,
-    skip_flags,
-    step_index,
+        in_specs=[VMEM] * 7 + [SMEM],
+        out_specs=[VMEM] * 3,
+        scratch_shapes=[pltpu.VMEM(hidden.shape, jnp.bfloat16)],
+        compiler_params=pltpu.CompilerParams(vmem_limit_bytes=16 * 2**20),
+        cost_estimate=pl.CostEstimate(
+            flops=2 * hidden.size * layout.rows, bytes_accessed=10**7, transcendentals=0
+        ),
+        name="head",
+    )(
+        hidden,
+        modulation,
+        head_weight.T,
+        head_bias.reshape(1, -1),
+        residual,
+        gain,
+        flags.reshape(1, -1),
+        step_index,
+    )
+
+
+def head_in_parts(
+    layout, hidden, modulation, head_weight, head_bias, residual, gain, flags, step_index
 ):
-    layout = Layout(*residual.shape)
-    places = lax.axis_size("seq")
-
-    def exchange(values, unit):
-        swapped = [values[0]] * len(values)
-        for n in [*range(2, len(values)), 1]:
-            pairs = [(s, s ^ (n * unit)) for s in range(places)]
-            swapped[n] = lax.ppermute(values[n], "seq", pairs)
-        return swapped
-
-    sources = exchange([residual] * layout.far, layout.near)
-    filters = bands(layout, cut_rows, cut_cols)
     values = hidden.astype(jnp.float32)
     moments = lax.psum((jnp.sum(values, axis=1), jnp.sum(values * values, axis=1)), "mp")
     average = moments[0] / D
@@ -329,24 +429,75 @@
         )
         + head_bias[:, None]
     )
-    w_low, w_high = band_weights(skip_flags, step_index, band_gain)
+    w_low, w_high = band_weights(flags, step_index, gain)
     row_high = GUIDE_EXTRA * jnp.repeat(w_high, 4)[:, None]
     row_low = GUIDE_EXTRA * jnp.repeat(w_low - w_high, 4)[:, None]
-    base = conditional + row_high * residual
     current = step_index[0]
-    step = sigma_at(current + 1) - sigma_at(current)
-
-    parts = mix(layout, filters, sources)
-    parts = exchange(parts, 1)
-    shape = residual.shape
-    return finish(
+    return (
+        conditional + row_high * residual,
+        jnp.broadcast_to(row_low, (layout.rows, LANES)),
+        jnp.broadcast_to(sigma_at(current + 1) - sigma_at(current), (8, LANES)),
+    )
+
+
+def finish(layout, parts, base, row_low, step, latent):
+    shape = jax.ShapeDtypeStruct((layout.rows, layout.tokens), jnp.float32)
+    return pl.pallas_call(
+        functools.partial(finish_kernel, layout),
+        out_shape=[shape, shape],
+        in_specs=[VMEM] * (layout.near + 4),
+        out_specs=[VMEM, VMEM],
+        scratch_shapes=[
+            pltpu.VMEM((pl.cdiv(layout.tokens, LANES), layout.rows, LANES), jnp.float32)
+        ],
+        compiler_params=pltpu.CompilerParams(vmem_limit_bytes=8 * 2**20),
+        name="finish",
+    )(*parts, base, row_low, step, latent)
+
+
+def body(
+    hidden,
+    modulation,
+    head_weight,
+    head_bias,
+    residual,
+    latent,
+    band_gain,
+    cut_rows,
+    cut_cols,
+    skip_flags,
+    step_index,
+):
+    layout = Layout(*residual.shape)
+    places = lax.axis_size("seq")
+
+    def exchange(values, unit):
+        swapped = [values[0]] * len(values)
+        for n in layout.order(len(values))[1:]:
+            pairs = [(s, s ^ (n * unit)) for s in range(places)]
+            swapped[n] = lax.ppermute(values[n], "seq", pairs)
+        return swapped
+
+    sources = exchange([residual] * layout.far, layout.near)
+    filters = bands(layout, cut_rows, cut_cols)
+    run_head = head if lax.axis_size("mp") == 1 else head_in_parts
+    base, row_low, step = run_head(
         layout,
-        parts,
-        base,
-        jnp.broadcast_to(row_low, shape),
-        jnp.broadcast_to(step, shape),
-        latent,
-    )
+        hidden,
+        modulation,
+        head_weight,
+        head_bias,
+        residual,
+        band_gain,
+        skip_flags,
+        step_index,
+    )
+    sources = [sources[k] for k in layout.order(layout.far)]
+    slots = list(range(layout.far))
+    half = layout.far // 2
+    carry = early(layout, filters, slots[:half], sources[:half])
+    parts = exchange(mix(layout, filters, carry, slots[half:], sources[half:]), 1)
+    return finish(layout, parts, base, row_low, step, latent)
 
 
 def solution(mesh):

time: 23 us -> 19.6 us (0.85)
  other arithmetic: 4 us -> 0 us
  Pallas kernels: 3.37 us -> 7.13 us
  matrix products: 2.88 us -> 0 us
  between operations: 3.57 us -> 2.76 us
  local copies, waits for them, and re-layouts: 0.42 us -> 0.89 us
    pallas_call x1 -> x3, Pallas kernels: 1.72 us -> 5.5 us  [the longest x1 3.39 us: head(): pl.pallas_call(functools.partial(head_kernel, layout), out_shape=[jax.Sha...]
    dot_general x1 -> x0, matrix products: 2.88 us -> none  [body(): lax.dot_general(head_weight, normed, (((0,), (1,)), ((), ())), preferred_...]
    reduce_sum x1 -> x0, other arithmetic: 2.45 us -> none  [body(): jnp.sum(values, axis=1)]
    add x1 -> x0, other arithmetic: 0.9 us -> none  [body(): 1.0 + modulation[1]]
    unnamed x12 -> x18, local copies, waits for them, and re-layouts: 0.03 us -> 0.89 us
    reduce_max x1 -> x0, other arithmetic: 0.63 us -> none  [band_weights(): last_full = jnp.max(jnp.where(computed, counter, -1))]
  transfers between devices with their start and end apart: 6 -> 6, of which waited for: 1 -> 3; matrix products, arithmetic and copies ran while one was open for 32% -> 0% of each run, Pallas kernels for 4% -> 27%
where the time goes in v2:
time: 19.6 us; the launch traced here: 19.5 us
  starting transfers between devices  7.82 us (40%)
  Pallas kernels  7.13 us (36%)
  between operations  2.76 us (14%)
  local copies, waits for them, and re-layouts  0.89 us (5%)
  waiting for transfers between devices  0.85 us (4%)
    ppermute x6, starting transfers between devices, exchange(): swapped[n] = lax.ppermute(values[n], 'seq', pairs)  7.82 us
    pallas_call x1, Pallas kernels, head(): pl.pallas_call(functools.partial(head_kernel, layout), out_shape=[jax.Sha...  3.39 us
    pallas_call x1, Pallas kernels, mix(): pl.pallas_call(functools.partial(mix_kernel, layout, slots), out_shape=[j...  1.14 us
    pallas_call x1, Pallas kernels, early(): pl.pallas_call(functools.partial(early_kernel, layout, slots), out_shape=...  0.97 us
    pallas_call x1, Pallas kernels, bands(): pl.pallas_call(functools.partial(bands_kernel, layout), out_shape=[col, c...  0.91 us
    unnamed x18, local copies, waits for them, and re-layouts  0.89 us
    ppermute x6, waiting for transfers between devices, exchange(): swapped[n] = lax.ppermute(values[n], 'seq', pairs)  0.85 us
    pallas_call x1, Pallas kernels, finish(): pl.pallas_call(functools.partial(finish_kernel, layout), out_shape=[shape...  0.72 us
  transfers between devices with their start and end apart: 6, of which 3 were waited for; matrix products, arithmetic and copies ran while one was open for 0% of the time, Pallas kernels for 27%

profile of v2, /device:TPU:0, one launch (start us, length us, event | category | flops | bytes accessed | tf_op | source)
XLA Modules:
  0.0 19.5 jit_solution(17199843342609568044)
XLA Ops:
  0.6 4.1 %collective-permute-start = (f32[64,225]{1,0:T(8,128)}, f32[64,225]{1,0:T(8,128)S(1)}, u32[]{:S(2)}, u32[]{:S(2)}) collective-permute-start(f32[64,225]{1,0:T(8,128)} %residual.1), channel_id=1, source_target_pairs={{0,8},{1,9},{2,10},{3,11},{4,12},{5,13},{6,14},{7,15},{8,0},{9,1},... | collective-permute-start | bytes 172808 | tf_op jit(solution)/shard_map/ppermute | solution.py:478
  4.8 1.3 %collective-permute-start.1 = (f32[64,225]{1,0:T(8,128)}, f32[64,225]{1,0:T(8,128)S(1)}, u32[]{:S(2)}, u32[]{:S(2)}) collective-permute-start(f32[64,225]{1,0:T(8,128)} %residual.1), channel_id=1, source_target_pairs={{0,12},{1,13},{2,14},{3,15},{4,8},{5,9},{6,10},{7,11},{8,4},{9,5},... | collective-permute-start | bytes 172808 | tf_op jit(solution)/shard_map/ppermute | solution.py:478
  6.1 0.2 %collective-permute-start.2 = (f32[64,225]{1,0:T(8,128)}, f32[64,225]{1,0:T(8,128)S(1)}, u32[]{:S(2)}, u32[]{:S(2)}) collective-permute-start(f32[64,225]{1,0:T(8,128)} %residual.1), channel_id=1, source_target_pairs={{0,4},{1,5},{2,6},{3,7},{4,0},{5,1},{6,2},{7,3},{8,12},{9,13},{10,... | collective-permute-start | bytes 172808 | tf_op jit(solution)/shard_map/ppermute | solution.py:478
  7.6 0.9 %bands.1 = (bf16[256,256]{1,0:T(8,128)(2,1)S(1)}, bf16[256,256]{1,0:T(8,128)(2,1)S(1)}, bf16[512,512]{1,0:T(8,128)(2,1)S(1)}, bf16[512,512]{1,0:T(8,128)(2,1)S(1)}) custom-call(s32[1]{0:T(128)S(6)} %copy.13.cut_rows, s32[1]{0:T(128)S(6)} %copy.14.cut_cols), custom_call_target="tpu_custom_call" | custom-call | flops 100000000 | bytes 1000000 | tf_op jit(solution)/shard_map/bands/pallas_call | solution.py:334
  8.6 0.1 collective-permute-done.refs_5_
  8.7 0.0 copy-start.2
  8.7 0.8 %copy-done.2 = f32[64,225]{1,0:T(8,128)S(1)} copy-done((f32[64,225]{1,0:T(8,128)S(1)}, f32[64,225]{1,0:T(8,128)}, u32[]{:S(2)}) %copy-start.2) | copy-done | bytes 57624
  9.5 1.0 %early.1.refs_4_ = f32[512,256]{1,0:T(8,128)S(1)} custom-call(bf16[256,256]{1,0:T(8,128)(2,1)S(1)} %get-tuple-element.13.refs_0_, bf16[256,256]{1,0:T(8,128)(2,1)S(1)} %get-tuple-element.14.refs_1_, bf16[512,512]{1,0:T(8,128)(2,1)S(1)} %get-tuple-element.15.refs_2_, bf16[512,512]{1,0:T(8,128)(2,1)S(1)} %get-tuple-element.16.refs_3_, ...), custom_call_target="tpu_custom_call" | custom-call | flops 1000000000 | bytes 1000000 | tf_op jit(solution)/shard_map/early/pallas_call | solution.py:357
  10.5 0.0 copy-start
  10.5 0.0 copy-start.1
  10.5 0.0 copy-start.3
  10.5 0.0 copy-start.5
  10.5 0.0 copy-start.6
  10.6 0.0 copy-start.7
  10.6 0.0 copy-start.8
  10.6 0.6 %collective-permute-done.1.refs_5_ = f32[64,225]{1,0:T(8,128)S(1)} collective-permute-done((f32[64,225]{1,0:T(8,128)}, f32[64,225]{1,0:T(8,128)S(1)}, u32[]{:S(2)}, u32[]{:S(2)}) %collective-permute-start.1) | collective-permute-done | bytes 57632 | tf_op jit(solution)/shard_map/ppermute | solution.py:478
  11.1 0.1 collective-permute-done.2.refs_6_
  11.3 1.1 %mix.1 = (f32[64,225]{1,0:T(8,128)S(1)}, f32[64,225]{1,0:T(8,128)S(1)}, f32[64,225]{1,0:T(8,128)S(1)}, f32[64,225]{1,0:T(8,128)S(1)}) custom-call(bf16[256,256]{1,0:T(8,128)(2,1)S(1)} %get-tuple-element.13.refs_0_, bf16[256,256]{1,0:T(8,128)(2,1)S(1)} %get-tuple-element.14.refs_1_, bf16[512,512]{1,0:T(8,128)(2,1)S(1)} %get-tuple-element.15.refs_2_, ...), custom_call_target="tpu_custom_call" | custom-call | flops 1000000000 | bytes 1000000 | tf_op jit(solution)/shard_map/mix/pallas_call | solution.py:371
  12.4 0.0 copy-start.4
  12.4 0.1 collective-permute-start.3
  12.5 2.0 %collective-permute-start.4 = (f32[64,225]{1,0:T(8,128)S(1)}, f32[64,225]{1,0:T(8,128)S(1)}, u32[]{:S(2)}, u32[]{:S(2)}) collective-permute-start(f32[64,225]{1,0:T(8,128)S(1)} %get-tuple-element.19), channel_id=1, source_target_pairs={{0,2},{1,3},{2,0},{3,1},{4,6},{5,7},{6,4},{7,5},{8,10},{9,11},{10,... | collective-permute-start | bytes 172808 | tf_op jit(solution)/shard_map/ppermute | solution.py:478
  14.5 0.0 collective-permute-start.5
  15.2 0.0 copy-done
  15.2 0.0 copy-done.1
  15.2 0.0 copy-done.3
  15.3 0.0 copy-done.5
  15.3 0.0 copy-done.6
  15.3 0.0 copy-done.7
  15.3 0.0 copy-done.8
  15.3 3.4 %head.1 = (f32[64,225]{1,0:T(8,128)S(1)}, f32[64,128]{1,0:T(8,128)S(1)}, f32[8,128]{1,0:T(8,128)S(1)}) custom-call(bf16[225,5120]{1,0:T(8,128)(2,1)S(1)} %copy-done, f32[2,5120]{1,0:T(2,128)S(1)} %copy-done.5, bf16[64,5120]{1,0:T(8,128)(2,1)S(1)} %bitcast.3, f32[1,64]{1,0:T(1,128)S(1)} %bitcast.4, f32[64,225]{1,0:T(8,128)S(1)} %copy-done.3, ...), custom_call_target="tpu_custom_call" | custom-call | flops 147456000 | bytes 10000000 | tf_op jit(solution)/shard_map/head/pallas_call | solution.py:384
  18.7 0.0 collective-permute-done.3.refs_1_
  18.7 0.0 collective-permute-done.4.refs_2_
  18.7 0.0 collective-permute-done.5.refs_3_
  18.7 0.0 copy-done.4
  18.7 0.7 %finish.1 = (f32[64,225]{1,0:T(8,128)}, f32[64,225]{1,0:T(8,128)}) custom-call(f32[64,225]{1,0:T(8,128)S(1)} %get-tuple-element.17.refs_0_, f32[64,225]{1,0:T(8,128)S(1)} %collective-permute-done.3.refs_1_, f32[64,225]{1,0:T(8,128)S(1)} %collective-permute-done.4.refs_2_, f32[64,225]{1,0:T(8,128)S(1)} %collective-permute-done.5.refs_3_, ...), custom_call_target="tpu_custom_call" | custom-call | tf_op jit(solution)/shard_map/finish/pallas_call | solution.py:445
Async XLA Ops:
  0.6 8.1 %collective-permute-start = (f32[64,225]{1,0:T(8,128)}, f32[64,225]{1,0:T(8,128)S(1)}, u32[]{:S(2)}, u32[]{:S(2)}) collective-permute-start(f32[64,225]{1,0:T(8,128)} %residual.1), channel_id=1, source_target_pairs={{0,8},{1,9},{2,10},{3,11},{4,12},{5,13},{6,14},{7,15},{8,0},{9,1},... | collective-permute-start | bytes 172808 | tf_op jit(solution)/shard_map/ppermute | solution.py:478
  4.8 6.4 %collective-permute-start.1 = (f32[64,225]{1,0:T(8,128)}, f32[64,225]{1,0:T(8,128)S(1)}, u32[]{:S(2)}, u32[]{:S(2)}) collective-permute-start(f32[64,225]{1,0:T(8,128)} %residual.1), channel_id=1, source_target_pairs={{0,12},{1,13},{2,14},{3,15},{4,8},{5,9},{6,10},{7,11},{8,4},{9,5},... | collective-permute-start | bytes 172808 | tf_op jit(solution)/shard_map/ppermute | solution.py:478
  6.1 5.2 %collective-permute-start.2 = (f32[64,225]{1,0:T(8,128)}, f32[64,225]{1,0:T(8,128)S(1)}, u32[]{:S(2)}, u32[]{:S(2)}) collective-permute-start(f32[64,225]{1,0:T(8,128)} %residual.1), channel_id=1, source_target_pairs={{0,4},{1,5},{2,6},{3,7},{4,0},{5,1},{6,2},{7,3},{8,12},{9,13},{10,... | collective-permute-start | bytes 172808 | tf_op jit(solution)/shard_map/ppermute | solution.py:478
  8.7 0.8 %copy-start.2 = (f32[64,225]{1,0:T(8,128)S(1)}, f32[64,225]{1,0:T(8,128)}, u32[]{:S(2)}) copy-start(f32[64,225]{1,0:T(8,128)} %residual.1) | copy-start | bytes 172804
  10.5 4.7 %copy-start = (bf16[225,5120]{1,0:T(8,128)(2,1)S(1)}, bf16[225,5120]{1,0:T(8,128)(2,1)}, u32[]{:S(2)}) copy-start(bf16[225,5120]{1,0:T(8,128)(2,1)} %hidden.1) | copy-start | bytes 6912004
  10.5 4.7 %copy-start.1 = (bf16[5120,64]{0,1:T(8,128)(2,1)S(1)}, bf16[5120,64]{0,1:T(8,128)(2,1)}, u32[]{:S(2)}) copy-start(bf16[5120,64]{0,1:T(8,128)(2,1)} %param.13) | copy-start | bytes 1966084
  10.5 4.7 %copy-start.3 = (f32[64,225]{1,0:T(8,128)S(1)}, f32[64,225]{1,0:T(8,128)}, u32[]{:S(2)}) copy-start(f32[64,225]{1,0:T(8,128)} %residual.1) | copy-start | bytes 172804
  10.5 4.7 %copy-start.5 = (f32[2,5120]{1,0:T(2,128)S(1)}, f32[2,5120]{1,0:T(2,128)}, u32[]{:S(2)}) copy-start(f32[2,5120]{1,0:T(2,128)} %modulation.1) | copy-start | bytes 122884
  10.5 4.7 %copy-start.6 = (f32[2,16]{1,0:T(2,128)S(1)}, f32[2,16]{1,0:T(2,128)}, u32[]{:S(2)}) copy-start(f32[2,16]{1,0:T(2,128)} %band_gain.1) | copy-start | bytes 388
  10.6 4.7 %copy-start.7 = (f32[64]{0:T(128)S(1)}, f32[64]{0:T(128)}, u32[]{:S(2)}) copy-start(f32[64]{0:T(128)} %param.14) | copy-start | bytes 772
  10.6 4.7 %copy-start.8 = (s32[50]{0:T(128)S(1)}, s32[50]{0:T(128)}, u32[]{:S(2)}) copy-start(s32[50]{0:T(128)} %param.20) | copy-start | bytes 604
  12.4 6.3 %copy-start.4 = (f32[64,225]{1,0:T(8,128)S(1)}, f32[64,225]{1,0:T(8,128)}, u32[]{:S(2)}) copy-start(f32[64,225]{1,0:T(8,128)} %refs_7_.1) | copy-start | bytes 172804
  12.4 6.2 %collective-permute-start.3 = (f32[64,225]{1,0:T(8,128)S(1)}, f32[64,225]{1,0:T(8,128)S(1)}, u32[]{:S(2)}, u32[]{:S(2)}) collective-permute-start(f32[64,225]{1,0:T(8,128)S(1)} %get-tuple-element.18), channel_id=1, source_target_pairs={{0,1},{1,0},{2,3},{3,2},{4,5},{5,4},{6,7},{7,6},{8,9},{9,8},{10,11... | collective-permute-start | bytes 172808 | tf_op jit(solution)/shard_map/ppermute | solution.py:478
  12.5 6.2 %collective-permute-start.4 = (f32[64,225]{1,0:T(8,128)S(1)}, f32[64,225]{1,0:T(8,128)S(1)}, u32[]{:S(2)}, u32[]{:S(2)}) collective-permute-start(f32[64,225]{1,0:T(8,128)S(1)} %get-tuple-element.19), channel_id=1, source_target_pairs={{0,2},{1,3},{2,0},{3,1},{4,6},{5,7},{6,4},{7,5},{8,10},{9,11},{10,... | collective-permute-start | bytes 172808 | tf_op jit(solution)/shard_map/ppermute | solution.py:478
  14.5 4.2 %collective-permute-start.5 = (f32[64,225]{1,0:T(8,128)S(1)}, f32[64,225]{1,0:T(8,128)S(1)}, u32[]{:S(2)}, u32[]{:S(2)}) collective-permute-start(f32[64,225]{1,0:T(8,128)S(1)} %get-tuple-element.20), channel_id=1, source_target_pairs={{0,3},{1,2},{2,1},{3,0},{4,7},{5,6},{6,5},{7,4},{8,11},{9,10},{10,... | collective-permute-start | bytes 172808 | tf_op jit(solution)/shard_map/ppermute | solution.py:478

commit v3 on v2

--- a/solution.py
+++ b/solution.py
@@ -75,7 +75,7 @@
 
     def owners(self, position):
         givers = [position ^ (k * self.near) for k in self.order(self.far)]
-        takers = [position ^ m for m in range(self.near)]
+        takers = [position ^ m for m in self.order(self.near)]
         return givers, takers
 
     def order(self, count):
@@ -88,42 +88,55 @@
         return 2 * (owner * self.tokens // PW)
 
 
-def wave_tables(places, length, cutoff):
-    modes = iota(places.shape, 1)
-    turns = lax.rem(places * modes, length).astype(jnp.float32)
+def waves(places, length):
+    turns = lax.rem(places * iota(places.shape, 1), length).astype(jnp.float32)
     angles = turns * (2.0 * math.pi / length)
-    table = jnp.concatenate([jnp.cos(angles), jnp.sin(angles)], axis=1)
+    return jnp.concatenate([jnp.cos(angles), jnp.sin(angles)], axis=1)
+
+
+def kept_modes(shape, length, cutoff):
+    modes = iota(shape, 1)
     weight = jnp.where((modes == 0) | (2 * modes == length), 1.0, 2.0) / length
     kept = jnp.where((modes <= cutoff) & (2 * modes <= length), weight, 0.0)
-    return table, jnp.concatenate([kept, kept], axis=1)
-
-
-def bands_kernel(layout, cut_rows, cut_cols, col_high, col_low, row_high, row_low):
+    return jnp.concatenate([kept, kept], axis=1)
+
+
+def bands_kernel(
+    layout,
+    cut_rows,
+    cut_cols,
+    col_high,
+    col_low,
+    row_high,
+    row_low,
+):
     seq_index = lax.axis_index("seq")
     position = lax.rem(seq_index, layout.members)
     frame = seq_index // layout.members
+
     shape = (2 * LANES, LANES)
     line = iota(shape, 0)
     odd = line >= LANES
     column = jnp.where(odd, line - LANES, line)
-    table, kept = wave_tables(2 * column + odd.astype(jnp.int32), W, cut_cols[frame])
+    table = waves(2 * column + odd.astype(jnp.int32), W)
     table = jnp.where(jnp.concatenate([column, column], axis=1) < PW, table, 0.0)
-    high, low = split(dot3(split(table * kept), split(table), ((1,), (1,))))
-    col_high[...] = high
-    col_low[...] = low
 
     def tables(owners):
-        shape = (len(owners) * layout.lines, LANES)
-        line = iota(shape, 0)
+        line = iota((len(owners) * layout.lines, LANES), 0)
         places = line
         for n, owner in enumerate(owners):
             start = layout.first_line(owner) - n * layout.lines
             places = jnp.where(line >= n * layout.lines, line + start, places)
-        return wave_tables(places, H, cut_rows[frame])
+        return waves(places, H)
 
     givers, takers = layout.owners(position)
-    given, kept = tables(givers)
-    taken, _ = tables(takers)
+    given = tables(givers)
+    taken = tables(takers)
+    kept = kept_modes(shape, W, cut_cols[frame])
+    high, low = split(dot3(split(table * kept), split(table), ((1,), (1,))))
+    col_high[...] = high
+    col_low[...] = low
+    kept = kept_modes((given.shape[0], LANES), H, cut_rows[frame])
     small = dot3(split(taken), split(given * kept), ((1,), (1,)))
     wide = given.shape[0]
     size = wide * layout.channels
@@ -142,7 +155,7 @@
 
 def filtered(layout, slots, sources, filters, scratch):
     span, groups, channels, tokens = layout.span, layout.groups, layout.channels, layout.tokens
-    col_high, col_low, row_high, row_low = filters
+    col_high, col_low = filters[:2]
     window, lines, data_high, data_low = scratch
     givers, _ = layout.owners(lax.rem(lax.axis_index("seq"), layout.members))
     lane = iota((layout.rows, LANES), 1)
@@ -175,64 +188,125 @@
                     place = (slice(first, first + channels), slice(dx * LANES, (dx + 1) * LANES))
                     data_high[place] = high
                     data_low[place] = low
-    mixed = dot3((data_high[...], data_low[...]), (col_high[...], col_low[...]))
-    each = layout.lines * channels
-    columns = slice(slots[0] * each, (slots[-1] + 1) * each)
-    return dot3((row_high[:, columns], row_low[:, columns]), split(mixed))
+    return dot3((data_high[...], data_low[...]), (col_high[...], col_low[...]))
+
+
+def slots_columns(layout, slots):
+    each = layout.lines * layout.channels
+    return slice(slots[0] * each, (slots[-1] + 1) * each)
 
 
 def early_kernel(layout, slots, *refs):
     sources = refs[4 : 4 + len(slots)]
     carry = refs[4 + len(slots)]
-    carry[...] = filtered(layout, slots, sources, refs[:4], refs[5 + len(slots) :])
-
-
-def mix_kernel(layout, slots, *refs):
-    near, span, groups = layout.near, layout.span, layout.groups
+    data = filtered(layout, slots, sources, refs[:4], refs[5 + len(slots) :])
+    columns = slots_columns(layout, slots)
+    carry[...] = dot3([f[:, columns] for f in refs[2:4]], split(data))
+
+
+def place_part(layout, mixed, taker, out):
+    span, groups = layout.span, layout.groups
     channels, tokens = layout.channels, layout.tokens
-    carry = refs[4]
+    lane = iota((channels, LANES), 1)
+    offset = layout.offset(taker)
+    back = lax.rem(LANES - offset, LANES)
+    for dy in range(2):
+        for dx in range(2):
+            placed = [None] * (groups + 1)
+
+            def put(group, value):
+                old = placed[group]
+                placed[group] = value if old is None else old + value
+
+            for r in range(span):
+                first = (r * 2 + dy) * channels
+                line = mixed[first : first + channels, dx * LANES : (dx + 1) * LANES]
+                group, start = divmod(r * PW, LANES)
+                if start:
+                    line = pltpu.roll(line, start, 1)
+                if start + PW <= LANES:
+                    put(group, line)
+                else:
+                    put(group, jnp.where(lane >= start, line, 0.0))
+                    put(group + 1, jnp.where(lane < start, line, 0.0))
+            turned = [pltpu.roll(p, back, 1) for p in placed[:groups]]
+            first = (dy * 2 + dx) * channels
+            for g in range(pl.cdiv(tokens, LANES)):
+                value = jnp.where(lane < LANES - offset, turned[g], turned[g + 1])
+                last = min(tokens, (g + 1) * LANES)
+                out[first : first + channels, g * LANES : last] = value[:, : last - g * LANES]
+
+
+def first_kernel(layout, slots, m, *refs):
+    filters, carry = refs[:4], refs[4]
     sources = refs[5 : 5 + len(slots)]
-    outs = refs[5 + len(slots) : 5 + len(slots) + near]
-    scratch = refs[5 + len(slots) + near :]
-    mixed = carry[...] + filtered(layout, slots, sources, refs[:4], scratch)
+    out, data_high, data_low = refs[5 + len(slots) : 8 + len(slots)]
+    high, low = split(filtered(layout, slots, sources, filters, refs[8 + len(slots) :]))
+    data_high[...] = high
+    data_low[...] = low
+    each = layout.lines * layout.channels
     _, takers = layout.owners(lax.rem(lax.axis_index("seq"), layout.members))
-    lane = iota((channels, LANES), 1)
-    for m in range(near):
-        offset = layout.offset(takers[m])
-        back = lax.rem(LANES - offset, LANES)
-        for dy in range(2):
-            for dx in range(2):
-                placed = [None] * (groups + 1)
-
-                def put(group, value):
-                    old = placed[group]
-                    placed[group] = value if old is None else old + value
-
-                for r in range(span):
-                    first = ((m * span + r) * 2 + dy) * channels
-                    line = mixed[first : first + channels, dx * LANES : (dx + 1) * LANES]
-                    group, start = divmod(r * PW, LANES)
-                    if start:
-                        line = pltpu.roll(line, start, 1)
-                    if start + PW <= LANES:
-                        put(group, line)
-                    else:
-                        put(group, jnp.where(lane >= start, line, 0.0))
-                        put(group + 1, jnp.where(lane < start, line, 0.0))
-                turned = [pltpu.roll(p, back, 1) for p in placed[:groups]]
-                first = (dy * 2 + dx) * channels
-                for g in range(pl.cdiv(tokens, LANES)):
-                    value = jnp.where(lane < LANES - offset, turned[g], turned[g + 1])
-                    last = min(tokens, (g + 1) * LANES)
-                    outs[m][first : first + channels, g * LANES : last] = value[
-                        :, : last - g * LANES
-                    ]
-
-
-def head_kernel(
+    rows = slice(m * each, (m + 1) * each)
+    columns = slots_columns(layout, slots)
+    mixed = carry[rows, :] + dot3([f[rows, columns] for f in filters[2:]], (high, low))
+    place_part(layout, mixed, takers[m], out)
+
+
+def rest_kernel(layout, slots, others, *refs):
+    row_high, row_low, carry, data_high, data_low = refs[:5]
+    _, takers = layout.owners(lax.rem(lax.axis_index("seq"), layout.members))
+    each = layout.lines * layout.channels
+    columns = slots_columns(layout, slots)
+    for m, out in zip(others, refs[5:]):
+        rows = slice(m * each, (m + 1) * each)
+        filters = [f[rows, columns] for f in (row_high, row_low)]
+        mixed = carry[rows, :] + dot3(filters, (data_high[...], data_low[...]))
+        place_part(layout, mixed, takers[m], out)
+
+
+def norm_kernel(hidden, modulation, normed, scale):
+    tokens, width = hidden.shape
+    tiles = [slice(t, t + LANES) for t in range(0, width, LANES)]
+    block, pair = 16, 2
+    scale[...] = 1.0 + modulation[1:2, :]
+
+    def moments(rows, count):
+        sums = [jnp.zeros((count, LANES), jnp.float32) for _ in range(2)]
+        squares = list(sums)
+        for t, columns in enumerate(tiles):
+            value = hidden[rows, columns].astype(jnp.float32)
+            sums[t % 2] += value
+            squares[t % 2] += value * value
+        average = jnp.sum(sums[0] + sums[1], axis=1, keepdims=True) / D
+        square = jnp.sum(squares[0] + squares[1], axis=1, keepdims=True) / D
+        scale_inv = lax.rsqrt(square - average * average + EPSILON)
+        return [jnp.broadcast_to(v, (count, LANES)) for v in (average, scale_inv)]
+
+    def norm(rows, average, scale_inv):
+        for columns in tiles:
+            value = hidden[rows, columns].astype(jnp.float32)
+            value = (value - average) * scale_inv
+            value = value * scale[:, columns] + modulation[0:1, columns]
+            normed[rows, columns] = value.astype(jnp.bfloat16)
+
+    whole = tokens // (block * pair)
+
+    @pl.loop(0, whole)
+    def _(n):
+        first = pl.multiple_of(n * (block * pair), block)
+        rows = [pl.ds(first + p * block, block) for p in range(pair)]
+        found = [moments(r, block) for r in rows]
+        for r, f in zip(rows, found):
+            norm(r, *f)
+
+    for first in range(whole * block * pair, tokens, block):
+        last = min(tokens, first + block)
+        norm(slice(first, last), *moments(slice(first, last), last - first))
+
+
+def project_kernel(
     layout,
-    hidden,
-    modulation,
+    normed,
     weight,
     bias,
     residual,
@@ -242,41 +316,7 @@
     base,
     row_low,
     step,
-    normed,
 ):
-    tokens, width = hidden.shape
-    tiles = width // LANES
-    block = 16
-
-    def norm(rows):
-        count = rows.size if isinstance(rows, pl.Slice) else rows.stop - rows.start
-        sums = [jnp.zeros((count, LANES), jnp.float32) for _ in range(4)]
-        squares = list(sums)
-        for t in range(tiles):
-            value = hidden[rows, t * LANES : (t + 1) * LANES].astype(jnp.float32)
-            sums[t % 4] += value
-            squares[t % 4] += value * value
-        total = jnp.sum((sums[0] + sums[1]) + (sums[2] + sums[3]), axis=1, keepdims=True)
-        square = jnp.sum(
-            (squares[0] + squares[1]) + (squares[2] + squares[3]), axis=1, keepdims=True
-        )
-        average = total / D
-        scale_inv = lax.rsqrt(square / D - average * average + EPSILON)
-        average = jnp.broadcast_to(average, (count, LANES))
-        scale_inv = jnp.broadcast_to(scale_inv, (count, LANES))
-        for t in range(tiles):
-            columns = slice(t * LANES, (t + 1) * LANES)
-            value = hidden[rows, columns].astype(jnp.float32)
-            value = (value - average) * scale_inv
-            value = value * (1.0 + modulation[1:2, columns]) + modulation[0:1, columns]
-            normed[rows, columns] = value.astype(jnp.bfloat16)
-
-    @pl.loop(0, tokens // block)
-    def _(n):
-        norm(pl.ds(pl.multiple_of(n * block, block), block))
-
-    if tokens % block:
-        norm(slice(tokens // block * block, tokens))
     conditional = lax.dot_general(
         normed[...],
         weight[...],
@@ -337,7 +377,7 @@
         in_specs=[SMEM, SMEM],
         out_specs=[VMEM] * 4,
         compiler_params=pltpu.CompilerParams(vmem_limit_bytes=8 * 2**20),
-        cost_estimate=pl.CostEstimate(flops=10**8, bytes_accessed=10**6, transcendentals=0),
+        cost_estimate=pl.CostEstimate(flops=10**9, bytes_accessed=2 * 10**7, transcendentals=0),
         name="bands",
     )(cut_rows, cut_cols)
 
@@ -366,39 +406,63 @@
     )(*filters, *sources)
 
 
-def mix(layout, filters, carry, slots, sources):
-    shape = (layout.rows, layout.tokens)
+def mix_first(layout, filters, carry, slots, sources, m):
+    wide = len(slots) * layout.lines * layout.channels
+    data = jax.ShapeDtypeStruct((wide, 2 * LANES), jnp.bfloat16)
     return pl.pallas_call(
-        functools.partial(mix_kernel, layout, slots),
-        out_shape=[jax.ShapeDtypeStruct(shape, jnp.float32)] * layout.near,
+        functools.partial(first_kernel, layout, slots, m),
+        out_shape=[jax.ShapeDtypeStruct((layout.rows, layout.tokens), jnp.float32), data, data],
         in_specs=[VMEM] * (5 + len(slots)),
-        out_specs=[VMEM] * layout.near,
+        out_specs=[VMEM] * 3,
         scratch_shapes=mix_scratch(layout, len(slots)),
         compiler_params=pltpu.CompilerParams(vmem_limit_bytes=8 * 2**20),
         cost_estimate=pl.CostEstimate(flops=10**9, bytes_accessed=10**6, transcendentals=0),
-        name="mix",
+        name="mix_first",
     )(*filters, carry, *sources)
 
 
+def mix_rest(layout, filters, carry, slots, data, others):
+    shape = jax.ShapeDtypeStruct((layout.rows, layout.tokens), jnp.float32)
+    return pl.pallas_call(
+        functools.partial(rest_kernel, layout, slots, others),
+        out_shape=[shape] * len(others),
+        in_specs=[VMEM] * 5,
+        out_specs=[VMEM] * len(others),
+        compiler_params=pltpu.CompilerParams(vmem_limit_bytes=8 * 2**20),
+        cost_estimate=pl.CostEstimate(flops=10**9, bytes_accessed=10**6, transcendentals=0),
+        name="mix_rest",
+    )(*filters[2:], carry, *data)
+
+
 def head(layout, hidden, modulation, head_weight, head_bias, residual, gain, flags, step_index):
+    normed = pl.pallas_call(
+        norm_kernel,
+        out_shape=jax.ShapeDtypeStruct(hidden.shape, jnp.bfloat16),
+        in_specs=[VMEM] * 2,
+        out_specs=VMEM,
+        scratch_shapes=[pltpu.VMEM((1, hidden.shape[1]), jnp.float32)],
+        compiler_params=pltpu.CompilerParams(vmem_limit_bytes=8 * 2**20),
+        cost_estimate=pl.CostEstimate(
+            flops=10 * hidden.size, bytes_accessed=10**7, transcendentals=0
+        ),
+        name="norm",
+    )(hidden, modulation)
     return pl.pallas_call(
-        functools.partial(head_kernel, layout),
+        functools.partial(project_kernel, layout),
         out_shape=[
             jax.ShapeDtypeStruct(residual.shape, jnp.float32),
             jax.ShapeDtypeStruct((layout.rows, LANES), jnp.float32),
             jax.ShapeDtypeStruct((8, LANES), jnp.float32),
         ],
-        in_specs=[VMEM] * 7 + [SMEM],
+        in_specs=[VMEM] * 6 + [SMEM],
         out_specs=[VMEM] * 3,
-        scratch_shapes=[pltpu.VMEM(hidden.shape, jnp.bfloat16)],
-        compiler_params=pltpu.CompilerParams(vmem_limit_bytes=16 * 2**20),
+        compiler_params=pltpu.CompilerParams(vmem_limit_bytes=8 * 2**20),
         cost_estimate=pl.CostEstimate(
-            flops=2 * hidden.size * layout.rows, bytes_accessed=10**7, transcendentals=0
+            flops=2 * hidden.size * layout.rows, bytes_accessed=3 * 10**6, transcendentals=0
         ),
-        name="head",
+        name="project",
     )(
-        hidden,
-        modulation,
+        normed,
         head_weight.T,
         head_bias.reshape(1, -1),
         residual,
@@ -472,10 +536,10 @@
     places = lax.axis_size("seq")
 
     def exchange(values, unit):
-        swapped = [values[0]] * len(values)
-        for n in layout.order(len(values))[1:]:
+        swapped = [values[0]]
+        for turn, n in enumerate(layout.order(len(values))[1:]):
             pairs = [(s, s ^ (n * unit)) for s in range(places)]
-            swapped[n] = lax.ppermute(values[n], "seq", pairs)
+            swapped.append(lax.ppermute(values[turn + 1], "seq", pairs))
         return swapped
 
     sources = exchange([residual] * layout.far, layout.near)
@@ -492,11 +556,13 @@
         skip_flags,
         step_index,
     )
-    sources = [sources[k] for k in layout.order(layout.far)]
     slots = list(range(layout.far))
     half = layout.far // 2
     carry = early(layout, filters, slots[:half], sources[:half])
-    parts = exchange(mix(layout, filters, carry, slots[half:], sources[half:]), 1)
+    late, others = slots[half:], [0, *range(2, layout.near)]
+    part, *data = mix_first(layout, filters, carry, late, sources[half:], 1)
+    own, *rest = mix_rest(layout, filters, carry, late, data, others)
+    parts = exchange([own, part, *rest], 1)
     return finish(layout, parts, base, row_low, step, latent)
 
 

time: 19.6 us -> 20.9 us (1.066)
  waiting for transfers between devices: 0.85 us -> 3.09 us
  local copies, waits for them, and re-layouts: 0.89 us -> 0.05 us
  Pallas kernels: 7.13 us -> 6.82 us
    ppermute x6, waiting for transfers between devices: 0.85 us -> 3.09 us  [exchange(): swapped.append(lax.ppermute(values[turn + 1], 'seq', pairs))]
    unnamed x18 -> x16, local copies, waits for them, and re-layouts: 0.89 us -> 0.05 us
    pallas_call x2 -> x4, Pallas kernels: 4.53 us -> 4.22 us  [the longest x1 1.97 us: head(): pl.pallas_call(norm_kernel, out_shape=jax.ShapeDtypeStruct(hidden.shape,...]
  transfers between devices with their start and end apart: 6 -> 6, of which waited for: 3 -> 2; matrix products, arithmetic and copies ran while one was open for 0% -> 0% of each run, Pallas kernels for 27% -> 23%
where the time goes in v3:
time: 20.9 us; the launch traced here: 20.7 us
  starting transfers between devices  7.99 us (38%)
  Pallas kernels  6.82 us (33%)
  waiting for transfers between devices  3.09 us (15%)
  between operations  2.77 us (13%)
    ppermute x6, starting transfers between devices, exchange(): swapped.append(lax.ppermute(values[turn + 1], 'seq', pairs))  7.99 us
    ppermute x6, waiting for transfers between devices, exchange(): swapped.append(lax.ppermute(values[turn + 1], 'seq', pairs))  3.09 us
    pallas_call x1, Pallas kernels, head(): pl.pallas_call(norm_kernel, out_shape=jax.ShapeDtypeStruct(hidden.shape,...  1.97 us
    pallas_call x1, Pallas kernels, early(): pl.pallas_call(functools.partial(early_kernel, layout, slots), out_shape=...  0.96 us
    pallas_call x1, Pallas kernels, bands(): pl.pallas_call(functools.partial(bands_kernel, layout), out_shape=[col, c...  0.91 us
    pallas_call x1, Pallas kernels, mix_first(): pl.pallas_call(functools.partial(first_kernel, layout, slots, m), out_sha...  0.91 us
    pallas_call x1, Pallas kernels, head(): pl.pallas_call(functools.partial(project_kernel, layout), out_shape=[jax....  0.83 us
    pallas_call x1, Pallas kernels, finish(): pl.pallas_call(functools.partial(finish_kernel, layout), out_shape=[shape...  0.72 us
  transfers between devices with their start and end apart: 6, of which 2 were waited for; matrix products, arithmetic and copies ran while one was open for 0% of the time, Pallas kernels for 23%

profile of v3, /device:TPU:0, one launch (start us, length us, event | category | flops | bytes accessed | tf_op | source)
XLA Modules:
  0.0 20.7 jit_solution(6796343509194912700)
XLA Ops:
  0.6 0.0 copy-start.2
  0.6 5.1 %collective-permute-start.1 = (f32[64,225]{1,0:T(8,128)}, f32[64,225]{1,0:T(8,128)S(1)}, u32[]{:S(2)}, u32[]{:S(2)}) collective-permute-start(f32[64,225]{1,0:T(8,128)} %residual.1), channel_id=1, source_target_pairs={{0,12},{1,13},{2,14},{3,15},{4,8},{5,9},{6,10},{7,11},{8,4},{9,5},... | collective-permute-start | bytes 172808 | tf_op jit(solution)/shard_map/ppermute | solution.py:542
  5.8 0.0 collective-permute-start
  5.8 0.6 %collective-permute-start.2 = (f32[64,225]{1,0:T(8,128)}, f32[64,225]{1,0:T(8,128)S(1)}, u32[]{:S(2)}, u32[]{:S(2)}) collective-permute-start(f32[64,225]{1,0:T(8,128)} %residual.1), channel_id=1, source_target_pairs={{0,4},{1,5},{2,6},{3,7},{4,0},{5,1},{6,2},{7,3},{8,12},{9,13},{10,... | collective-permute-start | bytes 172808 | tf_op jit(solution)/shard_map/ppermute | solution.py:542
  7.7 0.9 %bands.1 = (bf16[256,256]{1,0:T(8,128)(2,1)S(1)}, bf16[256,256]{1,0:T(8,128)(2,1)S(1)}, bf16[512,512]{1,0:T(8,128)(2,1)S(1)}, bf16[512,512]{1,0:T(8,128)(2,1)S(1)}) custom-call(s32[1]{0:T(128)S(6)} %copy.13.cut_rows, s32[1]{0:T(128)S(6)} %copy.14.cut_cols), custom_call_target="tpu_custom_call" | custom-call | flops 1000000000 | bytes 20000000 | tf_op jit(solution)/shard_map/bands/pallas_call | solution.py:374
  8.6 3.0 %collective-permute-done.refs_5_ = f32[64,225]{1,0:T(8,128)S(1)} collective-permute-done((f32[64,225]{1,0:T(8,128)}, f32[64,225]{1,0:T(8,128)S(1)}, u32[]{:S(2)}, u32[]{:S(2)}) %collective-permute-start) | collective-permute-done | bytes 57632 | tf_op jit(solution)/shard_map/ppermute | solution.py:542
  11.6 0.0 copy-done.2
  11.6 1.0 %early.1.refs_4_.refs_2_ = f32[512,256]{1,0:T(8,128)S(1)} custom-call(bf16[256,256]{1,0:T(8,128)(2,1)S(1)} %get-tuple-element.17.refs_0_, bf16[256,256]{1,0:T(8,128)(2,1)S(1)} %get-tuple-element.18.refs_1_, bf16[512,512]{1,0:T(8,128)(2,1)S(1)} %get-tuple-element.15.refs_2_.refs_0_, bf16[512,512]{1,0:T(8,128)(2,1)S(1)} %get-tuple-element.16.refs_3_.refs_1_, ...), custom_call_target="tpu_custom_call" | custom-call | flops 1000000000 | bytes 1000000 | tf_op jit(solution)/shard_map/early/pallas_call | solution.py:397
  12.6 0.0 collective-permute-done.1.refs_5_
  12.6 0.0 collective-permute-done.2.refs_6_
  12.6 0.9 %mix_first.1 = (f32[64,225]{1,0:T(8,128)S(1)}, bf16[256,256]{1,0:T(8,128)(2,1)S(1)}, bf16[256,256]{1,0:T(8,128)(2,1)S(1)}) custom-call(bf16[256,256]{1,0:T(8,128)(2,1)S(1)} %get-tuple-element.17.refs_0_, bf16[256,256]{1,0:T(8,128)(2,1)S(1)} %get-tuple-element.18.refs_1_, bf16[512,512]{1,0:T(8,128)(2,1)S(1)} %get-tuple-element.15.refs_2_.refs_0_, ...), custom_call_target="tpu_custom_call" | custom-call | flops 1000000000 | bytes 1000000 | tf_op jit(solution)/shard_map/mix_first/pallas_call | solution.py:412
  13.5 0.0 copy-start
  13.5 0.0 copy-start.4
  13.5 0.5 %mix_rest.1 = (f32[64,225]{1,0:T(8,128)S(1)}, f32[64,225]{1,0:T(8,128)S(1)}, f32[64,225]{1,0:T(8,128)S(1)}) custom-call(bf16[512,512]{1,0:T(8,128)(2,1)S(1)} %get-tuple-element.15.refs_2_.refs_0_, bf16[512,512]{1,0:T(8,128)(2,1)S(1)} %get-tuple-element.16.refs_3_.refs_1_, f32[512,256]{1,0:T(8,128)S(1)} %early.1.refs_4_.refs_2_, ...), custom_call_target="tpu_custom_call" | custom-call | flops 1000000000 | bytes 1000000 | tf_op jit(solution)/shard_map/mix_rest/pallas_call | solution.py:426
  14.0 0.9 %collective-permute-start.4 = (f32[64,225]{1,0:T(8,128)S(1)}, f32[64,225]{1,0:T(8,128)S(1)}, u32[]{:S(2)}, u32[]{:S(2)}) collective-permute-start(f32[64,225]{1,0:T(8,128)S(1)} %get-tuple-element.23), channel_id=1, source_target_pairs={{0,3},{1,2},{2,1},{3,0},{4,7},{5,6},{6,5},{7,4},{8,11},{9,10},{10,... | collective-permute-start | bytes 172808 | tf_op jit(solution)/shard_map/ppermute | solution.py:542
  15.0 0.7 %collective-permute-start.5 = (f32[64,225]{1,0:T(8,128)S(1)}, f32[64,225]{1,0:T(8,128)S(1)}, u32[]{:S(2)}, u32[]{:S(2)}) collective-permute-start(f32[64,225]{1,0:T(8,128)S(1)} %get-tuple-element.24), channel_id=1, source_target_pairs={{0,1},{1,0},{2,3},{3,2},{4,5},{5,4},{6,7},{7,6},{8,9},{9,8},{10,11... | collective-permute-start | bytes 172808 | tf_op jit(solution)/shard_map/ppermute | solution.py:542
  15.7 0.5 %collective-permute-start.3 = (f32[64,225]{1,0:T(8,128)S(1)}, f32[64,225]{1,0:T(8,128)S(1)}, u32[]{:S(2)}, u32[]{:S(2)}) collective-permute-start(f32[64,225]{1,0:T(8,128)S(1)} %get-tuple-element.22), channel_id=1, source_target_pairs={{0,2},{1,3},{2,0},{3,1},{4,6},{5,7},{6,4},{7,5},{8,10},{9,11},{10,... | collective-permute-start | bytes 172808 | tf_op jit(solution)/shard_map/ppermute | solution.py:542
  16.9 0.0 copy-done
  16.9 0.0 copy-done.4
  16.9 0.0 copy-start.1
  16.9 0.0 copy-start.5
  16.9 0.0 copy-start.6
  17.0 0.0 copy-start.7
  17.0 2.0 %norm.1.normed = bf16[225,5120]{1,0:T(8,128)(2,1)S(1)} custom-call(bf16[225,5120]{1,0:T(8,128)(2,1)S(1)} %copy-done, f32[2,5120]{1,0:T(2,128)S(1)} %copy-done.4), custom_call_target="tpu_custom_call" | custom-call | flops 11520000 | bytes 10000000 | tf_op jit(solution)/shard_map/norm/pallas_call | solution.py:438
  18.9 0.0 copy-start.3
  19.0 0.0 copy-done.1
  19.0 0.0 copy-done.5
  19.0 0.0 copy-done.6
  19.0 0.0 copy-done.7
  19.0 0.8 %project.1 = (f32[64,225]{1,0:T(8,128)S(1)}, f32[64,128]{1,0:T(8,128)S(1)}, f32[8,128]{1,0:T(8,128)S(1)}) custom-call(bf16[225,5120]{1,0:T(8,128)(2,1)S(1)} %norm.1.normed, bf16[64,5120]{1,0:T(8,128)(2,1)S(1)} %bitcast.3, f32[1,64]{1,0:T(1,128)S(1)} %bitcast.4, f32[64,225]{1,0:T(8,128)S(1)} %copy-done.2, f32[2,16]{1,0:T(2,128)S(1)} %copy-done.5, ...), custom_call_target="tpu_custom_call" | custom-call | flops 147456000 | bytes 3000000 | tf_op jit(solution)/shard_map/project/pallas_call | solution.py:450
  19.8 0.0 collective-permute-done.4.refs_2_
  19.9 0.0 collective-permute-done.5.refs_3_
  19.9 0.1 collective-permute-done.3.refs_1_
  20.0 0.0 copy-done.3
  20.0 0.7 %finish.1 = (f32[64,225]{1,0:T(8,128)}, f32[64,225]{1,0:T(8,128)}) custom-call(f32[64,225]{1,0:T(8,128)S(1)} %get-tuple-element.21.refs_0_, f32[64,225]{1,0:T(8,128)S(1)} %collective-permute-done.3.refs_1_, f32[64,225]{1,0:T(8,128)S(1)} %collective-permute-done.4.refs_2_, f32[64,225]{1,0:T(8,128)S(1)} %collective-permute-done.5.refs_3_, ...), custom_call_target="tpu_custom_call" | custom-call | tf_op jit(solution)/shard_map/finish/pallas_call | solution.py:509
Async XLA Ops:
  0.6 11.0 %copy-start.2 = (f32[64,225]{1,0:T(8,128)S(1)}, f32[64,225]{1,0:T(8,128)}, u32[]{:S(2)}) copy-start(f32[64,225]{1,0:T(8,128)} %residual.1) | copy-start | bytes 172804
  0.6 11.9 %collective-permute-start.1 = (f32[64,225]{1,0:T(8,128)}, f32[64,225]{1,0:T(8,128)S(1)}, u32[]{:S(2)}, u32[]{:S(2)}) collective-permute-start(f32[64,225]{1,0:T(8,128)} %residual.1), channel_id=1, source_target_pairs={{0,12},{1,13},{2,14},{3,15},{4,8},{5,9},{6,10},{7,11},{8,4},{9,5},... | collective-permute-start | bytes 172808 | tf_op jit(solution)/shard_map/ppermute | solution.py:542
  5.8 5.8 %collective-permute-start = (f32[64,225]{1,0:T(8,128)}, f32[64,225]{1,0:T(8,128)S(1)}, u32[]{:S(2)}, u32[]{:S(2)}) collective-permute-start(f32[64,225]{1,0:T(8,128)} %residual.1), channel_id=1, source_target_pairs={{0,8},{1,9},{2,10},{3,11},{4,12},{5,13},{6,14},{7,15},{8,0},{9,1},... | collective-permute-start | bytes 172808 | tf_op jit(solution)/shard_map/ppermute | solution.py:542
  5.8 6.8 %collective-permute-start.2 = (f32[64,225]{1,0:T(8,128)}, f32[64,225]{1,0:T(8,128)S(1)}, u32[]{:S(2)}, u32[]{:S(2)}) collective-permute-start(f32[64,225]{1,0:T(8,128)} %residual.1), channel_id=1, source_target_pairs={{0,4},{1,5},{2,6},{3,7},{4,0},{5,1},{6,2},{7,3},{8,12},{9,13},{10,... | collective-permute-start | bytes 172808 | tf_op jit(solution)/shard_map/ppermute | solution.py:542
  13.5 3.4 %copy-start = (bf16[225,5120]{1,0:T(8,128)(2,1)S(1)}, bf16[225,5120]{1,0:T(8,128)(2,1)}, u32[]{:S(2)}) copy-start(bf16[225,5120]{1,0:T(8,128)(2,1)} %hidden.1) | copy-start | bytes 6912004
  13.5 3.4 %copy-start.4 = (f32[2,5120]{1,0:T(2,128)S(1)}, f32[2,5120]{1,0:T(2,128)}, u32[]{:S(2)}) copy-start(f32[2,5120]{1,0:T(2,128)} %modulation.1) | copy-start | bytes 122884
  14.0 5.8 %collective-permute-start.4 = (f32[64,225]{1,0:T(8,128)S(1)}, f32[64,225]{1,0:T(8,128)S(1)}, u32[]{:S(2)}, u32[]{:S(2)}) collective-permute-start(f32[64,225]{1,0:T(8,128)S(1)} %get-tuple-element.23), channel_id=1, source_target_pairs={{0,3},{1,2},{2,1},{3,0},{4,7},{5,6},{6,5},{7,4},{8,11},{9,10},{10,... | collective-permute-start | bytes 172808 | tf_op jit(solution)/shard_map/ppermute | solution.py:542
  15.0 4.9 %collective-permute-start.5 = (f32[64,225]{1,0:T(8,128)S(1)}, f32[64,225]{1,0:T(8,128)S(1)}, u32[]{:S(2)}, u32[]{:S(2)}) collective-permute-start(f32[64,225]{1,0:T(8,128)S(1)} %get-tuple-element.24), channel_id=1, source_target_pairs={{0,1},{1,0},{2,3},{3,2},{4,5},{5,4},{6,7},{7,6},{8,9},{9,8},{10,11... | collective-permute-start | bytes 172808 | tf_op jit(solution)/shard_map/ppermute | solution.py:542
  15.7 4.3 %collective-permute-start.3 = (f32[64,225]{1,0:T(8,128)S(1)}, f32[64,225]{1,0:T(8,128)S(1)}, u32[]{:S(2)}, u32[]{:S(2)}) collective-permute-start(f32[64,225]{1,0:T(8,128)S(1)} %get-tuple-element.22), channel_id=1, source_target_pairs={{0,2},{1,3},{2,0},{3,1},{4,6},{5,7},{6,4},{7,5},{8,10},{9,11},{10,... | collective-permute-start | bytes 172808 | tf_op jit(solution)/shard_map/ppermute | solution.py:542
  16.9 2.0 %copy-start.1 = (bf16[5120,64]{0,1:T(8,128)(2,1)S(1)}, bf16[5120,64]{0,1:T(8,128)(2,1)}, u32[]{:S(2)}) copy-start(bf16[5120,64]{0,1:T(8,128)(2,1)} %param.13) | copy-start | bytes 1966084
  16.9 2.0 %copy-start.5 = (f32[2,16]{1,0:T(2,128)S(1)}, f32[2,16]{1,0:T(2,128)}, u32[]{:S(2)}) copy-start(f32[2,16]{1,0:T(2,128)} %band_gain.1) | copy-start | bytes 388
  16.9 2.0 %copy-start.6 = (f32[64]{0:T(128)S(1)}, f32[64]{0:T(128)}, u32[]{:S(2)}) copy-start(f32[64]{0:T(128)} %param.14) | copy-start | bytes 772
  17.0 2.0 %copy-start.7 = (s32[50]{0:T(128)S(1)}, s32[50]{0:T(128)}, u32[]{:S(2)}) copy-start(s32[50]{0:T(128)} %param.20) | copy-start | bytes 604
  18.9 1.0 %copy-start.3 = (f32[64,225]{1,0:T(8,128)S(1)}, f32[64,225]{1,0:T(8,128)}, u32[]{:S(2)}) copy-start(f32[64,225]{1,0:T(8,128)} %refs_7_.1) | copy-start | bytes 172804

commit v4 on v3

--- a/solution.py
+++ b/solution.py
@@ -88,10 +88,21 @@
         return 2 * (owner * self.tokens // PW)
 
 
+def cosine_of_turns(turns):
+    angle = 2.0 * math.pi * (0.25 - jnp.abs(turns - 0.5))
+    square = angle * angle
+    series = jnp.full_like(square, -1.0 / math.factorial(11))
+    for power in (9, 7, 5, 3, 1):
+        series = series * square + (-1.0) ** (power // 2) / math.factorial(power)
+    return -angle * series
+
+
 def waves(places, length):
-    turns = lax.rem(places * iota(places.shape, 1), length).astype(jnp.float32)
-    angles = turns * (2.0 * math.pi / length)
-    return jnp.concatenate([jnp.cos(angles), jnp.sin(angles)], axis=1)
+    phase = (places * iota(places.shape, 1)).astype(jnp.float32)
+    phase = phase - length * jnp.floor((phase + 0.5) * (1.0 / length))
+    turns = phase * (1.0 / length)
+    later = jnp.where(turns < 0.25, turns + 0.75, turns - 0.25)
+    return jnp.concatenate([cosine_of_turns(turns), cosine_of_turns(later)], axis=1)
 
 
 def kept_modes(shape, length, cutoff):
@@ -101,25 +112,14 @@
     return jnp.concatenate([kept, kept], axis=1)
 
 
-def bands_kernel(
-    layout,
-    cut_rows,
-    cut_cols,
-    col_high,
-    col_low,
-    row_high,
-    row_low,
-):
+def bands_kernel(layout, cut_rows, cut_cols, col_filter, *row_filters):
     seq_index = lax.axis_index("seq")
     position = lax.rem(seq_index, layout.members)
     frame = seq_index // layout.members
 
-    shape = (2 * LANES, LANES)
-    line = iota(shape, 0)
-    odd = line >= LANES
-    column = jnp.where(odd, line - LANES, line)
-    table = waves(2 * column + odd.astype(jnp.int32), W)
-    table = jnp.where(jnp.concatenate([column, column], axis=1) < PW, table, 0.0)
+    column = iota((PW, LANES), 0)
+    gap = jnp.zeros((LANES - PW, 2 * LANES), jnp.float32)
+    table = jnp.concatenate([waves(2 * column, W), gap, waves(2 * column + 1, W), gap], axis=0)
 
     def tables(owners):
         line = iota((len(owners) * layout.lines, LANES), 0)
@@ -132,10 +132,10 @@
     givers, takers = layout.owners(position)
     given = tables(givers)
     taken = tables(takers)
-    kept = kept_modes(shape, W, cut_cols[frame])
+    kept = kept_modes((2 * LANES, LANES), W, cut_cols[frame])
     high, low = split(dot3(split(table * kept), split(table), ((1,), (1,))))
-    col_high[...] = high
-    col_low[...] = low
+    for n, part in enumerate((high, high, low)):
+        col_filter[n * 2 * LANES : (n + 1) * 2 * LANES, :] = part
     kept = kept_modes((given.shape[0], LANES), H, cut_rows[frame])
     small = dot3(split(taken), split(given * kept), ((1,), (1,)))
     wide = given.shape[0]
@@ -145,18 +145,26 @@
     )
     shape = (layout.channels, size)
     same = lax.rem(iota(shape, 1), layout.channels) == iota(shape, 0)
-    for part, out in zip(split(small), (row_high, row_low)):
+    each = size // len(row_filters)
+    for part, spots in zip(split(small), ((0, 2), (1,))):
         repeated = jnp.dot(part, spread, preferred_element_type=jnp.float32)
         for n in range(taken.shape[0]):
-            block = jnp.where(same, repeated[n : n + 1], 0.0)
+            block = jnp.where(same, repeated[n : n + 1], 0.0).astype(jnp.bfloat16)
             place = slice(n * layout.channels, (n + 1) * layout.channels)
-            out[place, :] = block.astype(jnp.bfloat16)
-
-
-def filtered(layout, slots, sources, filters, scratch):
+            for half, out in enumerate(row_filters):
+                for spot in spots:
+                    out[place, spot * each : (spot + 1) * each] = block[
+                        :, half * each : (half + 1) * each
+                    ]
+
+
+def product(left, right):
+    return jnp.dot(left, right, preferred_element_type=jnp.float32)
+
+
+def filtered(layout, slots, sources, col_filter, scratch):
     span, groups, channels, tokens = layout.span, layout.groups, layout.channels, layout.tokens
-    col_high, col_low = filters[:2]
-    window, lines, data_high, data_low = scratch
+    window, lines, data = scratch
     givers, _ = layout.owners(lax.rem(lax.axis_index("seq"), layout.members))
     lane = iota((layout.rows, LANES), 1)
     chunks = window.shape[1] // LANES
@@ -185,23 +193,17 @@
                 first = ((k * span + r) * 2 + dy) * channels
                 for dx in range(2):
                     high, low = split(lines[r, pl.ds(2 * dy + dx, channels, stride=4), :])
-                    place = (slice(first, first + channels), slice(dx * LANES, (dx + 1) * LANES))
-                    data_high[place] = high
-                    data_low[place] = low
-    return dot3((data_high[...], data_low[...]), (col_high[...], col_low[...]))
-
-
-def slots_columns(layout, slots):
-    each = layout.lines * layout.channels
-    return slice(slots[0] * each, (slots[-1] + 1) * each)
-
-
-def early_kernel(layout, slots, *refs):
-    sources = refs[4 : 4 + len(slots)]
-    carry = refs[4 + len(slots)]
-    data = filtered(layout, slots, sources, refs[:4], refs[5 + len(slots) :])
-    columns = slots_columns(layout, slots)
-    carry[...] = dot3([f[:, columns] for f in refs[2:4]], split(data))
+                    for n, part in enumerate((high, low, high)):
+                        left = (2 * n + dx) * LANES
+                        data[first : first + channels, left : left + LANES] = part
+    high, low = split(product(data[...], col_filter[...]))
+    return jnp.concatenate([high, high, low], axis=0)
+
+
+def early_kernel(layout, slots, col_filter, row_filter, *refs):
+    sources, carry = refs[: len(slots)], refs[len(slots)]
+    data = filtered(layout, slots, sources, col_filter, refs[len(slots) + 1 :])
+    carry[...] = product(row_filter[...], data)
 
 
 def place_part(layout, mixed, taker, out):
@@ -237,36 +239,28 @@
                 out[first : first + channels, g * LANES : last] = value[:, : last - g * LANES]
 
 
-def first_kernel(layout, slots, m, *refs):
-    filters, carry = refs[:4], refs[4]
-    sources = refs[5 : 5 + len(slots)]
-    out, data_high, data_low = refs[5 + len(slots) : 8 + len(slots)]
-    high, low = split(filtered(layout, slots, sources, filters, refs[8 + len(slots) :]))
-    data_high[...] = high
-    data_low[...] = low
+def first_kernel(layout, slots, m, col_filter, row_filter, carry, *refs):
+    sources = refs[: len(slots)]
+    out, data = refs[len(slots) : len(slots) + 2]
+    found = filtered(layout, slots, sources, col_filter, refs[len(slots) + 2 :])
+    data[...] = found
     each = layout.lines * layout.channels
     _, takers = layout.owners(lax.rem(lax.axis_index("seq"), layout.members))
     rows = slice(m * each, (m + 1) * each)
-    columns = slots_columns(layout, slots)
-    mixed = carry[rows, :] + dot3([f[rows, columns] for f in filters[2:]], (high, low))
-    place_part(layout, mixed, takers[m], out)
-
-
-def rest_kernel(layout, slots, others, *refs):
-    row_high, row_low, carry, data_high, data_low = refs[:5]
+    place_part(layout, carry[rows, :] + product(row_filter[rows, :], found), takers[m], out)
+
+
+def rest_kernel(layout, others, row_filter, carry, data, *outs):
     _, takers = layout.owners(lax.rem(lax.axis_index("seq"), layout.members))
     each = layout.lines * layout.channels
-    columns = slots_columns(layout, slots)
-    for m, out in zip(others, refs[5:]):
+    for m, out in zip(others, outs):
         rows = slice(m * each, (m + 1) * each)
-        filters = [f[rows, columns] for f in (row_high, row_low)]
-        mixed = carry[rows, :] + dot3(filters, (data_high[...], data_low[...]))
+        mixed = carry[rows, :] + product(row_filter[rows, :], data[...])
         place_part(layout, mixed, takers[m], out)
 
 
-def norm_kernel(hidden, modulation, normed, scale):
-    tokens, width = hidden.shape
-    tiles = [slice(t, t + LANES) for t in range(0, width, LANES)]
+def norm_rows(hidden, modulation, scale, normed, start, stop):
+    tiles = [slice(t, t + LANES) for t in range(0, hidden.shape[1], LANES)]
     block, pair = 16, 2
     scale[...] = 1.0 + modulation[1:2, :]
 
@@ -282,31 +276,38 @@
         scale_inv = lax.rsqrt(square - average * average + EPSILON)
         return [jnp.broadcast_to(v, (count, LANES)) for v in (average, scale_inv)]
 
-    def norm(rows, average, scale_inv):
+    def norm(rows, place, average, scale_inv):
         for columns in tiles:
             value = hidden[rows, columns].astype(jnp.float32)
             value = (value - average) * scale_inv
             value = value * scale[:, columns] + modulation[0:1, columns]
-            normed[rows, columns] = value.astype(jnp.bfloat16)
-
-    whole = tokens // (block * pair)
+            normed[place, columns] = value.astype(jnp.bfloat16)
+
+    whole = (stop - start) // (block * pair)
 
     @pl.loop(0, whole)
     def _(n):
         first = pl.multiple_of(n * (block * pair), block)
-        rows = [pl.ds(first + p * block, block) for p in range(pair)]
+        rows = [pl.ds(start + first + p * block, block) for p in range(pair)]
         found = [moments(r, block) for r in rows]
-        for r, f in zip(rows, found):
-            norm(r, *f)
-
-    for first in range(whole * block * pair, tokens, block):
-        last = min(tokens, first + block)
-        norm(slice(first, last), *moments(slice(first, last), last - first))
+        for p in range(pair):
+            norm(rows[p], pl.ds(first + p * block, block), *found[p])
+
+    for first in range(start + whole * block * pair, stop, block):
+        rows = slice(first, min(stop, first + block))
+        found = moments(rows, rows.stop - first)
+        norm(rows, slice(first - start, rows.stop - start), *found)
+
+
+def norm_kernel(hidden, modulation, normed, scale):
+    norm_rows(hidden, modulation, scale, normed, 0, normed.shape[0])
 
 
 def project_kernel(
     layout,
-    normed,
+    early_normed,
+    hidden,
+    modulation,
     weight,
     bias,
     residual,
@@ -316,15 +317,10 @@
     base,
     row_low,
     step,
+    normed,
+    scale,
 ):
-    conditional = lax.dot_general(
-        normed[...],
-        weight[...],
-        (((1,), (1,)), ((), ())),
-        preferred_element_type=jnp.float32,
-    )
-    conditional = (conditional + bias[...]).T
-
+    tokens, first = hidden.shape[0], early_normed.shape[0]
     current = jnp.full((1, 1), step_index[0], jnp.int32)
     counter = iota(skip_flags.shape, 1)
     computed = (skip_flags[...] == 0) & (counter <= current)
@@ -337,7 +333,18 @@
         jnp.sum(jnp.where(own, band_gain[n : n + 1, :], 0.0), axis=1, keepdims=True) * factor
         for n, factor in enumerate((1.0 + gap_ratio, 1.0 - 0.5 * gap_ratio))
     )
-    base[...] = conditional + GUIDE_EXTRA * w_high * residual[...]
+
+    def project(rows, columns):
+        conditional = lax.dot_general(
+            rows[...], weight[...], (((1,), (1,)), ((), ())), preferred_element_type=jnp.float32
+        )
+        conditional = (conditional + bias[...]).T
+        base[:, columns] = conditional + GUIDE_EXTRA * w_high * residual[:, columns]
+
+    if first:
+        project(early_normed, slice(0, first))
+    norm_rows(hidden, modulation, scale, normed, first, tokens)
+    project(normed, slice(first, tokens))
     row_low[...] = jnp.broadcast_to(GUIDE_EXTRA * (w_low - w_high), row_low.shape)
     step[...] = jnp.broadcast_to(sigma_at(current + 1) - sigma_at(current), step.shape)
 
@@ -369,13 +376,13 @@
 def bands(layout, cut_rows, cut_cols):
     wide = layout.far * layout.lines * layout.channels
     tall = layout.near * layout.lines * layout.channels
-    col = jax.ShapeDtypeStruct((2 * LANES, 2 * LANES), jnp.bfloat16)
-    row = jax.ShapeDtypeStruct((tall, wide), jnp.bfloat16)
+    col = jax.ShapeDtypeStruct((6 * LANES, 2 * LANES), jnp.bfloat16)
+    row = jax.ShapeDtypeStruct((tall, 3 * wide // 2), jnp.bfloat16)
     return pl.pallas_call(
         functools.partial(bands_kernel, layout),
-        out_shape=[col, col, row, row],
+        out_shape=[col, row, row],
         in_specs=[SMEM, SMEM],
-        out_specs=[VMEM] * 4,
+        out_specs=[VMEM] * 3,
         compiler_params=pltpu.CompilerParams(vmem_limit_bytes=8 * 2**20),
         cost_estimate=pl.CostEstimate(flops=10**9, bytes_accessed=2 * 10**7, transcendentals=0),
         name="bands",
@@ -383,12 +390,10 @@
 
 
 def mix_scratch(layout, count):
-    data = pltpu.VMEM((count * layout.lines * layout.channels, 2 * LANES), jnp.bfloat16)
     return [
         pltpu.VMEM((layout.rows, pl.cdiv(layout.tokens, LANES) * LANES), jnp.float32),
         pltpu.VMEM((layout.span, layout.rows, LANES), jnp.float32),
-        data,
-        data,
+        pltpu.VMEM((count * layout.lines * layout.channels, 6 * LANES), jnp.bfloat16),
     ]
 
 
@@ -397,7 +402,7 @@
     return pl.pallas_call(
         functools.partial(early_kernel, layout, slots),
         out_shape=jax.ShapeDtypeStruct((tall, 2 * LANES), jnp.float32),
-        in_specs=[VMEM] * (4 + len(slots)),
+        in_specs=[VMEM] * (2 + len(slots)),
         out_specs=VMEM,
         scratch_shapes=mix_scratch(layout, len(slots)),
         compiler_params=pltpu.CompilerParams(vmem_limit_bytes=8 * 2**20),
@@ -408,12 +413,14 @@
 
 def mix_first(layout, filters, carry, slots, sources, m):
     wide = len(slots) * layout.lines * layout.channels
-    data = jax.ShapeDtypeStruct((wide, 2 * LANES), jnp.bfloat16)
     return pl.pallas_call(
         functools.partial(first_kernel, layout, slots, m),
-        out_shape=[jax.ShapeDtypeStruct((layout.rows, layout.tokens), jnp.float32), data, data],
-        in_specs=[VMEM] * (5 + len(slots)),
-        out_specs=[VMEM] * 3,
+        out_shape=[
+            jax.ShapeDtypeStruct((layout.rows, layout.tokens), jnp.float32),
+            jax.ShapeDtypeStruct((3 * wide, 2 * LANES), jnp.bfloat16),
+        ],
+        in_specs=[VMEM] * (3 + len(slots)),
+        out_specs=[VMEM] * 2,
         scratch_shapes=mix_scratch(layout, len(slots)),
         compiler_params=pltpu.CompilerParams(vmem_limit_bytes=8 * 2**20),
         cost_estimate=pl.CostEstimate(flops=10**9, bytes_accessed=10**6, transcendentals=0),
@@ -421,26 +428,28 @@
     )(*filters, carry, *sources)
 
 
-def mix_rest(layout, filters, carry, slots, data, others):
+def mix_rest(layout, row_filter, carry, data, others):
     shape = jax.ShapeDtypeStruct((layout.rows, layout.tokens), jnp.float32)
     return pl.pallas_call(
-        functools.partial(rest_kernel, layout, slots, others),
+        functools.partial(rest_kernel, layout, others),
         out_shape=[shape] * len(others),
-        in_specs=[VMEM] * 5,
+        in_specs=[VMEM] * 3,
         out_specs=[VMEM] * len(others),
         compiler_params=pltpu.CompilerParams(vmem_limit_bytes=8 * 2**20),
         cost_estimate=pl.CostEstimate(flops=10**9, bytes_accessed=10**6, transcendentals=0),
         name="mix_rest",
-    )(*filters[2:], carry, *data)
+    )(row_filter, carry, data)
 
 
 def head(layout, hidden, modulation, head_weight, head_bias, residual, gain, flags, step_index):
+    first = hidden.shape[0] // LANES * LANES
+    scale = pltpu.VMEM((1, hidden.shape[1]), jnp.float32)
     normed = pl.pallas_call(
         norm_kernel,
-        out_shape=jax.ShapeDtypeStruct(hidden.shape, jnp.bfloat16),
+        out_shape=jax.ShapeDtypeStruct((first, hidden.shape[1]), jnp.bfloat16),
         in_specs=[VMEM] * 2,
         out_specs=VMEM,
-        scratch_shapes=[pltpu.VMEM((1, hidden.shape[1]), jnp.float32)],
+        scratch_shapes=[scale],
         compiler_params=pltpu.CompilerParams(vmem_limit_bytes=8 * 2**20),
         cost_estimate=pl.CostEstimate(
             flops=10 * hidden.size, bytes_accessed=10**7, transcendentals=0
@@ -454,8 +463,12 @@
             jax.ShapeDtypeStruct((layout.rows, LANES), jnp.float32),
             jax.ShapeDtypeStruct((8, LANES), jnp.float32),
         ],
-        in_specs=[VMEM] * 6 + [SMEM],
+        in_specs=[VMEM] * 8 + [SMEM],
         out_specs=[VMEM] * 3,
+        scratch_shapes=[
+            pltpu.VMEM((hidden.shape[0] - first, hidden.shape[1]), jnp.bfloat16),
+            scale,
+        ],
         compiler_params=pltpu.CompilerParams(vmem_limit_bytes=8 * 2**20),
         cost_estimate=pl.CostEstimate(
             flops=2 * hidden.size * layout.rows, bytes_accessed=3 * 10**6, transcendentals=0
@@ -463,6 +476,8 @@
         name="project",
     )(
         normed,
+        hidden,
+        modulation,
         head_weight.T,
         head_bias.reshape(1, -1),
         residual,
@@ -543,7 +558,7 @@
         return swapped
 
     sources = exchange([residual] * layout.far, layout.near)
-    filters = bands(layout, cut_rows, cut_cols)
+    col_filter, row_early, row_late = bands(layout, cut_rows, cut_cols)
     run_head = head if lax.axis_size("mp") == 1 else head_in_parts
     base, row_low, step = run_head(
         layout,
@@ -558,10 +573,10 @@
     )
     slots = list(range(layout.far))
     half = layout.far // 2
-    carry = early(layout, filters, slots[:half], sources[:half])
-    late, others = slots[half:], [0, *range(2, layout.near)]
-    part, *data = mix_first(layout, filters, carry, late, sources[half:], 1)
-    own, *rest = mix_rest(layout, filters, carry, late, data, others)
+    carry = early(layout, (col_filter, row_early), slots[:half], sources[:half])
+    filters = (col_filter, row_late)
+    part, data = mix_first(layout, filters, carry, slots[half:], sources[half:], 1)
+    own, *rest = mix_rest(layout, row_late, carry, data, [0, *range(2, layout.near)])
     parts = exchange([own, part, *rest], 1)
     return finish(layout, parts, base, row_low, step, latent)
 

time: 20.9 us -> 20.2 us (0.967)
  waiting for transfers between devices: 3.09 us -> 2.03 us
  Pallas kernels: 6.82 us -> 7.29 us
    pallas_call x1, Pallas kernels: 0.83 us -> 2.48 us  [head(): pl.pallas_call(functools.partial(project_kernel, layout), out_shape=[jax....]
    pallas_call x3, Pallas kernels: 3.39 us -> 2.22 us  [the longest x1 1.06 us: head(): pl.pallas_call(norm_kernel, out_shape=jax.ShapeDtypeStruct((first, hidden...]
    ppermute x6, waiting for transfers between devices: 3.09 us -> 2.03 us  [exchange(): swapped.append(lax.ppermute(values[turn + 1], 'seq', pairs))]
  transfers between devices with their start and end apart: 6 -> 6, of which waited for: 2 -> 3; matrix products, arithmetic and copies ran while one was open for 0% -> 0% of each run, Pallas kernels for 23% -> 26%
where the time goes in v4:
time: 20.2 us; the launch traced here: 20 us
  starting transfers between devices  7.92 us (39%)
  Pallas kernels  7.29 us (36%)
  between operations  2.76 us (14%)
  waiting for transfers between devices  2.03 us (10%)
    ppermute x6, starting transfers between devices, exchange(): swapped.append(lax.ppermute(values[turn + 1], 'seq', pairs))  7.92 us
    pallas_call x1, Pallas kernels, head(): pl.pallas_call(functools.partial(project_kernel, layout), out_shape=[jax....  2.48 us
    ppermute x6, waiting for transfers between devices, exchange(): swapped.append(lax.ppermute(values[turn + 1], 'seq', pairs))  2.03 us
    pallas_call x1, Pallas kernels, head(): pl.pallas_call(norm_kernel, out_shape=jax.ShapeDtypeStruct((first, hidden...  1.06 us
    pallas_call x1, Pallas kernels, early(): pl.pallas_call(functools.partial(early_kernel, layout, slots), out_shape=...  0.96 us
    pallas_call x1, Pallas kernels, mix_first(): pl.pallas_call(functools.partial(first_kernel, layout, slots, m), out_sha...  0.9 us
    pallas_call x1, Pallas kernels, finish(): pl.pallas_call(functools.partial(finish_kernel, layout), out_shape=[shape...  0.73 us
    pallas_call x1, Pallas kernels, bands(): pl.pallas_call(functools.partial(bands_kernel, layout), out_shape=[col, r...  0.65 us
  transfers between devices with their start and end apart: 6, of which 3 were waited for; matrix products, arithmetic and copies ran while one was open for 0% of the time, Pallas kernels for 26%

profile of v4, /device:TPU:0, one launch (start us, length us, event | category | flops | bytes accessed | tf_op | source)
XLA Modules:
  0.0 20.0 jit_solution(10318748305689353585)
XLA Ops:
  0.6 0.0 copy-start.3
  0.6 4.1 %collective-permute-start = (f32[64,225]{1,0:T(8,128)}, f32[64,225]{1,0:T(8,128)S(1)}, u32[]{:S(2)}, u32[]{:S(2)}) collective-permute-start(f32[64,225]{1,0:T(8,128)} %residual.1), channel_id=1, source_target_pairs={{0,8},{1,9},{2,10},{3,11},{4,12},{5,13},{6,14},{7,15},{8,0},{9,1},... | collective-permute-start | bytes 172808 | tf_op jit(solution)/shard_map/ppermute | solution.py:557
  4.8 1.3 %collective-permute-start.1 = (f32[64,225]{1,0:T(8,128)}, f32[64,225]{1,0:T(8,128)S(1)}, u32[]{:S(2)}, u32[]{:S(2)}) collective-permute-start(f32[64,225]{1,0:T(8,128)} %residual.1), channel_id=1, source_target_pairs={{0,12},{1,13},{2,14},{3,15},{4,8},{5,9},{6,10},{7,11},{8,4},{9,5},... | collective-permute-start | bytes 172808 | tf_op jit(solution)/shard_map/ppermute | solution.py:557
  6.1 0.2 %collective-permute-start.2 = (f32[64,225]{1,0:T(8,128)}, f32[64,225]{1,0:T(8,128)S(1)}, u32[]{:S(2)}, u32[]{:S(2)}) collective-permute-start(f32[64,225]{1,0:T(8,128)} %residual.1), channel_id=1, source_target_pairs={{0,4},{1,5},{2,6},{3,7},{4,0},{5,1},{6,2},{7,3},{8,12},{9,13},{10,... | collective-permute-start | bytes 172808 | tf_op jit(solution)/shard_map/ppermute | solution.py:557
  7.6 0.7 %bands.1 = (bf16[768,256]{1,0:T(8,128)(2,1)S(1)}, bf16[512,768]{1,0:T(8,128)(2,1)S(1)}, bf16[512,768]{1,0:T(8,128)(2,1)S(1)}) custom-call(s32[1]{0:T(128)S(6)} %copy.13.cut_rows, s32[1]{0:T(128)S(6)} %copy.14.cut_cols), custom_call_target="tpu_custom_call" | custom-call | flops 1000000000 | bytes 20000000 | tf_op jit(solution)/shard_map/bands/pallas_call | solution.py:381
  8.3 0.4 %collective-permute-done.refs_1_ = f32[64,225]{1,0:T(8,128)S(1)} collective-permute-done((f32[64,225]{1,0:T(8,128)}, f32[64,225]{1,0:T(8,128)S(1)}, u32[]{:S(2)}, u32[]{:S(2)}) %collective-permute-start) | collective-permute-done | bytes 57632 | tf_op jit(solution)/shard_map/ppermute | solution.py:557
  8.7 0.0 copy-done.3
  8.7 1.0 %early.1.carry = f32[512,256]{1,0:T(8,128)S(1)} custom-call(bf16[768,256]{1,0:T(8,128)(2,1)S(1)} %get-tuple-element.14.col_filter, bf16[512,768]{1,0:T(8,128)(2,1)S(1)} %get-tuple-element.15.row_filter, f32[64,225]{1,0:T(8,128)S(1)} %copy-done.3, f32[64,225]{1,0:T(8,128)S(1)} %collective-permute-done.refs_1_), custom_call_target="tpu_custom_call" | custom-call | flops 1000000000 | bytes 1000000 | tf_op jit(solution)/shard_map/early/pallas_call | solution.py:402
  9.7 1.5 %collective-permute-done.1.refs_0_ = f32[64,225]{1,0:T(8,128)S(1)} collective-permute-done((f32[64,225]{1,0:T(8,128)}, f32[64,225]{1,0:T(8,128)S(1)}, u32[]{:S(2)}, u32[]{:S(2)}) %collective-permute-start.1) | collective-permute-done | bytes 57632 | tf_op jit(solution)/shard_map/ppermute | solution.py:557
  11.2 0.1 collective-permute-done.2.refs_1_
  11.3 0.9 %mix_first.1 = (f32[64,225]{1,0:T(8,128)S(1)}, bf16[768,256]{1,0:T(8,128)(2,1)S(1)}) custom-call(bf16[768,256]{1,0:T(8,128)(2,1)S(1)} %get-tuple-element.14.col_filter, bf16[512,768]{1,0:T(8,128)(2,1)S(1)} %get-tuple-element.13.row_filter, f32[512,256]{1,0:T(8,128)S(1)} %early.1.carry, f32[64,225]{1,0:T(8,128)S(1)} %collective-permute-done.1.refs_0_, ...), custom_call_target="tpu_custom_call" | custom-call | flops 1000000000 | bytes 1000000 | tf_op jit(solution)/shard_map/mix_first/pallas_call | solution.py:416
  12.2 0.0 copy-start
  12.2 0.0 copy-start.2
  12.2 0.5 %mix_rest.1 = (f32[64,225]{1,0:T(8,128)S(1)}, f32[64,225]{1,0:T(8,128)S(1)}, f32[64,225]{1,0:T(8,128)S(1)}) custom-call(bf16[512,768]{1,0:T(8,128)(2,1)S(1)} %get-tuple-element.13.row_filter, f32[512,256]{1,0:T(8,128)S(1)} %early.1.carry, bf16[768,256]{1,0:T(8,128)(2,1)S(1)} %get-tuple-element.16.data), custom_call_target="tpu_custom_call" | custom-call | flops 1000000000 | bytes 1000000 | tf_op jit(solution)/shard_map/mix_rest/pallas_call | solution.py:433
  12.7 0.0 copy-start.1
  12.8 0.0 copy-start.5
  12.8 0.0 copy-start.6
  12.8 0.0 copy-start.7
  12.8 1.6 %collective-permute-start.3 = (f32[64,225]{1,0:T(8,128)S(1)}, f32[64,225]{1,0:T(8,128)S(1)}, u32[]{:S(2)}, u32[]{:S(2)}) collective-permute-start(f32[64,225]{1,0:T(8,128)S(1)} %get-tuple-element.18), channel_id=1, source_target_pairs={{0,2},{1,3},{2,0},{3,1},{4,6},{5,7},{6,4},{7,5},{8,10},{9,11},{10,... | collective-permute-start | bytes 172808 | tf_op jit(solution)/shard_map/ppermute | solution.py:557
  14.4 0.0 collective-permute-start.4
  14.4 0.6 %collective-permute-start.5 = (f32[64,225]{1,0:T(8,128)S(1)}, f32[64,225]{1,0:T(8,128)S(1)}, u32[]{:S(2)}, u32[]{:S(2)}) collective-permute-start(f32[64,225]{1,0:T(8,128)S(1)} %get-tuple-element.20), channel_id=1, source_target_pairs={{0,1},{1,0},{2,3},{3,2},{4,5},{5,4},{6,7},{7,6},{8,9},{9,8},{10,11... | collective-permute-start | bytes 172808 | tf_op jit(solution)/shard_map/ppermute | solution.py:557
  15.7 0.0 copy-done
  15.7 0.0 copy-done.2
  15.7 1.1 %norm.1.early_normed = bf16[128,5120]{1,0:T(8,128)(2,1)S(1)} custom-call(bf16[225,5120]{1,0:T(8,128)(2,1)S(1)} %copy-done, f32[2,5120]{1,0:T(2,128)S(1)} %copy-done.2), custom_call_target="tpu_custom_call" | custom-call | flops 11520000 | bytes 10000000 | tf_op jit(solution)/shard_map/norm/pallas_call | solution.py:447
  16.7 0.0 copy-start.4
  16.8 0.0 copy-done.1
  16.8 0.0 copy-done.5
  16.8 0.0 copy-done.6
  16.8 0.0 copy-done.7
  16.8 2.5 %project.1 = (f32[64,225]{1,0:T(8,128)S(1)}, f32[64,128]{1,0:T(8,128)S(1)}, f32[8,128]{1,0:T(8,128)S(1)}) custom-call(bf16[128,5120]{1,0:T(8,128)(2,1)S(1)} %norm.1.early_normed, bf16[225,5120]{1,0:T(8,128)(2,1)S(1)} %copy-done, f32[2,5120]{1,0:T(2,128)S(1)} %copy-done.2, bf16[64,5120]{1,0:T(8,128)(2,1)S(1)} %bitcast.3, f32[1,64]{1,0:T(1,128)S(1)} %bitcast.4, ...), custom_call_target="tpu_custom_call" | custom-call | flops 147456000 | bytes 3000000 | tf_op jit(solution)/shard_map/project/pallas_call | solution.py:459
  19.3 0.0 collective-permute-done.3.refs_1_
  19.3 0.0 collective-permute-done.4.refs_2_
  19.3 0.0 collective-permute-done.5.refs_3_
  19.3 0.0 copy-done.4
  19.3 0.7 %finish.1 = (f32[64,225]{1,0:T(8,128)}, f32[64,225]{1,0:T(8,128)}) custom-call(f32[64,225]{1,0:T(8,128)S(1)} %get-tuple-element.17.refs_0_, f32[64,225]{1,0:T(8,128)S(1)} %collective-permute-done.3.refs_1_, f32[64,225]{1,0:T(8,128)S(1)} %collective-permute-done.4.refs_2_, f32[64,225]{1,0:T(8,128)S(1)} %collective-permute-done.5.refs_3_, ...), custom_call_target="tpu_custom_call" | custom-call | tf_op jit(solution)/shard_map/finish/pallas_call | solution.py:524
Async XLA Ops:
  0.6 8.1 %copy-start.3 = (f32[64,225]{1,0:T(8,128)S(1)}, f32[64,225]{1,0:T(8,128)}, u32[]{:S(2)}) copy-start(f32[64,225]{1,0:T(8,128)} %residual.1) | copy-start | bytes 172804
  0.6 8.1 %collective-permute-start = (f32[64,225]{1,0:T(8,128)}, f32[64,225]{1,0:T(8,128)S(1)}, u32[]{:S(2)}, u32[]{:S(2)}) collective-permute-start(f32[64,225]{1,0:T(8,128)} %residual.1), channel_id=1, source_target_pairs={{0,8},{1,9},{2,10},{3,11},{4,12},{5,13},{6,14},{7,15},{8,0},{9,1},... | collective-permute-start | bytes 172808 | tf_op jit(solution)/shard_map/ppermute | solution.py:557
  4.8 6.4 %collective-permute-start.1 = (f32[64,225]{1,0:T(8,128)}, f32[64,225]{1,0:T(8,128)S(1)}, u32[]{:S(2)}, u32[]{:S(2)}) collective-permute-start(f32[64,225]{1,0:T(8,128)} %residual.1), channel_id=1, source_target_pairs={{0,12},{1,13},{2,14},{3,15},{4,8},{5,9},{6,10},{7,11},{8,4},{9,5},... | collective-permute-start | bytes 172808 | tf_op jit(solution)/shard_map/ppermute | solution.py:557
  6.1 5.2 %collective-permute-start.2 = (f32[64,225]{1,0:T(8,128)}, f32[64,225]{1,0:T(8,128)S(1)}, u32[]{:S(2)}, u32[]{:S(2)}) collective-permute-start(f32[64,225]{1,0:T(8,128)} %residual.1), channel_id=1, source_target_pairs={{0,4},{1,5},{2,6},{3,7},{4,0},{5,1},{6,2},{7,3},{8,12},{9,13},{10,... | collective-permute-start | bytes 172808 | tf_op jit(solution)/shard_map/ppermute | solution.py:557
  12.2 3.4 %copy-start = (bf16[225,5120]{1,0:T(8,128)(2,1)S(1)}, bf16[225,5120]{1,0:T(8,128)(2,1)}, u32[]{:S(2)}) copy-start(bf16[225,5120]{1,0:T(8,128)(2,1)} %hidden.3) | copy-start | bytes 6912004
  12.2 3.4 %copy-start.2 = (f32[2,5120]{1,0:T(2,128)S(1)}, f32[2,5120]{1,0:T(2,128)}, u32[]{:S(2)}) copy-start(f32[2,5120]{1,0:T(2,128)} %modulation.3) | copy-start | bytes 122884
  12.7 4.0 %copy-start.1 = (bf16[5120,64]{0,1:T(8,128)(2,1)S(1)}, bf16[5120,64]{0,1:T(8,128)(2,1)}, u32[]{:S(2)}) copy-start(bf16[5120,64]{0,1:T(8,128)(2,1)} %param.13) | copy-start | bytes 1966084
  12.8 4.0 %copy-start.5 = (f32[2,16]{1,0:T(2,128)S(1)}, f32[2,16]{1,0:T(2,128)}, u32[]{:S(2)}) copy-start(f32[2,16]{1,0:T(2,128)} %band_gain.1) | copy-start | bytes 388
  12.8 4.0 %copy-start.6 = (f32[64]{0:T(128)S(1)}, f32[64]{0:T(128)}, u32[]{:S(2)}) copy-start(f32[64]{0:T(128)} %param.14) | copy-start | bytes 772
  12.8 4.0 %copy-start.7 = (s32[50]{0:T(128)S(1)}, s32[50]{0:T(128)}, u32[]{:S(2)}) copy-start(s32[50]{0:T(128)} %param.20) | copy-start | bytes 604
  12.8 6.5 %collective-permute-start.3 = (f32[64,225]{1,0:T(8,128)S(1)}, f32[64,225]{1,0:T(8,128)S(1)}, u32[]{:S(2)}, u32[]{:S(2)}) collective-permute-start(f32[64,225]{1,0:T(8,128)S(1)} %get-tuple-element.18), channel_id=1, source_target_pairs={{0,2},{1,3},{2,0},{3,1},{4,6},{5,7},{6,4},{7,5},{8,10},{9,11},{10,... | collective-permute-start | bytes 172808 | tf_op jit(solution)/shard_map/ppermute | solution.py:557
  14.4 4.9 %collective-permute-start.4 = (f32[64,225]{1,0:T(8,128)S(1)}, f32[64,225]{1,0:T(8,128)S(1)}, u32[]{:S(2)}, u32[]{:S(2)}) collective-permute-start(f32[64,225]{1,0:T(8,128)S(1)} %get-tuple-element.19), channel_id=1, source_target_pairs={{0,3},{1,2},{2,1},{3,0},{4,7},{5,6},{6,5},{7,4},{8,11},{9,10},{10,... | collective-permute-start | bytes 172808 | tf_op jit(solution)/shard_map/ppermute | solution.py:557
  14.4 4.9 %collective-permute-start.5 = (f32[64,225]{1,0:T(8,128)S(1)}, f32[64,225]{1,0:T(8,128)S(1)}, u32[]{:S(2)}, u32[]{:S(2)}) collective-permute-start(f32[64,225]{1,0:T(8,128)S(1)} %get-tuple-element.20), channel_id=1, source_target_pairs={{0,1},{1,0},{2,3},{3,2},{4,5},{5,4},{6,7},{7,6},{8,9},{9,8},{10,11... | collective-permute-start | bytes 172808 | tf_op jit(solution)/shard_map/ppermute | solution.py:557
  16.7 2.6 %copy-start.4 = (f32[64,225]{1,0:T(8,128)S(1)}, f32[64,225]{1,0:T(8,128)}, u32[]{:S(2)}) copy-start(f32[64,225]{1,0:T(8,128)} %refs_7_.1) | copy-start | bytes 172804

commit v5 on v4

--- a/solution.py
+++ b/solution.py
@@ -74,12 +74,15 @@
         self.groups = pl.cdiv(self.span * PW, LANES)
 
     def owners(self, position):
-        givers = [position ^ (k * self.near) for k in self.order(self.far)]
-        takers = [position ^ m for m in self.order(self.near)]
+        givers = [position ^ (k * self.near) for k in self.far_order()]
+        takers = [position ^ m for m in self.near_order()]
         return givers, takers
 
-    def order(self, count):
-        return [0, *range(2, count), 1][:count]
+    def far_order(self):
+        return [0, *range(2, self.far), 1][: self.far]
+
+    def near_order(self):
+        return [0, *range(self.near - 1, 0, -1)]
 
     def offset(self, owner):
         return lax.rem(owner * self.tokens, PW)
@@ -259,7 +262,7 @@
         place_part(layout, mixed, takers[m], out)
 
 
-def norm_rows(hidden, modulation, scale, normed, start, stop):
+def norm_rows(hidden, modulation, scale, normed, start, stop, unroll=False):
     tiles = [slice(t, t + LANES) for t in range(0, hidden.shape[1], LANES)]
     block, pair = 16, 2
     scale[...] = 1.0 + modulation[1:2, :]
@@ -285,7 +288,7 @@
 
     whole = (stop - start) // (block * pair)
 
-    @pl.loop(0, whole)
+    @pl.loop(0, whole, unroll=unroll)
     def _(n):
         first = pl.multiple_of(n * (block * pair), block)
         rows = [pl.ds(start + first + p * block, block) for p in range(pair)]
@@ -343,7 +346,7 @@
 
     if first:
         project(early_normed, slice(0, first))
-    norm_rows(hidden, modulation, scale, normed, first, tokens)
+    norm_rows(hidden, modulation, scale, normed, first, tokens, unroll=True)
     project(normed, slice(first, tokens))
     row_low[...] = jnp.broadcast_to(GUIDE_EXTRA * (w_low - w_high), row_low.shape)
     step[...] = jnp.broadcast_to(sigma_at(current + 1) - sigma_at(current), step.shape)
@@ -550,14 +553,15 @@
     layout = Layout(*residual.shape)
     places = lax.axis_size("seq")
 
-    def exchange(values, unit):
+    def exchange(values, masks):
         swapped = [values[0]]
-        for turn, n in enumerate(layout.order(len(values))[1:]):
-            pairs = [(s, s ^ (n * unit)) for s in range(places)]
+        for turn, mask in enumerate(masks[1:]):
+            pairs = [(s, s ^ mask) for s in range(places)]
             swapped.append(lax.ppermute(values[turn + 1], "seq", pairs))
         return swapped
 
-    sources = exchange([residual] * layout.far, layout.near)
+    masks = [k * layout.near for k in layout.far_order()]
+    sources = exchange([residual] * layout.far, masks)
     col_filter, row_early, row_late = bands(layout, cut_rows, cut_cols)
     run_head = head if lax.axis_size("mp") == 1 else head_in_parts
     base, row_low, step = run_head(
@@ -577,7 +581,7 @@
     filters = (col_filter, row_late)
     part, data = mix_first(layout, filters, carry, slots[half:], sources[half:], 1)
     own, *rest = mix_rest(layout, row_late, carry, data, [0, *range(2, layout.near)])
-    parts = exchange([own, part, *rest], 1)
+    parts = exchange([own, part, *rest], layout.near_order())
     return finish(layout, parts, base, row_low, step, latent)
 
 

time: 20.2 us -> 19.6 us (0.970)
  Pallas kernels: 7.29 us -> 6.11 us
  waiting for transfers between devices: 2.03 us -> 2.85 us
  starting transfers between devices: 7.92 us -> 7.63 us
    pallas_call x1, Pallas kernels: 2.48 us -> 1.3 us  [head(): pl.pallas_call(functools.partial(project_kernel, layout), out_shape=[jax....]
    ppermute x6, waiting for transfers between devices: 2.03 us -> 2.85 us  [exchange(): swapped.append(lax.ppermute(values[turn + 1], 'seq', pairs))]
    ppermute x6, starting transfers between devices: 7.92 us -> 7.63 us  [exchange(): swapped.append(lax.ppermute(values[turn + 1], 'seq', pairs))]
  transfers between devices with their start and end apart: 6 -> 6, of which waited for: 3 -> 4; matrix products, arithmetic and copies ran while one was open for 0% -> 0% of each run, Pallas kernels for 26% -> 21%
where the time goes in v5:
time: 19.6 us; the launch traced here: 19.4 us
  starting transfers between devices  7.63 us (39%)
  Pallas kernels  6.11 us (31%)
  waiting for transfers between devices  2.85 us (15%)
  between operations  2.75 us (14%)
    ppermute x6, starting transfers between devices, exchange(): swapped.append(lax.ppermute(values[turn + 1], 'seq', pairs))  7.63 us
    ppermute x6, waiting for transfers between devices, exchange(): swapped.append(lax.ppermute(values[turn + 1], 'seq', pairs))  2.85 us
    pallas_call x1, Pallas kernels, head(): pl.pallas_call(functools.partial(project_kernel, layout), out_shape=[jax....  1.3 us
    pallas_call x1, Pallas kernels, head(): pl.pallas_call(norm_kernel, out_shape=jax.ShapeDtypeStruct((first, hidden...  1.06 us
    pallas_call x1, Pallas kernels, early(): pl.pallas_call(functools.partial(early_kernel, layout, slots), out_shape=...  0.96 us
    pallas_call x1, Pallas kernels, mix_first(): pl.pallas_call(functools.partial(first_kernel, layout, slots, m), out_sha...  0.9 us
    pallas_call x1, Pallas kernels, finish(): pl.pallas_call(functools.partial(finish_kernel, layout), out_shape=[shape...  0.72 us
    pallas_call x1, Pallas kernels, bands(): pl.pallas_call(functools.partial(bands_kernel, layout), out_shape=[col, r...  0.65 us
  transfers between devices with their start and end apart: 6, of which 4 were waited for; matrix products, arithmetic and copies ran while one was open for 0% of the time, Pallas kernels for 21%

profile of v5, /device:TPU:0, one launch (start us, length us, event | category | flops | bytes accessed | tf_op | source)
XLA Modules:
  0.0 19.4 jit_solution(9247390771160487499)
XLA Ops:
  0.6 0.0 copy-start.3
  0.6 4.1 %collective-permute-start = (f32[64,225]{1,0:T(8,128)}, f32[64,225]{1,0:T(8,128)S(1)}, u32[]{:S(2)}, u32[]{:S(2)}) collective-permute-start(f32[64,225]{1,0:T(8,128)} %residual.1), channel_id=1, source_target_pairs={{0,8},{1,9},{2,10},{3,11},{4,12},{5,13},{6,14},{7,15},{8,0},{9,1},... | collective-permute-start | bytes 172808 | tf_op jit(solution)/shard_map/ppermute | solution.py:560
  4.8 1.3 %collective-permute-start.1 = (f32[64,225]{1,0:T(8,128)}, f32[64,225]{1,0:T(8,128)S(1)}, u32[]{:S(2)}, u32[]{:S(2)}) collective-permute-start(f32[64,225]{1,0:T(8,128)} %residual.1), channel_id=1, source_target_pairs={{0,12},{1,13},{2,14},{3,15},{4,8},{5,9},{6,10},{7,11},{8,4},{9,5},... | collective-permute-start | bytes 172808 | tf_op jit(solution)/shard_map/ppermute | solution.py:560
  6.1 0.2 %collective-permute-start.2 = (f32[64,225]{1,0:T(8,128)}, f32[64,225]{1,0:T(8,128)S(1)}, u32[]{:S(2)}, u32[]{:S(2)}) collective-permute-start(f32[64,225]{1,0:T(8,128)} %residual.1), channel_id=1, source_target_pairs={{0,4},{1,5},{2,6},{3,7},{4,0},{5,1},{6,2},{7,3},{8,12},{9,13},{10,... | collective-permute-start | bytes 172808 | tf_op jit(solution)/shard_map/ppermute | solution.py:560
  7.6 0.7 %bands.1 = (bf16[768,256]{1,0:T(8,128)(2,1)S(1)}, bf16[512,768]{1,0:T(8,128)(2,1)S(1)}, bf16[512,768]{1,0:T(8,128)(2,1)S(1)}) custom-call(s32[1]{0:T(128)S(6)} %copy.13.cut_rows, s32[1]{0:T(128)S(6)} %copy.14.cut_cols), custom_call_target="tpu_custom_call" | custom-call | flops 1000000000 | bytes 20000000 | tf_op jit(solution)/shard_map/bands/pallas_call | solution.py:384
  8.3 0.4 %collective-permute-done.refs_1_ = f32[64,225]{1,0:T(8,128)S(1)} collective-permute-done((f32[64,225]{1,0:T(8,128)}, f32[64,225]{1,0:T(8,128)S(1)}, u32[]{:S(2)}, u32[]{:S(2)}) %collective-permute-start) | collective-permute-done | bytes 57632 | tf_op jit(solution)/shard_map/ppermute | solution.py:560
  8.7 0.0 copy-done.3
  8.7 1.0 %early.1.carry = f32[512,256]{1,0:T(8,128)S(1)} custom-call(bf16[768,256]{1,0:T(8,128)(2,1)S(1)} %get-tuple-element.14.col_filter, bf16[512,768]{1,0:T(8,128)(2,1)S(1)} %get-tuple-element.15.row_filter, f32[64,225]{1,0:T(8,128)S(1)} %copy-done.3, f32[64,225]{1,0:T(8,128)S(1)} %collective-permute-done.refs_1_), custom_call_target="tpu_custom_call" | custom-call | flops 1000000000 | bytes 1000000 | tf_op jit(solution)/shard_map/early/pallas_call | solution.py:405
  9.7 1.5 %collective-permute-done.1.refs_0_ = f32[64,225]{1,0:T(8,128)S(1)} collective-permute-done((f32[64,225]{1,0:T(8,128)}, f32[64,225]{1,0:T(8,128)S(1)}, u32[]{:S(2)}, u32[]{:S(2)}) %collective-permute-start.1) | collective-permute-done | bytes 57632 | tf_op jit(solution)/shard_map/ppermute | solution.py:560
  11.2 0.1 collective-permute-done.2.refs_1_
  11.3 0.9 %mix_first.1 = (f32[64,225]{1,0:T(8,128)S(1)}, bf16[768,256]{1,0:T(8,128)(2,1)S(1)}) custom-call(bf16[768,256]{1,0:T(8,128)(2,1)S(1)} %get-tuple-element.14.col_filter, bf16[512,768]{1,0:T(8,128)(2,1)S(1)} %get-tuple-element.13.row_filter, f32[512,256]{1,0:T(8,128)S(1)} %early.1.carry, f32[64,225]{1,0:T(8,128)S(1)} %collective-permute-done.1.refs_0_, ...), custom_call_target="tpu_custom_call" | custom-call | flops 1000000000 | bytes 1000000 | tf_op jit(solution)/shard_map/mix_first/pallas_call | solution.py:419
  12.2 0.0 copy-start
  12.2 0.0 copy-start.2
  12.2 0.5 %mix_rest.1 = (f32[64,225]{1,0:T(8,128)S(1)}, f32[64,225]{1,0:T(8,128)S(1)}, f32[64,225]{1,0:T(8,128)S(1)}) custom-call(bf16[512,768]{1,0:T(8,128)(2,1)S(1)} %get-tuple-element.13.row_filter, f32[512,256]{1,0:T(8,128)S(1)} %early.1.carry, bf16[768,256]{1,0:T(8,128)(2,1)S(1)} %get-tuple-element.16.data), custom_call_target="tpu_custom_call" | custom-call | flops 1000000000 | bytes 1000000 | tf_op jit(solution)/shard_map/mix_rest/pallas_call | solution.py:436
  12.7 0.0 copy-start.1
  12.8 0.0 copy-start.5
  12.8 0.0 copy-start.6
  12.8 0.0 copy-start.7
  12.8 0.1 collective-permute-start.3
  12.9 1.6 %collective-permute-start.4 = (f32[64,225]{1,0:T(8,128)S(1)}, f32[64,225]{1,0:T(8,128)S(1)}, u32[]{:S(2)}, u32[]{:S(2)}) collective-permute-start(f32[64,225]{1,0:T(8,128)S(1)} %get-tuple-element.19), channel_id=1, source_target_pairs={{0,2},{1,3},{2,0},{3,1},{4,6},{5,7},{6,4},{7,5},{8,10},{9,11},{10,... | collective-permute-start | bytes 172808 | tf_op jit(solution)/shard_map/ppermute | solution.py:560
  14.4 0.3 %collective-permute-start.5 = (f32[64,225]{1,0:T(8,128)S(1)}, f32[64,225]{1,0:T(8,128)S(1)}, u32[]{:S(2)}, u32[]{:S(2)}) collective-permute-start(f32[64,225]{1,0:T(8,128)S(1)} %get-tuple-element.20), channel_id=1, source_target_pairs={{0,1},{1,0},{2,3},{3,2},{4,5},{5,4},{6,7},{7,6},{8,9},{9,8},{10,11... | collective-permute-start | bytes 172808 | tf_op jit(solution)/shard_map/ppermute | solution.py:560
  15.4 0.0 copy-done
  15.4 0.0 copy-done.2
  15.4 1.1 %norm.1.early_normed = bf16[128,5120]{1,0:T(8,128)(2,1)S(1)} custom-call(bf16[225,5120]{1,0:T(8,128)(2,1)S(1)} %copy-done, f32[2,5120]{1,0:T(2,128)S(1)} %copy-done.2), custom_call_target="tpu_custom_call" | custom-call | flops 11520000 | bytes 10000000 | tf_op jit(solution)/shard_map/norm/pallas_call | solution.py:450
  16.5 0.0 copy-start.4
  16.5 0.0 copy-done.1
  16.5 0.0 copy-done.5
  16.5 0.0 copy-done.6
  16.5 0.0 copy-done.7
  16.5 1.3 %project.1 = (f32[64,225]{1,0:T(8,128)S(1)}, f32[64,128]{1,0:T(8,128)S(1)}, f32[8,128]{1,0:T(8,128)S(1)}) custom-call(bf16[128,5120]{1,0:T(8,128)(2,1)S(1)} %norm.1.early_normed, bf16[225,5120]{1,0:T(8,128)(2,1)S(1)} %copy-done, f32[2,5120]{1,0:T(2,128)S(1)} %copy-done.2, bf16[64,5120]{1,0:T(8,128)(2,1)S(1)} %bitcast.3, f32[1,64]{1,0:T(1,128)S(1)} %bitcast.4, ...), custom_call_target="tpu_custom_call" | custom-call | flops 147456000 | bytes 3000000 | tf_op jit(solution)/shard_map/project/pallas_call | solution.py:462
  17.8 0.0 collective-permute-done.3.refs_1_
  17.8 0.8 %collective-permute-done.4.refs_2_ = f32[64,225]{1,0:T(8,128)S(1)} collective-permute-done((f32[64,225]{1,0:T(8,128)S(1)}, f32[64,225]{1,0:T(8,128)S(1)}, u32[]{:S(2)}, u32[]{:S(2)}) %collective-permute-start.4) | collective-permute-done | bytes 57632 | tf_op jit(solution)/shard_map/ppermute | solution.py:560
  18.7 0.0 collective-permute-done.5.refs_3_
  18.7 0.0 copy-done.4
  18.7 0.7 %finish.1 = (f32[64,225]{1,0:T(8,128)}, f32[64,225]{1,0:T(8,128)}) custom-call(f32[64,225]{1,0:T(8,128)S(1)} %get-tuple-element.17.refs_0_, f32[64,225]{1,0:T(8,128)S(1)} %collective-permute-done.3.refs_1_, f32[64,225]{1,0:T(8,128)S(1)} %collective-permute-done.4.refs_2_, f32[64,225]{1,0:T(8,128)S(1)} %collective-permute-done.5.refs_3_, ...), custom_call_target="tpu_custom_call" | custom-call | tf_op jit(solution)/shard_map/finish/pallas_call | solution.py:527
Async XLA Ops:
  0.6 8.1 %copy-start.3 = (f32[64,225]{1,0:T(8,128)S(1)}, f32[64,225]{1,0:T(8,128)}, u32[]{:S(2)}) copy-start(f32[64,225]{1,0:T(8,128)} %residual.1) | copy-start | bytes 172804
  0.6 8.1 %collective-permute-start = (f32[64,225]{1,0:T(8,128)}, f32[64,225]{1,0:T(8,128)S(1)}, u32[]{:S(2)}, u32[]{:S(2)}) collective-permute-start(f32[64,225]{1,0:T(8,128)} %residual.1), channel_id=1, source_target_pairs={{0,8},{1,9},{2,10},{3,11},{4,12},{5,13},{6,14},{7,15},{8,0},{9,1},... | collective-permute-start | bytes 172808 | tf_op jit(solution)/shard_map/ppermute | solution.py:560
  4.8 6.4 %collective-permute-start.1 = (f32[64,225]{1,0:T(8,128)}, f32[64,225]{1,0:T(8,128)S(1)}, u32[]{:S(2)}, u32[]{:S(2)}) collective-permute-start(f32[64,225]{1,0:T(8,128)} %residual.1), channel_id=1, source_target_pairs={{0,12},{1,13},{2,14},{3,15},{4,8},{5,9},{6,10},{7,11},{8,4},{9,5},... | collective-permute-start | bytes 172808 | tf_op jit(solution)/shard_map/ppermute | solution.py:560
  6.1 5.2 %collective-permute-start.2 = (f32[64,225]{1,0:T(8,128)}, f32[64,225]{1,0:T(8,128)S(1)}, u32[]{:S(2)}, u32[]{:S(2)}) collective-permute-start(f32[64,225]{1,0:T(8,128)} %residual.1), channel_id=1, source_target_pairs={{0,4},{1,5},{2,6},{3,7},{4,0},{5,1},{6,2},{7,3},{8,12},{9,13},{10,... | collective-permute-start | bytes 172808 | tf_op jit(solution)/shard_map/ppermute | solution.py:560
  12.2 3.2 %copy-start = (bf16[225,5120]{1,0:T(8,128)(2,1)S(1)}, bf16[225,5120]{1,0:T(8,128)(2,1)}, u32[]{:S(2)}) copy-start(bf16[225,5120]{1,0:T(8,128)(2,1)} %hidden.3) | copy-start | bytes 6912004
  12.2 3.2 %copy-start.2 = (f32[2,5120]{1,0:T(2,128)S(1)}, f32[2,5120]{1,0:T(2,128)}, u32[]{:S(2)}) copy-start(f32[2,5120]{1,0:T(2,128)} %modulation.3) | copy-start | bytes 122884
  12.7 3.7 %copy-start.1 = (bf16[5120,64]{0,1:T(8,128)(2,1)S(1)}, bf16[5120,64]{0,1:T(8,128)(2,1)}, u32[]{:S(2)}) copy-start(bf16[5120,64]{0,1:T(8,128)(2,1)} %param.13) | copy-start | bytes 1966084
  12.8 3.7 %copy-start.5 = (f32[2,16]{1,0:T(2,128)S(1)}, f32[2,16]{1,0:T(2,128)}, u32[]{:S(2)}) copy-start(f32[2,16]{1,0:T(2,128)} %band_gain.1) | copy-start | bytes 388
  12.8 3.7 %copy-start.6 = (f32[64]{0:T(128)S(1)}, f32[64]{0:T(128)}, u32[]{:S(2)}) copy-start(f32[64]{0:T(128)} %param.14) | copy-start | bytes 772
  12.8 3.7 %copy-start.7 = (s32[50]{0:T(128)S(1)}, s32[50]{0:T(128)}, u32[]{:S(2)}) copy-start(s32[50]{0:T(128)} %param.20) | copy-start | bytes 604
  12.8 5.0 %collective-permute-start.3 = (f32[64,225]{1,0:T(8,128)S(1)}, f32[64,225]{1,0:T(8,128)S(1)}, u32[]{:S(2)}, u32[]{:S(2)}) collective-permute-start(f32[64,225]{1,0:T(8,128)S(1)} %get-tuple-element.18), channel_id=1, source_target_pairs={{0,3},{1,2},{2,1},{3,0},{4,7},{5,6},{6,5},{7,4},{8,11},{9,10},{10,... | collective-permute-start | bytes 172808 | tf_op jit(solution)/shard_map/ppermute | solution.py:560
  12.9 5.8 %collective-permute-start.4 = (f32[64,225]{1,0:T(8,128)S(1)}, f32[64,225]{1,0:T(8,128)S(1)}, u32[]{:S(2)}, u32[]{:S(2)}) collective-permute-start(f32[64,225]{1,0:T(8,128)S(1)} %get-tuple-element.19), channel_id=1, source_target_pairs={{0,2},{1,3},{2,0},{3,1},{4,6},{5,7},{6,4},{7,5},{8,10},{9,11},{10,... | collective-permute-start | bytes 172808 | tf_op jit(solution)/shard_map/ppermute | solution.py:560
  14.4 4.2 %collective-permute-start.5 = (f32[64,225]{1,0:T(8,128)S(1)}, f32[64,225]{1,0:T(8,128)S(1)}, u32[]{:S(2)}, u32[]{:S(2)}) collective-permute-start(f32[64,225]{1,0:T(8,128)S(1)} %get-tuple-element.20), channel_id=1, source_target_pairs={{0,1},{1,0},{2,3},{3,2},{4,5},{5,4},{6,7},{7,6},{8,9},{9,8},{10,11... | collective-permute-start | bytes 172808 | tf_op jit(solution)/shard_map/ppermute | solution.py:560
  16.5 2.2 %copy-start.4 = (f32[64,225]{1,0:T(8,128)S(1)}, f32[64,225]{1,0:T(8,128)}, u32[]{:S(2)}) copy-start(f32[64,225]{1,0:T(8,128)} %refs_7_.1) | copy-start | bytes 172804

commit v6 on v5

--- a/solution.py
+++ b/solution.py
@@ -199,7 +199,12 @@
                     for n, part in enumerate((high, low, high)):
                         left = (2 * n + dx) * LANES
                         data[first : first + channels, left : left + LANES] = part
-    high, low = split(product(data[...], col_filter[...]))
+    each = layout.lines * channels
+    halves = [
+        split(product(data[k * each : (k + 1) * each, :], col_filter[...]))
+        for k in range(len(slots))
+    ]
+    high, low = (jnp.concatenate(h, axis=0) for h in zip(*halves))
     return jnp.concatenate([high, high, low], axis=0)
 
 
@@ -303,7 +308,7 @@
 
 
 def norm_kernel(hidden, modulation, normed, scale):
-    norm_rows(hidden, modulation, scale, normed, 0, normed.shape[0])
+    norm_rows(hidden, modulation, scale, normed, 0, normed.shape[0], unroll=True)
 
 
 def project_kernel(

time: 19.6 us -> 19.5 us (level)
  Pallas kernels: 6.11 us -> 5.79 us
  waiting for transfers between devices: 2.85 us -> 3.13 us
    ppermute x6, waiting for transfers between devices: 2.85 us -> 3.13 us  [exchange(): swapped.append(lax.ppermute(values[turn + 1], 'seq', pairs))]
  transfers between devices with their start and end apart: 6 -> 6, of which waited for: 4 -> 4; matrix products, arithmetic and copies ran while one was open for 0% -> 0% of each run, Pallas kernels for 21% -> 19%
where the time goes in v6:
time: 19.5 us; the launch traced here: 19.3 us
  starting transfers between devices  7.63 us (39%)
  Pallas kernels  5.79 us (30%)
  waiting for transfers between devices  3.13 us (16%)
  between operations  2.75 us (14%)
    ppermute x6, starting transfers between devices, exchange(): swapped.append(lax.ppermute(values[turn + 1], 'seq', pairs))  7.63 us
    ppermute x6, waiting for transfers between devices, exchange(): swapped.append(lax.ppermute(values[turn + 1], 'seq', pairs))  3.13 us
    pallas_call x1, Pallas kernels, head(): pl.pallas_call(functools.partial(project_kernel, layout), out_shape=[jax....  1.3 us
    pallas_call x1, Pallas kernels, head(): pl.pallas_call(norm_kernel, out_shape=jax.ShapeDtypeStruct((first, hidden...  0.92 us
    pallas_call x1, Pallas kernels, mix_first(): pl.pallas_call(functools.partial(first_kernel, layout, slots, m), out_sha...  0.86 us
    pallas_call x1, Pallas kernels, early(): pl.pallas_call(functools.partial(early_kernel, layout, slots), out_shape=...  0.82 us
    pallas_call x1, Pallas kernels, finish(): pl.pallas_call(functools.partial(finish_kernel, layout), out_shape=[shape...  0.72 us
    pallas_call x1, Pallas kernels, bands(): pl.pallas_call(functools.partial(bands_kernel, layout), out_shape=[col, r...  0.65 us
  transfers between devices with their start and end apart: 6, of which 4 were waited for; matrix products, arithmetic and copies ran while one was open for 0% of the time, Pallas kernels for 19%

profile of v6, /device:TPU:0, one launch (start us, length us, event | category | flops | bytes accessed | tf_op | source)
XLA Modules:
  0.0 19.3 jit_solution(6410997828700368633)
XLA Ops:
  0.6 0.0 copy-start.3
  0.6 4.1 %collective-permute-start = (f32[64,225]{1,0:T(8,128)}, f32[64,225]{1,0:T(8,128)S(1)}, u32[]{:S(2)}, u32[]{:S(2)}) collective-permute-start(f32[64,225]{1,0:T(8,128)} %residual.1), channel_id=1, source_target_pairs={{0,8},{1,9},{2,10},{3,11},{4,12},{5,13},{6,14},{7,15},{8,0},{9,1},... | collective-permute-start | bytes 172808 | tf_op jit(solution)/shard_map/ppermute | solution.py:565
  4.8 1.3 %collective-permute-start.1 = (f32[64,225]{1,0:T(8,128)}, f32[64,225]{1,0:T(8,128)S(1)}, u32[]{:S(2)}, u32[]{:S(2)}) collective-permute-start(f32[64,225]{1,0:T(8,128)} %residual.1), channel_id=1, source_target_pairs={{0,12},{1,13},{2,14},{3,15},{4,8},{5,9},{6,10},{7,11},{8,4},{9,5},... | collective-permute-start | bytes 172808 | tf_op jit(solution)/shard_map/ppermute | solution.py:565
  6.1 0.2 %collective-permute-start.2 = (f32[64,225]{1,0:T(8,128)}, f32[64,225]{1,0:T(8,128)S(1)}, u32[]{:S(2)}, u32[]{:S(2)}) collective-permute-start(f32[64,225]{1,0:T(8,128)} %residual.1), channel_id=1, source_target_pairs={{0,4},{1,5},{2,6},{3,7},{4,0},{5,1},{6,2},{7,3},{8,12},{9,13},{10,... | collective-permute-start | bytes 172808 | tf_op jit(solution)/shard_map/ppermute | solution.py:565
  7.6 0.7 %bands.1 = (bf16[768,256]{1,0:T(8,128)(2,1)S(1)}, bf16[512,768]{1,0:T(8,128)(2,1)S(1)}, bf16[512,768]{1,0:T(8,128)(2,1)S(1)}) custom-call(s32[1]{0:T(128)S(6)} %copy.13.cut_rows, s32[1]{0:T(128)S(6)} %copy.14.cut_cols), custom_call_target="tpu_custom_call" | custom-call | flops 1000000000 | bytes 20000000 | tf_op jit(solution)/shard_map/bands/pallas_call | solution.py:389
  8.3 0.4 %collective-permute-done.refs_1_ = f32[64,225]{1,0:T(8,128)S(1)} collective-permute-done((f32[64,225]{1,0:T(8,128)}, f32[64,225]{1,0:T(8,128)S(1)}, u32[]{:S(2)}, u32[]{:S(2)}) %collective-permute-start) | collective-permute-done | bytes 57632 | tf_op jit(solution)/shard_map/ppermute | solution.py:565
  8.7 0.0 copy-done.3
  8.7 0.8 %early.1.carry = f32[512,256]{1,0:T(8,128)S(1)} custom-call(bf16[768,256]{1,0:T(8,128)(2,1)S(1)} %get-tuple-element.14.col_filter, bf16[512,768]{1,0:T(8,128)(2,1)S(1)} %get-tuple-element.15.row_filter, f32[64,225]{1,0:T(8,128)S(1)} %copy-done.3, f32[64,225]{1,0:T(8,128)S(1)} %collective-permute-done.refs_1_), custom_call_target="tpu_custom_call" | custom-call | flops 1000000000 | bytes 1000000 | tf_op jit(solution)/shard_map/early/pallas_call | solution.py:410
  9.5 1.6 %collective-permute-done.1.refs_0_ = f32[64,225]{1,0:T(8,128)S(1)} collective-permute-done((f32[64,225]{1,0:T(8,128)}, f32[64,225]{1,0:T(8,128)S(1)}, u32[]{:S(2)}, u32[]{:S(2)}) %collective-permute-start.1) | collective-permute-done | bytes 57632 | tf_op jit(solution)/shard_map/ppermute | solution.py:565
  11.2 0.1 collective-permute-done.2.refs_1_
  11.3 0.9 %mix_first.1 = (f32[64,225]{1,0:T(8,128)S(1)}, bf16[768,256]{1,0:T(8,128)(2,1)S(1)}) custom-call(bf16[768,256]{1,0:T(8,128)(2,1)S(1)} %get-tuple-element.14.col_filter, bf16[512,768]{1,0:T(8,128)(2,1)S(1)} %get-tuple-element.13.row_filter, f32[512,256]{1,0:T(8,128)S(1)} %early.1.carry, f32[64,225]{1,0:T(8,128)S(1)} %collective-permute-done.1.refs_0_, ...), custom_call_target="tpu_custom_call" | custom-call | flops 1000000000 | bytes 1000000 | tf_op jit(solution)/shard_map/mix_first/pallas_call | solution.py:424
  12.2 0.0 copy-start
  12.2 0.0 copy-start.2
  12.2 0.5 %mix_rest.1 = (f32[64,225]{1,0:T(8,128)S(1)}, f32[64,225]{1,0:T(8,128)S(1)}, f32[64,225]{1,0:T(8,128)S(1)}) custom-call(bf16[512,768]{1,0:T(8,128)(2,1)S(1)} %get-tuple-element.13.row_filter, f32[512,256]{1,0:T(8,128)S(1)} %early.1.carry, bf16[768,256]{1,0:T(8,128)(2,1)S(1)} %get-tuple-element.16.data), custom_call_target="tpu_custom_call" | custom-call | flops 1000000000 | bytes 1000000 | tf_op jit(solution)/shard_map/mix_rest/pallas_call | solution.py:441
  12.7 0.0 copy-start.1
  12.7 0.0 copy-start.5
  12.7 0.0 copy-start.6
  12.7 0.0 copy-start.7
  12.8 0.1 collective-permute-start.3
  12.8 1.6 %collective-permute-start.4 = (f32[64,225]{1,0:T(8,128)S(1)}, f32[64,225]{1,0:T(8,128)S(1)}, u32[]{:S(2)}, u32[]{:S(2)}) collective-permute-start(f32[64,225]{1,0:T(8,128)S(1)} %get-tuple-element.19), channel_id=1, source_target_pairs={{0,2},{1,3},{2,0},{3,1},{4,6},{5,7},{6,4},{7,5},{8,10},{9,11},{10,... | collective-permute-start | bytes 172808 | tf_op jit(solution)/shard_map/ppermute | solution.py:565
  14.4 0.3 %collective-permute-start.5 = (f32[64,225]{1,0:T(8,128)S(1)}, f32[64,225]{1,0:T(8,128)S(1)}, u32[]{:S(2)}, u32[]{:S(2)}) collective-permute-start(f32[64,225]{1,0:T(8,128)S(1)} %get-tuple-element.20), channel_id=1, source_target_pairs={{0,1},{1,0},{2,3},{3,2},{4,5},{5,4},{6,7},{7,6},{8,9},{9,8},{10,11... | collective-permute-start | bytes 172808 | tf_op jit(solution)/shard_map/ppermute | solution.py:565
  15.3 0.0 copy-done
  15.3 0.0 copy-done.2
  15.4 0.9 %norm.1.early_normed = bf16[128,5120]{1,0:T(8,128)(2,1)S(1)} custom-call(bf16[225,5120]{1,0:T(8,128)(2,1)S(1)} %copy-done, f32[2,5120]{1,0:T(2,128)S(1)} %copy-done.2), custom_call_target="tpu_custom_call" | custom-call | flops 11520000 | bytes 10000000 | tf_op jit(solution)/shard_map/norm/pallas_call | solution.py:455
  16.3 0.0 copy-start.4
  16.3 0.0 copy-done.1
  16.3 0.0 copy-done.5
  16.3 0.0 copy-done.6
  16.3 0.0 copy-done.7
  16.3 1.3 %project.1 = (f32[64,225]{1,0:T(8,128)S(1)}, f32[64,128]{1,0:T(8,128)S(1)}, f32[8,128]{1,0:T(8,128)S(1)}) custom-call(bf16[128,5120]{1,0:T(8,128)(2,1)S(1)} %norm.1.early_normed, bf16[225,5120]{1,0:T(8,128)(2,1)S(1)} %copy-done, f32[2,5120]{1,0:T(2,128)S(1)} %copy-done.2, bf16[64,5120]{1,0:T(8,128)(2,1)S(1)} %bitcast.3, f32[1,64]{1,0:T(1,128)S(1)} %bitcast.4, ...), custom_call_target="tpu_custom_call" | custom-call | flops 147456000 | bytes 3000000 | tf_op jit(solution)/shard_map/project/pallas_call | solution.py:467
  17.6 0.0 collective-permute-done.3.refs_1_
  17.7 1.0 %collective-permute-done.4.refs_2_ = f32[64,225]{1,0:T(8,128)S(1)} collective-permute-done((f32[64,225]{1,0:T(8,128)S(1)}, f32[64,225]{1,0:T(8,128)S(1)}, u32[]{:S(2)}, u32[]{:S(2)}) %collective-permute-start.4) | collective-permute-done | bytes 57632 | tf_op jit(solution)/shard_map/ppermute | solution.py:565
  18.6 0.0 collective-permute-done.5.refs_3_
  18.6 0.0 copy-done.4
  18.6 0.7 %finish.1 = (f32[64,225]{1,0:T(8,128)}, f32[64,225]{1,0:T(8,128)}) custom-call(f32[64,225]{1,0:T(8,128)S(1)} %get-tuple-element.17.refs_0_, f32[64,225]{1,0:T(8,128)S(1)} %collective-permute-done.3.refs_1_, f32[64,225]{1,0:T(8,128)S(1)} %collective-permute-done.4.refs_2_, f32[64,225]{1,0:T(8,128)S(1)} %collective-permute-done.5.refs_3_, ...), custom_call_target="tpu_custom_call" | custom-call | tf_op jit(solution)/shard_map/finish/pallas_call | solution.py:532
Async XLA Ops:
  0.6 8.1 %copy-start.3 = (f32[64,225]{1,0:T(8,128)S(1)}, f32[64,225]{1,0:T(8,128)}, u32[]{:S(2)}) copy-start(f32[64,225]{1,0:T(8,128)} %residual.1) | copy-start | bytes 172804
  0.6 8.1 %collective-permute-start = (f32[64,225]{1,0:T(8,128)}, f32[64,225]{1,0:T(8,128)S(1)}, u32[]{:S(2)}, u32[]{:S(2)}) collective-permute-start(f32[64,225]{1,0:T(8,128)} %residual.1), channel_id=1, source_target_pairs={{0,8},{1,9},{2,10},{3,11},{4,12},{5,13},{6,14},{7,15},{8,0},{9,1},... | collective-permute-start | bytes 172808 | tf_op jit(solution)/shard_map/ppermute | solution.py:565
  4.8 6.4 %collective-permute-start.1 = (f32[64,225]{1,0:T(8,128)}, f32[64,225]{1,0:T(8,128)S(1)}, u32[]{:S(2)}, u32[]{:S(2)}) collective-permute-start(f32[64,225]{1,0:T(8,128)} %residual.1), channel_id=1, source_target_pairs={{0,12},{1,13},{2,14},{3,15},{4,8},{5,9},{6,10},{7,11},{8,4},{9,5},... | collective-permute-start | bytes 172808 | tf_op jit(solution)/shard_map/ppermute | solution.py:565
  6.1 5.2 %collective-permute-start.2 = (f32[64,225]{1,0:T(8,128)}, f32[64,225]{1,0:T(8,128)S(1)}, u32[]{:S(2)}, u32[]{:S(2)}) collective-permute-start(f32[64,225]{1,0:T(8,128)} %residual.1), channel_id=1, source_target_pairs={{0,4},{1,5},{2,6},{3,7},{4,0},{5,1},{6,2},{7,3},{8,12},{9,13},{10,... | collective-permute-start | bytes 172808 | tf_op jit(solution)/shard_map/ppermute | solution.py:565
  12.2 3.2 %copy-start = (bf16[225,5120]{1,0:T(8,128)(2,1)S(1)}, bf16[225,5120]{1,0:T(8,128)(2,1)}, u32[]{:S(2)}) copy-start(bf16[225,5120]{1,0:T(8,128)(2,1)} %hidden.3) | copy-start | bytes 6912004
  12.2 3.2 %copy-start.2 = (f32[2,5120]{1,0:T(2,128)S(1)}, f32[2,5120]{1,0:T(2,128)}, u32[]{:S(2)}) copy-start(f32[2,5120]{1,0:T(2,128)} %modulation.3) | copy-start | bytes 122884
  12.7 3.6 %copy-start.1 = (bf16[5120,64]{0,1:T(8,128)(2,1)S(1)}, bf16[5120,64]{0,1:T(8,128)(2,1)}, u32[]{:S(2)}) copy-start(bf16[5120,64]{0,1:T(8,128)(2,1)} %param.13) | copy-start | bytes 1966084
  12.7 3.6 %copy-start.5 = (f32[2,16]{1,0:T(2,128)S(1)}, f32[2,16]{1,0:T(2,128)}, u32[]{:S(2)}) copy-start(f32[2,16]{1,0:T(2,128)} %band_gain.1) | copy-start | bytes 388
  12.7 3.6 %copy-start.6 = (f32[64]{0:T(128)S(1)}, f32[64]{0:T(128)}, u32[]{:S(2)}) copy-start(f32[64]{0:T(128)} %param.14) | copy-start | bytes 772
  12.7 3.6 %copy-start.7 = (s32[50]{0:T(128)S(1)}, s32[50]{0:T(128)}, u32[]{:S(2)}) copy-start(s32[50]{0:T(128)} %param.20) | copy-start | bytes 604
  12.8 4.9 %collective-permute-start.3 = (f32[64,225]{1,0:T(8,128)S(1)}, f32[64,225]{1,0:T(8,128)S(1)}, u32[]{:S(2)}, u32[]{:S(2)}) collective-permute-start(f32[64,225]{1,0:T(8,128)S(1)} %get-tuple-element.18), channel_id=1, source_target_pairs={{0,3},{1,2},{2,1},{3,0},{4,7},{5,6},{6,5},{7,4},{8,11},{9,10},{10,... | collective-permute-start | bytes 172808 | tf_op jit(solution)/shard_map/ppermute | solution.py:565
  12.8 5.8 %collective-permute-start.4 = (f32[64,225]{1,0:T(8,128)S(1)}, f32[64,225]{1,0:T(8,128)S(1)}, u32[]{:S(2)}, u32[]{:S(2)}) collective-permute-start(f32[64,225]{1,0:T(8,128)S(1)} %get-tuple-element.19), channel_id=1, source_target_pairs={{0,2},{1,3},{2,0},{3,1},{4,6},{5,7},{6,4},{7,5},{8,10},{9,11},{10,... | collective-permute-start | bytes 172808 | tf_op jit(solution)/shard_map/ppermute | solution.py:565
  14.4 4.2 %collective-permute-start.5 = (f32[64,225]{1,0:T(8,128)S(1)}, f32[64,225]{1,0:T(8,128)S(1)}, u32[]{:S(2)}, u32[]{:S(2)}) collective-permute-start(f32[64,225]{1,0:T(8,128)S(1)} %get-tuple-element.20), channel_id=1, source_target_pairs={{0,1},{1,0},{2,3},{3,2},{4,5},{5,4},{6,7},{7,6},{8,9},{9,8},{10,11... | collective-permute-start | bytes 172808 | tf_op jit(solution)/shard_map/ppermute | solution.py:565
  16.3 2.3 %copy-start.4 = (f32[64,225]{1,0:T(8,128)S(1)}, f32[64,225]{1,0:T(8,128)}, u32[]{:S(2)}) copy-start(f32[64,225]{1,0:T(8,128)} %refs_7_.1) | copy-start | bytes 172804

commit v7 on v6

--- a/solution.py
+++ b/solution.py
@@ -71,7 +71,6 @@
             for p in range(self.members)
         )
         self.lines = 2 * self.span
-        self.groups = pl.cdiv(self.span * PW, LANES)
 
     def owners(self, position):
         givers = [position ^ (k * self.near) for k in self.far_order()]
@@ -86,6 +85,9 @@
 
     def offset(self, owner):
         return lax.rem(owner * self.tokens, PW)
+
+    def tiles(self, r):
+        return range((r * PW - PW + 1) // LANES, (r * PW + PW - 1) // LANES + 1)
 
     def first_line(self, owner):
         return 2 * (owner * self.tokens // PW)
@@ -166,7 +168,7 @@
 
 
 def filtered(layout, slots, sources, col_filter, scratch):
-    span, groups, channels, tokens = layout.span, layout.groups, layout.channels, layout.tokens
+    span, channels, tokens = layout.span, layout.channels, layout.tokens
     window, lines, data = scratch
     givers, _ = layout.owners(lax.rem(lax.axis_index("seq"), layout.members))
     lane = iota((layout.rows, LANES), 1)
@@ -175,21 +177,16 @@
     window[...] = jnp.zeros_like(window)
     for k, (slot, source) in enumerate(zip(slots, sources)):
         window[:, :tokens] = source[...]
-        offset = layout.offset(givers[slot])
-        turned = [
-            pltpu.roll(window[:, g * LANES : (g + 1) * LANES], offset, 1) for g in range(chunks)
-        ]
-        turned = [blank] + turned + [blank] * (groups - chunks)
-        placed = [jnp.where(lane >= offset, turned[g + 1], turned[g]) for g in range(groups)]
+        tiles = [window[:, g * LANES : (g + 1) * LANES] for g in range(chunks)]
         for r in range(span):
-            group, start = divmod(r * PW, LANES)
-            if start == 0:
-                line = placed[group]
-            else:
-                line = pltpu.roll(placed[group], LANES - start, 1)
-                if start + PW > LANES:
-                    rest = pltpu.roll(placed[group + 1], LANES - start, 1)
-                    line = jnp.where(lane < LANES - start, line, rest)
+            start = r * PW - layout.offset(givers[slot])
+            line = None
+            for g in layout.tiles(r):
+                if 0 <= g < chunks:
+                    turned = pltpu.roll(tiles[g], lax.rem(layout.span * LANES - start, LANES), 1)
+                else:
+                    turned = blank
+                line = turned if line is None else jnp.where(lane >= g * LANES - start, turned, line)
             lines[r] = line
         for r in range(span):
             for dy in range(2):
@@ -215,34 +212,23 @@
 
 
 def place_part(layout, mixed, taker, out):
-    span, groups = layout.span, layout.groups
-    channels, tokens = layout.channels, layout.tokens
+    span, channels, tokens = layout.span, layout.channels, layout.tokens
     lane = iota((channels, LANES), 1)
-    offset = layout.offset(taker)
-    back = lax.rem(LANES - offset, LANES)
+    starts = [r * PW - layout.offset(taker) for r in range(span)]
     for dy in range(2):
         for dx in range(2):
-            placed = [None] * (groups + 1)
-
-            def put(group, value):
-                old = placed[group]
-                placed[group] = value if old is None else old + value
-
-            for r in range(span):
+            placed = [None] * pl.cdiv(tokens, LANES)
+            for r, start in enumerate(starts):
                 first = (r * 2 + dy) * channels
                 line = mixed[first : first + channels, dx * LANES : (dx + 1) * LANES]
-                group, start = divmod(r * PW, LANES)
-                if start:
-                    line = pltpu.roll(line, start, 1)
-                if start + PW <= LANES:
-                    put(group, line)
-                else:
-                    put(group, jnp.where(lane >= start, line, 0.0))
-                    put(group + 1, jnp.where(lane < start, line, 0.0))
-            turned = [pltpu.roll(p, back, 1) for p in placed[:groups]]
+                line = pltpu.roll(line, lax.rem(start + LANES, LANES), 1)
+                for g in layout.tiles(r):
+                    if 0 <= g < len(placed):
+                        place = lane + (g * LANES - start)
+                        value = jnp.where((place >= 0) & (place < LANES), line, 0.0)
+                        placed[g] = value if placed[g] is None else placed[g] + value
             first = (dy * 2 + dx) * channels
-            for g in range(pl.cdiv(tokens, LANES)):
-                value = jnp.where(lane < LANES - offset, turned[g], turned[g + 1])
+            for g, value in enumerate(placed):
                 last = min(tokens, (g + 1) * LANES)
                 out[first : first + channels, g * LANES : last] = value[:, : last - g * LANES]
 

time: 19.5 us -> 19.3 us (0.990)
  Pallas kernels: 5.79 us -> 5.48 us
where the time goes in v7:
time: 19.3 us; the launch traced here: 19.1 us
  starting transfers between devices  7.63 us (40%)
  Pallas kernels  5.48 us (28%)
  waiting for transfers between devices  3.19 us (17%)
  between operations  2.75 us (14%)
    ppermute x6, starting transfers between devices, exchange(): swapped.append(lax.ppermute(values[turn + 1], 'seq', pairs))  7.63 us
    ppermute x6, waiting for transfers between devices, exchange(): swapped.append(lax.ppermute(values[turn + 1], 'seq', pairs))  3.19 us
    pallas_call x1, Pallas kernels, head(): pl.pallas_call(functools.partial(project_kernel, layout), out_shape=[jax....  1.3 us
    pallas_call x1, Pallas kernels, head(): pl.pallas_call(norm_kernel, out_shape=jax.ShapeDtypeStruct((first, hidden...  0.92 us
    pallas_call x1, Pallas kernels, early(): pl.pallas_call(functools.partial(early_kernel, layout, slots), out_shape=...  0.76 us
    pallas_call x1, Pallas kernels, finish(): pl.pallas_call(functools.partial(finish_kernel, layout), out_shape=[shape...  0.72 us
    pallas_call x1, Pallas kernels, mix_first(): pl.pallas_call(functools.partial(first_kernel, layout, slots, m), out_sha...  0.71 us
    pallas_call x1, Pallas kernels, bands(): pl.pallas_call(functools.partial(bands_kernel, layout), out_shape=[col, r...  0.65 us
  transfers between devices with their start and end apart: 6, of which 4 were waited for; matrix products, arithmetic and copies ran while one was open for 0% of the time, Pallas kernels for 19%

profile of v7, /device:TPU:0, one launch (start us, length us, event | category | flops | bytes accessed | tf_op | source)
XLA Modules:
  0.0 19.1 jit_solution(9997042310971425063)
XLA Ops:
  0.6 0.0 copy-start.3
  0.6 4.1 %collective-permute-start = (f32[64,225]{1,0:T(8,128)}, f32[64,225]{1,0:T(8,128)S(1)}, u32[]{:S(2)}, u32[]{:S(2)}) collective-permute-start(f32[64,225]{1,0:T(8,128)} %residual.1), channel_id=1, source_target_pairs={{0,8},{1,9},{2,10},{3,11},{4,12},{5,13},{6,14},{7,15},{8,0},{9,1},... | collective-permute-start | bytes 172808 | tf_op jit(solution)/shard_map/ppermute | solution.py:551
  4.8 1.3 %collective-permute-start.1 = (f32[64,225]{1,0:T(8,128)}, f32[64,225]{1,0:T(8,128)S(1)}, u32[]{:S(2)}, u32[]{:S(2)}) collective-permute-start(f32[64,225]{1,0:T(8,128)} %residual.1), channel_id=1, source_target_pairs={{0,12},{1,13},{2,14},{3,15},{4,8},{5,9},{6,10},{7,11},{8,4},{9,5},... | collective-permute-start | bytes 172808 | tf_op jit(solution)/shard_map/ppermute | solution.py:551
  6.1 0.2 %collective-permute-start.2 = (f32[64,225]{1,0:T(8,128)}, f32[64,225]{1,0:T(8,128)S(1)}, u32[]{:S(2)}, u32[]{:S(2)}) collective-permute-start(f32[64,225]{1,0:T(8,128)} %residual.1), channel_id=1, source_target_pairs={{0,4},{1,5},{2,6},{3,7},{4,0},{5,1},{6,2},{7,3},{8,12},{9,13},{10,... | collective-permute-start | bytes 172808 | tf_op jit(solution)/shard_map/ppermute | solution.py:551
  7.6 0.7 %bands.1 = (bf16[768,256]{1,0:T(8,128)(2,1)S(1)}, bf16[512,768]{1,0:T(8,128)(2,1)S(1)}, bf16[512,768]{1,0:T(8,128)(2,1)S(1)}) custom-call(s32[1]{0:T(128)S(6)} %copy.13.cut_rows, s32[1]{0:T(128)S(6)} %copy.14.cut_cols), custom_call_target="tpu_custom_call" | custom-call | flops 1000000000 | bytes 20000000 | tf_op jit(solution)/shard_map/bands/pallas_call | solution.py:375
  8.3 0.4 %collective-permute-done.refs_1_ = f32[64,225]{1,0:T(8,128)S(1)} collective-permute-done((f32[64,225]{1,0:T(8,128)}, f32[64,225]{1,0:T(8,128)S(1)}, u32[]{:S(2)}, u32[]{:S(2)}) %collective-permute-start) | collective-permute-done | bytes 57632 | tf_op jit(solution)/shard_map/ppermute | solution.py:551
  8.7 0.0 copy-done.3
  8.7 0.8 %early.1.carry = f32[512,256]{1,0:T(8,128)S(1)} custom-call(bf16[768,256]{1,0:T(8,128)(2,1)S(1)} %get-tuple-element.14.col_filter, bf16[512,768]{1,0:T(8,128)(2,1)S(1)} %get-tuple-element.15.row_filter, f32[64,225]{1,0:T(8,128)S(1)} %copy-done.3, f32[64,225]{1,0:T(8,128)S(1)} %collective-permute-done.refs_1_), custom_call_target="tpu_custom_call" | custom-call | flops 1000000000 | bytes 1000000 | tf_op jit(solution)/shard_map/early/pallas_call | solution.py:396
  9.5 1.7 %collective-permute-done.1.refs_0_ = f32[64,225]{1,0:T(8,128)S(1)} collective-permute-done((f32[64,225]{1,0:T(8,128)}, f32[64,225]{1,0:T(8,128)S(1)}, u32[]{:S(2)}, u32[]{:S(2)}) %collective-permute-start.1) | collective-permute-done | bytes 57632 | tf_op jit(solution)/shard_map/ppermute | solution.py:551
  11.2 0.1 collective-permute-done.2.refs_1_
  11.3 0.7 %mix_first.1 = (f32[64,225]{1,0:T(8,128)S(1)}, bf16[768,256]{1,0:T(8,128)(2,1)S(1)}) custom-call(bf16[768,256]{1,0:T(8,128)(2,1)S(1)} %get-tuple-element.14.col_filter, bf16[512,768]{1,0:T(8,128)(2,1)S(1)} %get-tuple-element.13.row_filter, f32[512,256]{1,0:T(8,128)S(1)} %early.1.carry, f32[64,225]{1,0:T(8,128)S(1)} %collective-permute-done.1.refs_0_, ...), custom_call_target="tpu_custom_call" | custom-call | flops 1000000000 | bytes 1000000 | tf_op jit(solution)/shard_map/mix_first/pallas_call | solution.py:410
  12.0 0.0 copy-start
  12.0 0.0 copy-start.2
  12.0 0.4 %mix_rest.1 = (f32[64,225]{1,0:T(8,128)S(1)}, f32[64,225]{1,0:T(8,128)S(1)}, f32[64,225]{1,0:T(8,128)S(1)}) custom-call(bf16[512,768]{1,0:T(8,128)(2,1)S(1)} %get-tuple-element.13.row_filter, f32[512,256]{1,0:T(8,128)S(1)} %early.1.carry, bf16[768,256]{1,0:T(8,128)(2,1)S(1)} %get-tuple-element.16.data), custom_call_target="tpu_custom_call" | custom-call | flops 1000000000 | bytes 1000000 | tf_op jit(solution)/shard_map/mix_rest/pallas_call | solution.py:427
  12.5 0.0 copy-start.1
  12.5 0.0 copy-start.5
  12.5 0.0 copy-start.6
  12.5 0.0 copy-start.7
  12.5 0.1 collective-permute-start.3
  12.6 1.6 %collective-permute-start.4 = (f32[64,225]{1,0:T(8,128)S(1)}, f32[64,225]{1,0:T(8,128)S(1)}, u32[]{:S(2)}, u32[]{:S(2)}) collective-permute-start(f32[64,225]{1,0:T(8,128)S(1)} %get-tuple-element.19), channel_id=1, source_target_pairs={{0,2},{1,3},{2,0},{3,1},{4,6},{5,7},{6,4},{7,5},{8,10},{9,11},{10,... | collective-permute-start | bytes 172808 | tf_op jit(solution)/shard_map/ppermute | solution.py:551
  14.1 0.3 %collective-permute-start.5 = (f32[64,225]{1,0:T(8,128)S(1)}, f32[64,225]{1,0:T(8,128)S(1)}, u32[]{:S(2)}, u32[]{:S(2)}) collective-permute-start(f32[64,225]{1,0:T(8,128)S(1)} %get-tuple-element.20), channel_id=1, source_target_pairs={{0,1},{1,0},{2,3},{3,2},{4,5},{5,4},{6,7},{7,6},{8,9},{9,8},{10,11... | collective-permute-start | bytes 172808 | tf_op jit(solution)/shard_map/ppermute | solution.py:551
  15.1 0.0 copy-done
  15.1 0.0 copy-done.2
  15.1 0.9 %norm.1.early_normed = bf16[128,5120]{1,0:T(8,128)(2,1)S(1)} custom-call(bf16[225,5120]{1,0:T(8,128)(2,1)S(1)} %copy-done, f32[2,5120]{1,0:T(2,128)S(1)} %copy-done.2), custom_call_target="tpu_custom_call" | custom-call | flops 11520000 | bytes 10000000 | tf_op jit(solution)/shard_map/norm/pallas_call | solution.py:441
  16.0 0.0 copy-start.4
  16.0 0.0 copy-done.1
  16.1 0.0 copy-done.5
  16.1 0.0 copy-done.6
  16.1 0.0 copy-done.7
  16.1 1.3 %project.1 = (f32[64,225]{1,0:T(8,128)S(1)}, f32[64,128]{1,0:T(8,128)S(1)}, f32[8,128]{1,0:T(8,128)S(1)}) custom-call(bf16[128,5120]{1,0:T(8,128)(2,1)S(1)} %norm.1.early_normed, bf16[225,5120]{1,0:T(8,128)(2,1)S(1)} %copy-done, f32[2,5120]{1,0:T(2,128)S(1)} %copy-done.2, bf16[64,5120]{1,0:T(8,128)(2,1)S(1)} %bitcast.3, f32[1,64]{1,0:T(1,128)S(1)} %bitcast.4, ...), custom_call_target="tpu_custom_call" | custom-call | flops 147456000 | bytes 3000000 | tf_op jit(solution)/shard_map/project/pallas_call | solution.py:453
  17.4 0.0 collective-permute-done.3.refs_1_
  17.4 1.0 %collective-permute-done.4.refs_2_ = f32[64,225]{1,0:T(8,128)S(1)} collective-permute-done((f32[64,225]{1,0:T(8,128)S(1)}, f32[64,225]{1,0:T(8,128)S(1)}, u32[]{:S(2)}, u32[]{:S(2)}) %collective-permute-start.4) | collective-permute-done | bytes 57632 | tf_op jit(solution)/shard_map/ppermute | solution.py:551
  18.4 0.0 collective-permute-done.5.refs_3_
  18.4 0.0 copy-done.4
  18.4 0.7 %finish.1 = (f32[64,225]{1,0:T(8,128)}, f32[64,225]{1,0:T(8,128)}) custom-call(f32[64,225]{1,0:T(8,128)S(1)} %get-tuple-element.17.refs_0_, f32[64,225]{1,0:T(8,128)S(1)} %collective-permute-done.3.refs_1_, f32[64,225]{1,0:T(8,128)S(1)} %collective-permute-done.4.refs_2_, f32[64,225]{1,0:T(8,128)S(1)} %collective-permute-done.5.refs_3_, ...), custom_call_target="tpu_custom_call" | custom-call | tf_op jit(solution)/shard_map/finish/pallas_call | solution.py:518
Async XLA Ops:
  0.6 8.1 %copy-start.3 = (f32[64,225]{1,0:T(8,128)S(1)}, f32[64,225]{1,0:T(8,128)}, u32[]{:S(2)}) copy-start(f32[64,225]{1,0:T(8,128)} %residual.1) | copy-start | bytes 172804
  0.6 8.1 %collective-permute-start = (f32[64,225]{1,0:T(8,128)}, f32[64,225]{1,0:T(8,128)S(1)}, u32[]{:S(2)}, u32[]{:S(2)}) collective-permute-start(f32[64,225]{1,0:T(8,128)} %residual.1), channel_id=1, source_target_pairs={{0,8},{1,9},{2,10},{3,11},{4,12},{5,13},{6,14},{7,15},{8,0},{9,1},... | collective-permute-start | bytes 172808 | tf_op jit(solution)/shard_map/ppermute | solution.py:551
  4.8 6.4 %collective-permute-start.1 = (f32[64,225]{1,0:T(8,128)}, f32[64,225]{1,0:T(8,128)S(1)}, u32[]{:S(2)}, u32[]{:S(2)}) collective-permute-start(f32[64,225]{1,0:T(8,128)} %residual.1), channel_id=1, source_target_pairs={{0,12},{1,13},{2,14},{3,15},{4,8},{5,9},{6,10},{7,11},{8,4},{9,5},... | collective-permute-start | bytes 172808 | tf_op jit(solution)/shard_map/ppermute | solution.py:551
  6.1 5.2 %collective-permute-start.2 = (f32[64,225]{1,0:T(8,128)}, f32[64,225]{1,0:T(8,128)S(1)}, u32[]{:S(2)}, u32[]{:S(2)}) collective-permute-start(f32[64,225]{1,0:T(8,128)} %residual.1), channel_id=1, source_target_pairs={{0,4},{1,5},{2,6},{3,7},{4,0},{5,1},{6,2},{7,3},{8,12},{9,13},{10,... | collective-permute-start | bytes 172808 | tf_op jit(solution)/shard_map/ppermute | solution.py:551
  12.0 3.1 %copy-start = (bf16[225,5120]{1,0:T(8,128)(2,1)S(1)}, bf16[225,5120]{1,0:T(8,128)(2,1)}, u32[]{:S(2)}) copy-start(bf16[225,5120]{1,0:T(8,128)(2,1)} %hidden.3) | copy-start | bytes 6912004
  12.0 3.1 %copy-start.2 = (f32[2,5120]{1,0:T(2,128)S(1)}, f32[2,5120]{1,0:T(2,128)}, u32[]{:S(2)}) copy-start(f32[2,5120]{1,0:T(2,128)} %modulation.3) | copy-start | bytes 122884
  12.5 3.6 %copy-start.1 = (bf16[5120,64]{0,1:T(8,128)(2,1)S(1)}, bf16[5120,64]{0,1:T(8,128)(2,1)}, u32[]{:S(2)}) copy-start(bf16[5120,64]{0,1:T(8,128)(2,1)} %param.13) | copy-start | bytes 1966084
  12.5 3.6 %copy-start.5 = (f32[2,16]{1,0:T(2,128)S(1)}, f32[2,16]{1,0:T(2,128)}, u32[]{:S(2)}) copy-start(f32[2,16]{1,0:T(2,128)} %band_gain.1) | copy-start | bytes 388
  12.5 3.6 %copy-start.6 = (f32[64]{0:T(128)S(1)}, f32[64]{0:T(128)}, u32[]{:S(2)}) copy-start(f32[64]{0:T(128)} %param.14) | copy-start | bytes 772
  12.5 3.6 %copy-start.7 = (s32[50]{0:T(128)S(1)}, s32[50]{0:T(128)}, u32[]{:S(2)}) copy-start(s32[50]{0:T(128)} %param.20) | copy-start | bytes 604
  12.5 4.9 %collective-permute-start.3 = (f32[64,225]{1,0:T(8,128)S(1)}, f32[64,225]{1,0:T(8,128)S(1)}, u32[]{:S(2)}, u32[]{:S(2)}) collective-permute-start(f32[64,225]{1,0:T(8,128)S(1)} %get-tuple-element.18), channel_id=1, source_target_pairs={{0,3},{1,2},{2,1},{3,0},{4,7},{5,6},{6,5},{7,4},{8,11},{9,10},{10,... | collective-permute-start | bytes 172808 | tf_op jit(solution)/shard_map/ppermute | solution.py:551
  12.6 5.8 %collective-permute-start.4 = (f32[64,225]{1,0:T(8,128)S(1)}, f32[64,225]{1,0:T(8,128)S(1)}, u32[]{:S(2)}, u32[]{:S(2)}) collective-permute-start(f32[64,225]{1,0:T(8,128)S(1)} %get-tuple-element.19), channel_id=1, source_target_pairs={{0,2},{1,3},{2,0},{3,1},{4,6},{5,7},{6,4},{7,5},{8,10},{9,11},{10,... | collective-permute-start | bytes 172808 | tf_op jit(solution)/shard_map/ppermute | solution.py:551
  14.1 4.2 %collective-permute-start.5 = (f32[64,225]{1,0:T(8,128)S(1)}, f32[64,225]{1,0:T(8,128)S(1)}, u32[]{:S(2)}, u32[]{:S(2)}) collective-permute-start(f32[64,225]{1,0:T(8,128)S(1)} %get-tuple-element.20), channel_id=1, source_target_pairs={{0,1},{1,0},{2,3},{3,2},{4,5},{5,4},{6,7},{7,6},{8,9},{9,8},{10,11... | collective-permute-start | bytes 172808 | tf_op jit(solution)/shard_map/ppermute | solution.py:551
  16.0 2.3 %copy-start.4 = (f32[64,225]{1,0:T(8,128)S(1)}, f32[64,225]{1,0:T(8,128)}, u32[]{:S(2)}) copy-start(f32[64,225]{1,0:T(8,128)} %refs_7_.1) | copy-start | bytes 172804

commit v8 on v7

--- a/solution.py
+++ b/solution.py
@@ -346,24 +346,40 @@
 def finish_kernel(layout, *refs):
     near, channels, tokens = layout.near, layout.channels, layout.tokens
     parts = refs[:near]
-    base, row_low, step, latent, velocity, latent_next, total = refs[near:]
+    base, row_low, step, latent, velocity_hbm, latent_next_hbm = refs[near : near + 6]
+    total, velocity, latent_next, sems = refs[near + 6 :]
     for g in range(total.shape[0]):
         last = min(tokens, (g + 1) * LANES)
         columns = slice(g * LANES, last)
-        width = slice(0, last - g * LANES)
         low_band = parts[0][:, columns]
         for m in range(1, near):
             low_band += parts[m][:, columns]
-        total[g, :, width] = low_band
-        for c in range(channels):
+        total[g, :, : last - g * LANES] = low_band
+    copies = []
+    for half in range(2):
+        for c in range(half * channels // 2, (half + 1) * channels // 2):
             rows = slice(4 * c, 4 * c + 4)
-            low_band = total[g, pl.ds(c, 4, stride=channels), :][:, width]
-            value = base[rows, columns] + row_low[rows, width] * low_band
-            velocity[rows, columns] = value
-            latent_next[rows, columns] = latent[rows, columns] + step[:4, width] * value
+            for g in range(total.shape[0]):
+                last = min(tokens, (g + 1) * LANES)
+                columns = slice(g * LANES, last)
+                width = slice(0, last - g * LANES)
+                low_band = total[g, pl.ds(c, 4, stride=channels), :][:, width]
+                value = base[rows, columns] + row_low[rows, width] * low_band
+                velocity[rows, columns] = value
+                latent_next[rows, columns] = latent[rows, columns] + step[:4, width] * value
+        rows = slice(half * 2 * channels, (half + 1) * 2 * channels)
+        for n, (here, there) in enumerate(
+            ((velocity, velocity_hbm), (latent_next, latent_next_hbm))
+        ):
+            copy = pltpu.make_async_copy(here.at[rows], there.at[rows], sems.at[half, n])
+            copy.start()
+            copies.append(copy)
+    for copy in copies:
+        copy.wait()
 
 
 VMEM = pl.BlockSpec(memory_space=pltpu.VMEM)
+HBM = pl.BlockSpec(memory_space=pltpu.HBM)
 SMEM = pl.BlockSpec(memory_space=pltpu.SMEM)
 
 
@@ -519,9 +535,12 @@
         functools.partial(finish_kernel, layout),
         out_shape=[shape, shape],
         in_specs=[VMEM] * (layout.near + 4),
-        out_specs=[VMEM, VMEM],
+        out_specs=[HBM, HBM],
         scratch_shapes=[
-            pltpu.VMEM((pl.cdiv(layout.tokens, LANES), layout.rows, LANES), jnp.float32)
+            pltpu.VMEM((pl.cdiv(layout.tokens, LANES), layout.rows, LANES), jnp.float32),
+            pltpu.VMEM(shape.shape, jnp.float32),
+            pltpu.VMEM(shape.shape, jnp.float32),
+            pltpu.SemaphoreType.DMA((2, 2)),
         ],
         compiler_params=pltpu.CompilerParams(vmem_limit_bytes=8 * 2**20),
         name="finish",

time: 19.3 us -> 19.3 us (level)
  no operation moved by 1% of the time
where the time goes in v8:
time: 19.3 us; the launch traced here: 19.1 us
  starting transfers between devices  7.63 us (40%)
  Pallas kernels  5.49 us (28%)
  waiting for transfers between devices  3.19 us (17%)
  between operations  2.75 us (14%)
    ppermute x6, starting transfers between devices, exchange(): swapped.append(lax.ppermute(values[turn + 1], 'seq', pairs))  7.63 us
    ppermute x6, waiting for transfers between devices, exchange(): swapped.append(lax.ppermute(values[turn + 1], 'seq', pairs))  3.19 us
    pallas_call x1, Pallas kernels, head(): pl.pallas_call(functools.partial(project_kernel, layout), out_shape=[jax....  1.3 us
    pallas_call x1, Pallas kernels, head(): pl.pallas_call(norm_kernel, out_shape=jax.ShapeDtypeStruct((first, hidden...  0.92 us
    pallas_call x1, Pallas kernels, early(): pl.pallas_call(functools.partial(early_kernel, layout, slots), out_shape=...  0.76 us
    pallas_call x1, Pallas kernels, finish(): pl.pallas_call(functools.partial(finish_kernel, layout), out_shape=[shape...  0.73 us
    pallas_call x1, Pallas kernels, mix_first(): pl.pallas_call(functools.partial(first_kernel, layout, slots, m), out_sha...  0.71 us
    pallas_call x1, Pallas kernels, bands(): pl.pallas_call(functools.partial(bands_kernel, layout), out_shape=[col, r...  0.65 us
  transfers between devices with their start and end apart: 6, of which 4 were waited for; matrix products, arithmetic and copies ran while one was open for 0% of the time, Pallas kernels for 19%

profile of v8, /device:TPU:0, one launch (start us, length us, event | category | flops | bytes accessed | tf_op | source)
XLA Modules:
  0.0 19.1 jit_solution(3925906496729813969)
XLA Ops:
  0.6 0.0 copy-start.3
  0.6 4.1 %collective-permute-start = (f32[64,225]{1,0:T(8,128)}, f32[64,225]{1,0:T(8,128)S(1)}, u32[]{:S(2)}, u32[]{:S(2)}) collective-permute-start(f32[64,225]{1,0:T(8,128)} %residual.1), channel_id=1, source_target_pairs={{0,8},{1,9},{2,10},{3,11},{4,12},{5,13},{6,14},{7,15},{8,0},{9,1},... | collective-permute-start | bytes 172808 | tf_op jit(solution)/shard_map/ppermute | solution.py:570
  4.8 1.3 %collective-permute-start.1 = (f32[64,225]{1,0:T(8,128)}, f32[64,225]{1,0:T(8,128)S(1)}, u32[]{:S(2)}, u32[]{:S(2)}) collective-permute-start(f32[64,225]{1,0:T(8,128)} %residual.1), channel_id=1, source_target_pairs={{0,12},{1,13},{2,14},{3,15},{4,8},{5,9},{6,10},{7,11},{8,4},{9,5},... | collective-permute-start | bytes 172808 | tf_op jit(solution)/shard_map/ppermute | solution.py:570
  6.1 0.2 %collective-permute-start.2 = (f32[64,225]{1,0:T(8,128)}, f32[64,225]{1,0:T(8,128)S(1)}, u32[]{:S(2)}, u32[]{:S(2)}) collective-permute-start(f32[64,225]{1,0:T(8,128)} %residual.1), channel_id=1, source_target_pairs={{0,4},{1,5},{2,6},{3,7},{4,0},{5,1},{6,2},{7,3},{8,12},{9,13},{10,... | collective-permute-start | bytes 172808 | tf_op jit(solution)/shard_map/ppermute | solution.py:570
  7.6 0.7 %bands.1 = (bf16[768,256]{1,0:T(8,128)(2,1)S(1)}, bf16[512,768]{1,0:T(8,128)(2,1)S(1)}, bf16[512,768]{1,0:T(8,128)(2,1)S(1)}) custom-call(s32[1]{0:T(128)S(6)} %copy.13.cut_rows, s32[1]{0:T(128)S(6)} %copy.14.cut_cols), custom_call_target="tpu_custom_call" | custom-call | flops 1000000000 | bytes 20000000 | tf_op jit(solution)/shard_map/bands/pallas_call | solution.py:391
  8.3 0.4 %collective-permute-done.refs_1_ = f32[64,225]{1,0:T(8,128)S(1)} collective-permute-done((f32[64,225]{1,0:T(8,128)}, f32[64,225]{1,0:T(8,128)S(1)}, u32[]{:S(2)}, u32[]{:S(2)}) %collective-permute-start) | collective-permute-done | bytes 57632 | tf_op jit(solution)/shard_map/ppermute | solution.py:570
  8.7 0.0 copy-done.3
  8.7 0.8 %early.1.carry = f32[512,256]{1,0:T(8,128)S(1)} custom-call(bf16[768,256]{1,0:T(8,128)(2,1)S(1)} %get-tuple-element.14.col_filter, bf16[512,768]{1,0:T(8,128)(2,1)S(1)} %get-tuple-element.15.row_filter, f32[64,225]{1,0:T(8,128)S(1)} %copy-done.3, f32[64,225]{1,0:T(8,128)S(1)} %collective-permute-done.refs_1_), custom_call_target="tpu_custom_call" | custom-call | flops 1000000000 | bytes 1000000 | tf_op jit(solution)/shard_map/early/pallas_call | solution.py:412
  9.5 1.7 %collective-permute-done.1.refs_0_ = f32[64,225]{1,0:T(8,128)S(1)} collective-permute-done((f32[64,225]{1,0:T(8,128)}, f32[64,225]{1,0:T(8,128)S(1)}, u32[]{:S(2)}, u32[]{:S(2)}) %collective-permute-start.1) | collective-permute-done | bytes 57632 | tf_op jit(solution)/shard_map/ppermute | solution.py:570
  11.2 0.1 collective-permute-done.2.refs_1_
  11.3 0.7 %mix_first.1 = (f32[64,225]{1,0:T(8,128)S(1)}, bf16[768,256]{1,0:T(8,128)(2,1)S(1)}) custom-call(bf16[768,256]{1,0:T(8,128)(2,1)S(1)} %get-tuple-element.14.col_filter, bf16[512,768]{1,0:T(8,128)(2,1)S(1)} %get-tuple-element.13.row_filter, f32[512,256]{1,0:T(8,128)S(1)} %early.1.carry, f32[64,225]{1,0:T(8,128)S(1)} %collective-permute-done.1.refs_0_, ...), custom_call_target="tpu_custom_call" | custom-call | flops 1000000000 | bytes 1000000 | tf_op jit(solution)/shard_map/mix_first/pallas_call | solution.py:426
  12.0 0.0 copy-start
  12.0 0.0 copy-start.2
  12.0 0.4 %mix_rest.1 = (f32[64,225]{1,0:T(8,128)S(1)}, f32[64,225]{1,0:T(8,128)S(1)}, f32[64,225]{1,0:T(8,128)S(1)}) custom-call(bf16[512,768]{1,0:T(8,128)(2,1)S(1)} %get-tuple-element.13.row_filter, f32[512,256]{1,0:T(8,128)S(1)} %early.1.carry, bf16[768,256]{1,0:T(8,128)(2,1)S(1)} %get-tuple-element.16.data), custom_call_target="tpu_custom_call" | custom-call | flops 1000000000 | bytes 1000000 | tf_op jit(solution)/shard_map/mix_rest/pallas_call | solution.py:443
  12.5 0.0 copy-start.1
  12.5 0.0 copy-start.5
  12.5 0.0 copy-start.6
  12.5 0.0 copy-start.7
  12.5 0.1 collective-permute-start.3
  12.6 1.6 %collective-permute-start.4 = (f32[64,225]{1,0:T(8,128)S(1)}, f32[64,225]{1,0:T(8,128)S(1)}, u32[]{:S(2)}, u32[]{:S(2)}) collective-permute-start(f32[64,225]{1,0:T(8,128)S(1)} %get-tuple-element.19), channel_id=1, source_target_pairs={{0,2},{1,3},{2,0},{3,1},{4,6},{5,7},{6,4},{7,5},{8,10},{9,11},{10,... | collective-permute-start | bytes 172808 | tf_op jit(solution)/shard_map/ppermute | solution.py:570
  14.1 0.3 %collective-permute-start.5 = (f32[64,225]{1,0:T(8,128)S(1)}, f32[64,225]{1,0:T(8,128)S(1)}, u32[]{:S(2)}, u32[]{:S(2)}) collective-permute-start(f32[64,225]{1,0:T(8,128)S(1)} %get-tuple-element.20), channel_id=1, source_target_pairs={{0,1},{1,0},{2,3},{3,2},{4,5},{5,4},{6,7},{7,6},{8,9},{9,8},{10,11... | collective-permute-start | bytes 172808 | tf_op jit(solution)/shard_map/ppermute | solution.py:570
  15.1 0.0 copy-done
  15.1 0.0 copy-done.2
  15.1 0.9 %norm.1.early_normed = bf16[128,5120]{1,0:T(8,128)(2,1)S(1)} custom-call(bf16[225,5120]{1,0:T(8,128)(2,1)S(1)} %copy-done, f32[2,5120]{1,0:T(2,128)S(1)} %copy-done.2), custom_call_target="tpu_custom_call" | custom-call | flops 11520000 | bytes 10000000 | tf_op jit(solution)/shard_map/norm/pallas_call | solution.py:457
  16.0 0.0 copy-start.4
  16.0 0.0 copy-done.1
  16.1 0.0 copy-done.5
  16.1 0.0 copy-done.6
  16.1 0.0 copy-done.7
  16.1 1.3 %project.1 = (f32[64,225]{1,0:T(8,128)S(1)}, f32[64,128]{1,0:T(8,128)S(1)}, f32[8,128]{1,0:T(8,128)S(1)}) custom-call(bf16[128,5120]{1,0:T(8,128)(2,1)S(1)} %norm.1.early_normed, bf16[225,5120]{1,0:T(8,128)(2,1)S(1)} %copy-done, f32[2,5120]{1,0:T(2,128)S(1)} %copy-done.2, bf16[64,5120]{1,0:T(8,128)(2,1)S(1)} %bitcast.3, f32[1,64]{1,0:T(1,128)S(1)} %bitcast.4, ...), custom_call_target="tpu_custom_call" | custom-call | flops 147456000 | bytes 3000000 | tf_op jit(solution)/shard_map/project/pallas_call | solution.py:469
  17.4 0.0 collective-permute-done.3.refs_1_
  17.4 1.0 %collective-permute-done.4.refs_2_ = f32[64,225]{1,0:T(8,128)S(1)} collective-permute-done((f32[64,225]{1,0:T(8,128)S(1)}, f32[64,225]{1,0:T(8,128)S(1)}, u32[]{:S(2)}, u32[]{:S(2)}) %collective-permute-start.4) | collective-permute-done | bytes 57632 | tf_op jit(solution)/shard_map/ppermute | solution.py:570
  18.4 0.0 collective-permute-done.5.refs_3_
  18.4 0.0 copy-done.4
  18.4 0.7 %finish.1 = (f32[64,225]{1,0:T(8,128)}, f32[64,225]{1,0:T(8,128)}) custom-call(f32[64,225]{1,0:T(8,128)S(1)} %get-tuple-element.17.refs_0_, f32[64,225]{1,0:T(8,128)S(1)} %collective-permute-done.3.refs_1_, f32[64,225]{1,0:T(8,128)S(1)} %collective-permute-done.4.refs_2_, f32[64,225]{1,0:T(8,128)S(1)} %collective-permute-done.5.refs_3_, ...), custom_call_target="tpu_custom_call" | custom-call | tf_op jit(solution)/shard_map/finish/pallas_call | solution.py:534
Async XLA Ops:
  0.6 8.1 %copy-start.3 = (f32[64,225]{1,0:T(8,128)S(1)}, f32[64,225]{1,0:T(8,128)}, u32[]{:S(2)}) copy-start(f32[64,225]{1,0:T(8,128)} %residual.1) | copy-start | bytes 172804
  0.6 8.1 %collective-permute-start = (f32[64,225]{1,0:T(8,128)}, f32[64,225]{1,0:T(8,128)S(1)}, u32[]{:S(2)}, u32[]{:S(2)}) collective-permute-start(f32[64,225]{1,0:T(8,128)} %residual.1), channel_id=1, source_target_pairs={{0,8},{1,9},{2,10},{3,11},{4,12},{5,13},{6,14},{7,15},{8,0},{9,1},... | collective-permute-start | bytes 172808 | tf_op jit(solution)/shard_map/ppermute | solution.py:570
  4.8 6.4 %collective-permute-start.1 = (f32[64,225]{1,0:T(8,128)}, f32[64,225]{1,0:T(8,128)S(1)}, u32[]{:S(2)}, u32[]{:S(2)}) collective-permute-start(f32[64,225]{1,0:T(8,128)} %residual.1), channel_id=1, source_target_pairs={{0,12},{1,13},{2,14},{3,15},{4,8},{5,9},{6,10},{7,11},{8,4},{9,5},... | collective-permute-start | bytes 172808 | tf_op jit(solution)/shard_map/ppermute | solution.py:570
  6.1 5.2 %collective-permute-start.2 = (f32[64,225]{1,0:T(8,128)}, f32[64,225]{1,0:T(8,128)S(1)}, u32[]{:S(2)}, u32[]{:S(2)}) collective-permute-start(f32[64,225]{1,0:T(8,128)} %residual.1), channel_id=1, source_target_pairs={{0,4},{1,5},{2,6},{3,7},{4,0},{5,1},{6,2},{7,3},{8,12},{9,13},{10,... | collective-permute-start | bytes 172808 | tf_op jit(solution)/shard_map/ppermute | solution.py:570
  12.0 3.1 %copy-start = (bf16[225,5120]{1,0:T(8,128)(2,1)S(1)}, bf16[225,5120]{1,0:T(8,128)(2,1)}, u32[]{:S(2)}) copy-start(bf16[225,5120]{1,0:T(8,128)(2,1)} %hidden.3) | copy-start | bytes 6912004
  12.0 3.1 %copy-start.2 = (f32[2,5120]{1,0:T(2,128)S(1)}, f32[2,5120]{1,0:T(2,128)}, u32[]{:S(2)}) copy-start(f32[2,5120]{1,0:T(2,128)} %modulation.3) | copy-start | bytes 122884
  12.5 3.6 %copy-start.1 = (bf16[5120,64]{0,1:T(8,128)(2,1)S(1)}, bf16[5120,64]{0,1:T(8,128)(2,1)}, u32[]{:S(2)}) copy-start(bf16[5120,64]{0,1:T(8,128)(2,1)} %param.13) | copy-start | bytes 1966084
  12.5 3.6 %copy-start.5 = (f32[2,16]{1,0:T(2,128)S(1)}, f32[2,16]{1,0:T(2,128)}, u32[]{:S(2)}) copy-start(f32[2,16]{1,0:T(2,128)} %band_gain.1) | copy-start | bytes 388
  12.5 3.6 %copy-start.6 = (f32[64]{0:T(128)S(1)}, f32[64]{0:T(128)}, u32[]{:S(2)}) copy-start(f32[64]{0:T(128)} %param.14) | copy-start | bytes 772
  12.5 3.6 %copy-start.7 = (s32[50]{0:T(128)S(1)}, s32[50]{0:T(128)}, u32[]{:S(2)}) copy-start(s32[50]{0:T(128)} %param.20) | copy-start | bytes 604
  12.5 4.9 %collective-permute-start.3 = (f32[64,225]{1,0:T(8,128)S(1)}, f32[64,225]{1,0:T(8,128)S(1)}, u32[]{:S(2)}, u32[]{:S(2)}) collective-permute-start(f32[64,225]{1,0:T(8,128)S(1)} %get-tuple-element.18), channel_id=1, source_target_pairs={{0,3},{1,2},{2,1},{3,0},{4,7},{5,6},{6,5},{7,4},{8,11},{9,10},{10,... | collective-permute-start | bytes 172808 | tf_op jit(solution)/shard_map/ppermute | solution.py:570
  12.6 5.8 %collective-permute-start.4 = (f32[64,225]{1,0:T(8,128)S(1)}, f32[64,225]{1,0:T(8,128)S(1)}, u32[]{:S(2)}, u32[]{:S(2)}) collective-permute-start(f32[64,225]{1,0:T(8,128)S(1)} %get-tuple-element.19), channel_id=1, source_target_pairs={{0,2},{1,3},{2,0},{3,1},{4,6},{5,7},{6,4},{7,5},{8,10},{9,11},{10,... | collective-permute-start | bytes 172808 | tf_op jit(solution)/shard_map/ppermute | solution.py:570
  14.1 4.2 %collective-permute-start.5 = (f32[64,225]{1,0:T(8,128)S(1)}, f32[64,225]{1,0:T(8,128)S(1)}, u32[]{:S(2)}, u32[]{:S(2)}) collective-permute-start(f32[64,225]{1,0:T(8,128)S(1)} %get-tuple-element.20), channel_id=1, source_target_pairs={{0,1},{1,0},{2,3},{3,2},{4,5},{5,4},{6,7},{7,6},{8,9},{9,8},{10,11... | collective-permute-start | bytes 172808 | tf_op jit(solution)/shard_map/ppermute | solution.py:570
  16.0 2.3 %copy-start.4 = (f32[64,225]{1,0:T(8,128)S(1)}, f32[64,225]{1,0:T(8,128)}, u32[]{:S(2)}) copy-start(f32[64,225]{1,0:T(8,128)} %refs_7_.1) | copy-start | bytes 172804
